TPU v7x, 32 devices: a whole 2x2x4 slice. The times are simulated.
32 devices in a mesh: wide: 8 (over z, y), narrow: 4 (over x, core).
Axes of the slice: x: 2, y: 2, z: 4, core: 2. Of those that a mesh axis runs over, the one named last changes fastest.
Arguments:
- tokens: bfloat16 [16384, 768], P(('wide', 'narrow')), may hold values from -6 to 6
- band_mask: int32 [32, 8], P(('wide', 'narrow')), may hold values from 0 to 1, as said below
- out_grad: bfloat16 [16384, 768], P(('wide', 'narrow')), may hold values from -6 to 6
- norm1_gain: float32 [768], P(('wide', 'narrow')), may hold values from 0.1 to 1.9
- norm1_shift: float32 [768], P(('wide', 'narrow')), may hold values from -3 to 3
- qkv_weight: float32 [768, 2304], P(('wide', 'narrow')), may hold values from -0.21875 to 0.21875
- qv_bias: float32 [1536], P(('wide', 'narrow')), may hold values from -3 to 3
- out_weight: float32 [768, 768], P(('wide', 'narrow')), may hold values from -4 to 4
- out_bias: float32 [768], P(('wide', 'narrow')), may hold values from -3 to 3
- norm2_gain: float32 [768], P(('wide', 'narrow')), may hold values from 0.1 to 1.9
- norm2_shift: float32 [768], P(('wide', 'narrow')), may hold values from -3 to 3
- up_weight: float32 [768, 3072], P(('wide', 'narrow')), may hold values from -0.21875 to 0.21875
- up_bias: float32 [3072], P(('wide', 'narrow')), may hold values from -3 to 3
- down_weight: float32 [3072, 768], P(('wide', 'narrow')), may hold values from -0.109375 to 0.109375
- down_bias: float32 [768], P(('wide', 'narrow')), may hold values from -3 to 3
Outputs:
- output: bfloat16 [16384, 768], P(('wide', 'narrow'))
- input_grad: bfloat16 [16384, 768], P(('wide', 'narrow'))
- norm1_gain_grad: float32 [768], P(('wide', 'narrow'))
- norm1_shift_grad: float32 [768], P(('wide', 'narrow'))
- qkv_weight_grad: float32 [768, 2304], P(('wide', 'narrow'))
- qv_bias_grad: float32 [1536], P(('wide', 'narrow'))
- out_weight_grad: float32 [768, 768], P(('wide', 'narrow'))
- out_bias_grad: float32 [768], P(('wide', 'narrow'))
- norm2_gain_grad: float32 [768], P(('wide', 'narrow'))
- norm2_shift_grad: float32 [768], P(('wide', 'narrow'))
- up_weight_grad: float32 [768, 3072], P(('wide', 'narrow'))
- up_bias_grad: float32 [3072], P(('wide', 'narrow'))
- down_weight_grad: float32 [3072, 768], P(('wide', 'narrow'))
- down_bias_grad: float32 [768], P(('wide', 'narrow'))
Inputs may be any that keep to these rules, and one draw needn't show every extreme that they name: `band_mask`: each cube keeps at least 6 of its 8 spectral groups, and some cube keeps exactly that many.
All inputs are finite; a program needn't handle non-finite values.
Results may differ from a plain program's by a relative error of at most 0.012.
The roundings to bfloat16 on the way count: a program that leaves them out, or rounds other values in their place, can miss the bound.
Values may be sent and summed in bfloat16 or wider, within the bound.
A program may use at most 192 MiB of HBM per device.

v0:
```python
import math

import jax
import jax.numpy as jnp
from jax import lax
from jax.sharding import PartitionSpec as P

HEAD = 64
HEAD_GROUP = 4
QBLOCK = 512


NORM_EPSILON = 1e-05


def normalize(values, gain, shift):
    centre = jnp.mean(values, axis=1, keepdims=True)
    centred = values - centre
    factor = lax.rsqrt(jnp.mean(centred * centred, axis=1, keepdims=True) + NORM_EPSILON)
    normed = centred * factor
    return (normed * gain + shift, normed, factor)


def normalize_back(upstream, normed, factor, gain):
    gain_grad = jnp.sum(upstream * normed, axis=0)
    shift_grad = jnp.sum(upstream, axis=0)
    scaled = upstream * gain
    inner = (
        scaled
        - jnp.mean(scaled, axis=1, keepdims=True)
        - normed * jnp.mean(scaled * normed, axis=1, keepdims=True)
    )
    return (factor * inner, gain_grad, shift_grad)


def gelu_slope(values):
    cumulative = 0.5 * (1.0 + lax.erf(values * (1.0 / math.sqrt(2.0))))
    return cumulative + values * jnp.exp(-0.5 * values * values) * (1.0 / math.sqrt(2.0 * math.pi))


def to_groups(matrix, count):
    return matrix.reshape(matrix.shape[0], count, -1).transpose(1, 0, 2)


def from_groups(stacked):
    return stacked.transpose(1, 0, 2).reshape(stacked.shape[1], -1)


def attend_forward(query_cols, key_cols, value_cols, key_live):
    row_count, span_cols = key_cols.shape
    head_width = span_cols // HEAD_GROUP
    scaling = 1.0 / math.sqrt(head_width)
    key_rows = key_cols.reshape(row_count, HEAD_GROUP, head_width)
    value_rows = value_cols.reshape(row_count, HEAD_GROUP, head_width)
    query_blocks = query_cols.reshape(row_count // QBLOCK, QBLOCK, HEAD_GROUP, head_width)

    def one_block(query_rows):
        scores = (
            jnp.einsum("qhd,khd->hqk", query_rows, key_rows, preferred_element_type=jnp.float32)
            * scaling
        )
        scores = jnp.where(key_live[None, None, :], scores, -jnp.inf)
        largest = jnp.max(scores, axis=2, keepdims=True)
        expo = jnp.exp(scores - largest)
        totals = jnp.sum(expo, axis=2, keepdims=True)
        weights_low = (expo / totals).astype(jnp.bfloat16)
        mixture = jnp.einsum(
            "hqk,khd->qhd", weights_low, value_rows, preferred_element_type=jnp.float32
        )
        return (mixture.reshape(QBLOCK, span_cols), largest[:, :, 0] + jnp.log(totals[:, :, 0]))

    mixture, logsum = lax.map(one_block, query_blocks)
    return (mixture.reshape(row_count, span_cols), logsum)


def attend_backward(query_cols, key_cols, value_cols, grad_cols, logsum, key_live):
    row_count, span_cols = key_cols.shape
    head_width = span_cols // HEAD_GROUP
    scaling = 1.0 / math.sqrt(head_width)
    key_rows = key_cols.reshape(row_count, HEAD_GROUP, head_width)
    value_rows = value_cols.reshape(row_count, HEAD_GROUP, head_width)
    query_blocks = query_cols.reshape(row_count // QBLOCK, QBLOCK, HEAD_GROUP, head_width)
    grad_blocks = grad_cols.reshape(row_count // QBLOCK, QBLOCK, HEAD_GROUP, head_width)

    def one_block(carry, items):
        key_acc, value_acc = carry
        query_rows, grad_rows, block_logsum = items
        scores = (
            jnp.einsum("qhd,khd->hqk", query_rows, key_rows, preferred_element_type=jnp.float32)
            * scaling
        )
        scores = jnp.where(key_live[None, None, :], scores, -jnp.inf)
        probs = jnp.exp(scores - block_logsum[:, :, None])
        value_acc = value_acc + jnp.einsum(
            "hqk,qhd->khd",
            probs.astype(jnp.bfloat16),
            grad_rows,
            preferred_element_type=jnp.float32,
        )
        prob_grad = jnp.einsum(
            "qhd,khd->hqk", grad_rows, value_rows, preferred_element_type=jnp.float32
        )
        inner = jnp.sum(probs * prob_grad, axis=2, keepdims=True)
        score_grad = (probs * (prob_grad - inner)).astype(jnp.bfloat16)
        query_grad = (
            jnp.einsum("hqk,khd->qhd", score_grad, key_rows, preferred_element_type=jnp.float32)
            * scaling
        )
        key_acc = (
            key_acc
            + jnp.einsum("hqk,qhd->khd", score_grad, query_rows, preferred_element_type=jnp.float32)
            * scaling
        )
        return ((key_acc, value_acc), query_grad.reshape(QBLOCK, span_cols))

    empty = jnp.zeros((row_count, HEAD_GROUP, head_width), jnp.float32)
    (key_grad, value_grad), query_grad = lax.scan(
        one_block, (empty, empty), (query_blocks, grad_blocks, logsum)
    )
    return (
        query_grad.reshape(row_count, span_cols),
        key_grad.reshape(row_count, span_cols),
        value_grad.reshape(row_count, span_cols),
    )


def body(
    tokens,
    band_mask,
    out_grad,
    norm1_gain,
    norm1_shift,
    qkv_weight,
    qv_bias,
    out_weight,
    out_bias,
    norm2_gain,
    norm2_shift,
    up_weight,
    up_bias,
    down_weight,
    down_bias,
):
    row_count, width = tokens.shape
    group_count = width // (HEAD_GROUP * HEAD)
    present = jnp.repeat(band_mask[0].astype(jnp.float32), row_count // band_mask.shape[1])
    key_live = present > 0.5
    column_mask = present[:, None]
    gain_one, shift_one, w_qkv, b_qv, w_out, b_out = (
        lax.all_gather(norm1_gain.astype(jnp.bfloat16), ("wide", "narrow"), axis=0, tiled=True),
        lax.all_gather(norm1_shift.astype(jnp.bfloat16), ("wide", "narrow"), axis=0, tiled=True),
        lax.all_gather(qkv_weight.astype(jnp.bfloat16), ("wide", "narrow"), axis=0, tiled=True),
        lax.all_gather(qv_bias.astype(jnp.bfloat16), ("wide", "narrow"), axis=0, tiled=True),
        lax.all_gather(out_weight.astype(jnp.bfloat16), ("wide", "narrow"), axis=0, tiled=True),
        lax.all_gather(out_bias.astype(jnp.bfloat16), ("wide", "narrow"), axis=0, tiled=True),
    )
    inputs = tokens.astype(jnp.float32)
    normed_one, unit_one, factor_one = normalize(
        inputs, gain_one.astype(jnp.float32), shift_one.astype(jnp.float32)
    )
    normed_one = normed_one.astype(jnp.bfloat16)
    bias_wide = b_qv.astype(jnp.float32)
    bias_full = jnp.concatenate(
        [bias_wide[:width], jnp.zeros((width,), jnp.float32), bias_wide[width:]]
    )
    joined = (jnp.dot(normed_one, w_qkv, preferred_element_type=jnp.float32) + bias_full).astype(
        jnp.bfloat16
    )
    query_groups = to_groups(joined[:, :width], group_count)
    key_groups = to_groups(joined[:, width : 2 * width], group_count)
    value_groups = to_groups(joined[:, 2 * width :], group_count)
    mixture, logsum = lax.map(
        lambda items: attend_forward(items[0], items[1], items[2], key_live),
        (query_groups, key_groups, value_groups),
    )
    mixture = from_groups(mixture).astype(jnp.bfloat16)
    attention = jnp.dot(mixture, w_out, preferred_element_type=jnp.float32) + b_out.astype(
        jnp.float32
    )
    middle = inputs + column_mask * attention
    gain_two, shift_two, w_up, b_up, w_down, b_down = (
        lax.all_gather(norm2_gain.astype(jnp.bfloat16), ("wide", "narrow"), axis=0, tiled=True),
        lax.all_gather(norm2_shift.astype(jnp.bfloat16), ("wide", "narrow"), axis=0, tiled=True),
        lax.all_gather(up_weight.astype(jnp.bfloat16), ("wide", "narrow"), axis=0, tiled=True),
        lax.all_gather(up_bias.astype(jnp.bfloat16), ("wide", "narrow"), axis=0, tiled=True),
        lax.all_gather(down_weight.astype(jnp.bfloat16), ("wide", "narrow"), axis=0, tiled=True),
        lax.all_gather(down_bias.astype(jnp.bfloat16), ("wide", "narrow"), axis=0, tiled=True),
    )
    normed_two, unit_two, factor_two = normalize(
        middle, gain_two.astype(jnp.float32), shift_two.astype(jnp.float32)
    )
    normed_two = normed_two.astype(jnp.bfloat16)
    hidden = jnp.dot(normed_two, w_up, preferred_element_type=jnp.float32) + b_up.astype(
        jnp.float32
    )
    active = jax.nn.gelu(hidden, approximate=False).astype(jnp.bfloat16)
    branch = jnp.dot(active, w_down, preferred_element_type=jnp.float32) + b_down.astype(
        jnp.float32
    )
    output = (middle + column_mask * branch).astype(jnp.bfloat16)
    back_gain_two, back_shift_two, back_up, back_up_bias, back_down, back_down_bias = (
        lax.all_gather(norm2_gain.astype(jnp.bfloat16), ("wide", "narrow"), axis=0, tiled=True),
        lax.all_gather(norm2_shift.astype(jnp.bfloat16), ("wide", "narrow"), axis=0, tiled=True),
        lax.all_gather(up_weight.astype(jnp.bfloat16), ("wide", "narrow"), axis=0, tiled=True),
        lax.all_gather(up_bias.astype(jnp.bfloat16), ("wide", "narrow"), axis=0, tiled=True),
        lax.all_gather(down_weight.astype(jnp.bfloat16), ("wide", "narrow"), axis=0, tiled=True),
        lax.all_gather(down_bias.astype(jnp.bfloat16), ("wide", "narrow"), axis=0, tiled=True),
    )
    upstream = out_grad.astype(jnp.float32)
    branch_grad = (column_mask * upstream).astype(jnp.bfloat16)
    down_weight_grad = jnp.einsum(
        "tf,td->fd", active, branch_grad, preferred_element_type=jnp.float32
    )
    down_bias_grad = jnp.sum(branch_grad.astype(jnp.float32), axis=0)
    active_grad = jnp.einsum(
        "td,fd->tf", branch_grad, back_down, preferred_element_type=jnp.float32
    )
    hidden_grad = (active_grad * gelu_slope(hidden)).astype(jnp.bfloat16)
    up_weight_grad = jnp.einsum(
        "td,tf->df", normed_two, hidden_grad, preferred_element_type=jnp.float32
    )
    up_bias_grad = jnp.sum(hidden_grad.astype(jnp.float32), axis=0)
    normed_two_grad = jnp.einsum(
        "tf,df->td", hidden_grad, back_up, preferred_element_type=jnp.float32
    )
    middle_part, norm2_gain_grad, norm2_shift_grad = normalize_back(
        normed_two_grad, unit_two, factor_two, back_gain_two.astype(jnp.float32)
    )
    (
        norm2_gain_grad,
        norm2_shift_grad,
        up_weight_grad,
        up_bias_grad,
        down_weight_grad,
        down_bias_grad,
    ) = (
        lax.psum_scatter(norm2_gain_grad, ("wide", "narrow"), scatter_dimension=0, tiled=True),
        lax.psum_scatter(norm2_shift_grad, ("wide", "narrow"), scatter_dimension=0, tiled=True),
        lax.psum_scatter(up_weight_grad, ("wide", "narrow"), scatter_dimension=0, tiled=True),
        lax.psum_scatter(up_bias_grad, ("wide", "narrow"), scatter_dimension=0, tiled=True),
        lax.psum_scatter(down_weight_grad, ("wide", "narrow"), scatter_dimension=0, tiled=True),
        lax.psum_scatter(down_bias_grad, ("wide", "narrow"), scatter_dimension=0, tiled=True),
    )
    middle_grad = upstream + middle_part
    back_gain_one, back_shift_one, back_qkv, back_qv, back_out, back_out_bias = (
        lax.all_gather(norm1_gain.astype(jnp.bfloat16), ("wide", "narrow"), axis=0, tiled=True),
        lax.all_gather(norm1_shift.astype(jnp.bfloat16), ("wide", "narrow"), axis=0, tiled=True),
        lax.all_gather(qkv_weight.astype(jnp.bfloat16), ("wide", "narrow"), axis=0, tiled=True),
        lax.all_gather(qv_bias.astype(jnp.bfloat16), ("wide", "narrow"), axis=0, tiled=True),
        lax.all_gather(out_weight.astype(jnp.bfloat16), ("wide", "narrow"), axis=0, tiled=True),
        lax.all_gather(out_bias.astype(jnp.bfloat16), ("wide", "narrow"), axis=0, tiled=True),
    )
    attention_grad = (column_mask * middle_grad).astype(jnp.bfloat16)
    out_weight_grad = jnp.einsum(
        "te,td->ed", mixture, attention_grad, preferred_element_type=jnp.float32
    )
    out_bias_grad = jnp.sum(attention_grad.astype(jnp.float32), axis=0)
    mixture_grad = jnp.einsum(
        "td,ed->te", attention_grad, back_out, preferred_element_type=jnp.float32
    ).astype(jnp.bfloat16)
    grad_groups = to_groups(mixture_grad, group_count)
    query_grad, key_grad, value_grad = lax.map(
        lambda items: attend_backward(items[0], items[1], items[2], items[3], items[4], key_live),
        (query_groups, key_groups, value_groups, grad_groups, logsum),
    )
    query_grad = from_groups(query_grad).astype(jnp.bfloat16)
    key_grad = from_groups(key_grad).astype(jnp.bfloat16)
    value_grad = from_groups(value_grad).astype(jnp.bfloat16)
    joined_grad = jnp.concatenate([query_grad, key_grad, value_grad], axis=1)
    qkv_weight_grad = jnp.einsum(
        "td,tc->dc", normed_one, joined_grad, preferred_element_type=jnp.float32
    )
    qv_bias_grad = jnp.concatenate(
        [
            jnp.sum(query_grad.astype(jnp.float32), axis=0),
            jnp.sum(value_grad.astype(jnp.float32), axis=0),
        ]
    )
    normed_one_grad = jnp.einsum(
        "tc,dc->td", joined_grad, back_qkv, preferred_element_type=jnp.float32
    )
    input_part, norm1_gain_grad, norm1_shift_grad = normalize_back(
        normed_one_grad, unit_one, factor_one, back_gain_one.astype(jnp.float32)
    )
    input_grad = (middle_grad + input_part).astype(jnp.bfloat16)
    (
        norm1_gain_grad,
        norm1_shift_grad,
        qkv_weight_grad,
        qv_bias_grad,
        out_weight_grad,
        out_bias_grad,
    ) = (
        lax.psum_scatter(norm1_gain_grad, ("wide", "narrow"), scatter_dimension=0, tiled=True),
        lax.psum_scatter(norm1_shift_grad, ("wide", "narrow"), scatter_dimension=0, tiled=True),
        lax.psum_scatter(qkv_weight_grad, ("wide", "narrow"), scatter_dimension=0, tiled=True),
        lax.psum_scatter(qv_bias_grad, ("wide", "narrow"), scatter_dimension=0, tiled=True),
        lax.psum_scatter(out_weight_grad, ("wide", "narrow"), scatter_dimension=0, tiled=True),
        lax.psum_scatter(out_bias_grad, ("wide", "narrow"), scatter_dimension=0, tiled=True),
    )
    return (
        output,
        input_grad,
        norm1_gain_grad,
        norm1_shift_grad,
        qkv_weight_grad,
        qv_bias_grad,
        out_weight_grad,
        out_bias_grad,
        norm2_gain_grad,
        norm2_shift_grad,
        up_weight_grad,
        up_bias_grad,
        down_weight_grad,
        down_bias_grad,
    )


def solution(mesh):
    placed = (
        P(("wide", "narrow"), None),
        P(("wide", "narrow"), None),
        P(("wide", "narrow"), None),
        P(("wide", "narrow")),
        P(("wide", "narrow")),
        P(("wide", "narrow"), None),
        P(("wide", "narrow")),
        P(("wide", "narrow"), None),
        P(("wide", "narrow")),
        P(("wide", "narrow")),
        P(("wide", "narrow")),
        P(("wide", "narrow"), None),
        P(("wide", "narrow")),
        P(("wide", "narrow"), None),
        P(("wide", "narrow")),
    )
    return jax.shard_map(
        body,
        mesh=mesh,
        in_specs=placed,
        out_specs=(
            P(("wide", "narrow"), None),
            P(("wide", "narrow"), None),
            P(("wide", "narrow")),
            P(("wide", "narrow")),
            P(("wide", "narrow"), None),
            P(("wide", "narrow")),
            P(("wide", "narrow"), None),
            P(("wide", "narrow")),
            P(("wide", "narrow")),
            P(("wide", "narrow")),
            P(("wide", "narrow"), None),
            P(("wide", "narrow")),
            P(("wide", "narrow"), None),
            P(("wide", "narrow")),
        ),
        check_vma=False,
    )
```

profile of v0, /device:TPU:0, one launch (start us, length us, event | category | flops | bytes accessed | tf_op | source)
XLA Modules:
  0.0 796.7 jit_solution(4265587532490640380)
XLA Ops:
  20.8 42.8 %all-reduce.17 = (bf16[1536]{0:T(1024)(128)(2,1)S(1)}, bf16[768]{0:T(1024)(128)(2,1)S(1)}, bf16[768]{0:T(1024)(128)(2,1)S(1)}, bf16[768]{0:T(1024)(128)(2,1)S(1)...) all-reduce(bf16[1536]{0:T(1024)(128)(2,1)S(1)} %dynamic-update-slic, ...), channel_id=1, replica_groups=mesh['wide'=8,'narrow'=4] {'wide','narrow'}, use_global_device_ids=true, to_apply=%add.2 | all-reduce | flops 9216 | bytes 36864
  67.4 7.3 all-gather.5.cloned.1.call-done
  74.7 4.4 fusion.31
  81.1 12.3 %while.28 = (s32[]{:T(128)}, bf16[3,512,256]{1,2,0:T(8,128)(2,1)}, f32[3,1,4,512]{3,2,1,0:T(4,128)S(1)}, bf16[3,512,256]{1,2,0:T(8,128)(2,1)S(1)}, bf16[3,512,25...) while((s32[]{:T(128)}, bf16[3,512,256]{1,2,0:T(8,128)(2,1)}, ...), condition=%wide.region_5.6_spmd.clone, body=%wide.region_2.5_spmd.clone.sunk | while | flops 281016832 | bytes 15804557 | solution.py:172
  93.4 37.6 %all-gather.7.cloned.1.call-done = bf16[768,768]{1,0:T(8,128)(2,1)} async-done(((bf16[24,768]{1,0:T(8,128)(2,1)}), bf16[768,768]{1,0:T(8,128)(2,1)}) %all-gather.7.cloned.1.call-update) | async-done | bytes 1179664 | tf_op jit(solution)/shard_map/all_gather | solution.py:154
  135.0 62.2 %all-gather.9.cloned.1.call-done = bf16[768,3072]{1,0:T(8,128)(2,1)} async-done(((bf16[24,3072]{1,0:T(8,128)(2,1)}), bf16[768,3072]{1,0:T(8,128)(2,1)}) %all-gather.9.cloned.1.call-update) | async-done | bytes 4718608 | tf_op jit(solution)/shard_map/all_gather | solution.py:184
  197.2 20.3 %fusion.17 = (bf16[512,3072]{1,0:T(8,128)(2,1)}, f32[512,3072]{1,0:T(8,128)}) fusion(f32[3072]{0:T(1024)S(1)} %convert_element_type.206, bf16[768,3072]{1,0:T(8,128)(2,1)} %all-gather.9.cloned.1.call-done, f32[512,768]{1,0:T(8,128)} %copy-done.3, f32[768]{0:T(1024)S(1)} %convert_element_type.202, f32[768]{0:T(1024)S(1)} %convert_element_type.200, ...), kind=kOutput, calls=%fused_computation.39 | convolution fusion | flops 2521694208 | bytes 15751168 | tf_op jit(solution)/shard_map/dot_general | solution.py:193
  217.4 45.5 %all-gather.11.cloned.1.call-done = bf16[3072,768]{1,0:T(8,128)(2,1)} async-done(((bf16[96,768]{1,0:T(8,128)(2,1)}), bf16[3072,768]{1,0:T(8,128)(2,1)}) %all-gather.11.cloned.1.call-update) | async-done | bytes 4718608 | tf_op jit(solution)/shard_map/all_gather | solution.py:186
  263.0 7.5 convert_reduce_fusion
  270.6 3.1 multiply_reduce_fusion.1
  286.0 39.4 %while.29 = (s32[]{:T(128)}, bf16[3,512,256]{1,2,0:T(8,128)(2,1)}, bf16[3,512,256]{1,2,0:T(8,128)(2,1)}, bf16[3,512,256]{1,2,0:T(8,128)(2,1)}, bf16[3,512,256]{1...) while((s32[]{:T(128)}, bf16[3,512,256]{1,2,0:T(8,128)(2,1)}, ...), condition=%wide.region_12.13_spmd.clone, body=%wide.region_10.12_spmd.clone.sunk | while | flops 687340032 | bytes 54593740 | solution.py:262
  289.9 3.9 multiply_reduce_fusion.7
  303.0 3.9 multiply_reduce_fusion.7
  316.2 3.9 multiply_reduce_fusion.7
  325.4 7.1 fusion.48
  333.9 7.2 fusion.57
  342.2 8.3 %fusion.52 = f32[3072,768]{1,0:T(8,128)} fusion(bf16[512,3072]{1,0:T(8,128)(2,1)} %get-tuple-element.279, bf16[512,768]{1,0:T(8,128)(2,1)S(1)} %copy-done.10, f32[512]{0:T(512)S(1)} %mul.184), kind=kOutput, calls=%fused_computation.115 | convolution fusion | flops 2417098752 | bytes 13371392 | tf_op jit(solution)/shard_map/tf,td->fd/dot_general | solution.py:211
  352.8 6.1 fusion.45
  358.9 40.4 %all-reduce.16 = (f32[768]{0:T(1024)S(1)}, f32[768]{0:T(1024)S(1)}, f32[1536]{0:T(1024)S(1)}, f32[768]{0:T(1024)S(1)}, f32[768]{0:T(1024)S(1)}, /*index=5*/f32[7...) all-reduce(f32[768]{0:T(1024)S(1)} %get-tuple-element.204, ...), channel_id=2, replica_groups=mesh['wide'=8,'narrow'=4] {'wide','narrow'}, use_global_device_ids=true, to_apply=%region_16.17.clone | all-reduce | flops 9216 | bytes 73728
  404.0 3.4 fusion.44
  407.4 6.0 add_convert_fusion
  413.4 92.7 %reduce-scatter.5.cloned.1.call-done = f32[24,2304]{1,0:T(8,128)} async-done(((f32[768,2304]{1,0:T(8,128)}), f32[24,2304]{1,0:T(8,128)}) %reduce-scatter.5.cloned.1.call-update) | async-done | bytes 221200 | tf_op jit(solution)/shard_map/reduce_scatter | solution.py:296
  506.2 141.3 %reduce-scatter.9.cloned.1.call-done = f32[24,3072]{1,0:T(8,128)} async-done(((f32[768,3072]{1,0:T(8,128)}), f32[24,3072]{1,0:T(8,128)}) %reduce-scatter.9.cloned.1.call-update) | async-done | bytes 294928 | tf_op jit(solution)/shard_map/reduce_scatter | solution.py:239
  647.5 141.9 %reduce-scatter.11.cloned.1.call-done = f32[96,768]{1,0:T(8,128)} async-done(((f32[3072,768]{1,0:T(8,128)}), f32[96,768]{1,0:T(8,128)}) %reduce-scatter.11.cloned.1.call-update) | async-done | bytes 294928 | tf_op jit(solution)/shard_map/reduce_scatter | solution.py:241
  (220 shorter events, 84.6 us)
Async XLA Ops:
  7.2 67.5 %all-gather.5.cloned.1.call-start = ((), (), s32[]{:S(2)}) async-start(), calls=%async_computation.4 | async-start | bytes 3649536 | tf_op jit(solution)/shard_map/all_gather | solution.py:152
  8.8 122.2 %all-gather.7.cloned.1.call-start = ((), (), s32[]{:S(2)}) async-start(), calls=%async_computation.5 | async-start | bytes 1216512 | tf_op jit(solution)/shard_map/all_gather | solution.py:154
  10.4 186.7 %all-gather.9.cloned.1.call-start = ((), (), s32[]{:S(2)}) async-start(), calls=%async_computation.6 | async-start | bytes 4866048 | tf_op jit(solution)/shard_map/all_gather | solution.py:184
  12.1 250.8 %all-gather.11.cloned.1.call-start = ((), (), s32[]{:S(2)}) async-start(), calls=%async_computation.7 | async-start | bytes 4866048 | tf_op jit(solution)/shard_map/all_gather | solution.py:186
  13.9 399.6 %reduce-scatter.7.cloned.1.call-start = ((), (), s32[]{:S(2)}) async-start(), calls=%async_computation.9 | async-start | bytes 2433024 | tf_op jit(solution)/shard_map/reduce_scatter | solution.py:298
  63.7 15.5 %copy-start.17 = (f32[768]{0:T(1024)}, f32[768]{0:T(1024)S(1)}, u32[]{:S(2)}) copy-start(f32[768]{0:T(1024)S(1)} %convert_element_type.187) | copy-start | bytes 9220
  63.7 15.5 %copy-start.13 = (f32[768]{0:T(1024)}, f32[768]{0:T(1024)S(1)}, u32[]{:S(2)}) copy-start(f32[768]{0:T(1024)S(1)} %convert_element_type.185) | copy-start | bytes 9220
  65.0 14.1 %copy-start.11 = (f32[512]{0:T(512)}, f32[512]{0:T(512)S(1)}, u32[]{:S(2)}) copy-start(f32[512]{0:T(512)S(1)} %broadcast_multiply_fusion.5) | copy-start | bytes 6148
  66.6 12.6 %copy-start.15 = (f32[512]{0:T(512)}, f32[512]{0:T(512)S(1)}, u32[]{:S(2)}) copy-start(f32[512]{0:T(512)S(1)} %add_rsqrt_fusion.1) | copy-start | bytes 6148
  81.1 49.9 %copy-start.1 = (bf16[512,768]{1,0:T(8,128)(2,1)S(1)}, bf16[512,768]{1,0:T(8,128)(2,1)}, u32[]{:S(2)}) copy-start(bf16[512,768]{1,0:T(8,128)(2,1)} %param.19) | copy-start | bytes 2359300
  135.0 128.0 %copy-start.8 = (bf16[512,768]{1,0:T(8,128)(2,1)S(1)}, bf16[512,768]{1,0:T(8,128)(2,1)}, u32[]{:S(2)}) copy-start(bf16[512,768]{1,0:T(8,128)(2,1)} %param.21) | copy-start | bytes 2359300
  263.0 7.6 copy-start.4
  263.0 7.6 copy-start.20
  283.1 223.1 %reduce-scatter.5.cloned.1.call-start = ((), (), s32[]{:S(2)}) async-start(), calls=%async_computation.8 | async-start | bytes 7299072 | tf_op jit(solution)/shard_map/reduce_scatter | solution.py:296
  286.0 39.4 %copy-start.12 = (f32[512]{0:T(512)S(1)}, f32[512]{0:T(512)}, u32[]{:S(2)}) copy-start(f32[512]{0:T(512)} %copy-done.11) | copy-start | bytes 6148
  286.0 39.4 %copy-start.14 = (f32[768]{0:T(1024)S(1)}, f32[768]{0:T(1024)}, u32[]{:S(2)}) copy-start(f32[768]{0:T(1024)} %copy-done.13) | copy-start | bytes 9220
  286.0 39.4 %copy-start.16 = (f32[512]{0:T(512)S(1)}, f32[512]{0:T(512)}, u32[]{:S(2)}) copy-start(f32[512]{0:T(512)} %copy-done.15) | copy-start | bytes 6148
  286.0 39.4 %copy-start.18 = (f32[768]{0:T(1024)S(1)}, f32[768]{0:T(1024)}, u32[]{:S(2)}) copy-start(f32[768]{0:T(1024)} %copy-done.17) | copy-start | bytes 9220
  289.9 3.9 copy-start
  303.0 3.9 copy-start
  316.2 3.9 copy-start
  332.5 315.0 %reduce-scatter.9.cloned.1.call-start = ((), (), s32[]{:S(2)}) async-start(), calls=%async_computation.10 | async-start | bytes 9732096 | tf_op jit(solution)/shard_map/reduce_scatter | solution.py:239
  341.1 448.3 %reduce-scatter.11.cloned.1.call-start = ((), (), s32[]{:S(2)}) async-start(), calls=%async_computation.11 | async-start | bytes 9732096 | tf_op jit(solution)/shard_map/reduce_scatter | solution.py:241
  399.3 8.1 %copy-start.21 = (bf16[512,3072]{1,0:T(8,128)(2,1)S(1)}, bf16[512,3072]{1,0:T(8,128)(2,1)}, u32[]{:S(2)}) copy-start(bf16[512,3072]{1,0:T(8,128)(2,1)} %get-tuple-element.279) | copy-start | bytes 9437188
  (9 other events, 16.9 us)
Sparse Core Ops, SparseCore 0:
  11.5 63.1 all-gather.4
  78.2 52.8 all-gather.6
  134.5 62.5 all-gather.8
  200.5 62.4 all-gather.10
  283.2 97.8 reduce-scatter.6
  388.2 117.9 reduce-scatter.4
  512.6 134.7 reduce-scatter.8
  655.0 134.4 reduce-scatter.10
where the time goes:
time: 806 us; the launch traced here: 797 us
  waiting for transfers between devices  529 us (66%)
  matrix products  111 us (14%)
  blocking collectives  83.2 us (10%)
  other arithmetic  29.4 us (4%)
  local copies, waits for them, and re-layouts  28.6 us (4%)
  between operations  14.9 us (2%)
    reduce_scatter x1, waiting for transfers between devices, body(): lax.psum_scatter(down_weight_grad, ('wide', 'narrow'), scatter_dimension=...  142 us
    reduce_scatter x1, waiting for transfers between devices, body(): lax.psum_scatter(up_weight_grad, ('wide', 'narrow'), scatter_dimension=0,...  141 us
    reduce_scatter x1, waiting for transfers between devices, body(): lax.psum_scatter(qkv_weight_grad, ('wide', 'narrow'), scatter_dimension=0...  92.7 us
    unnamed x2, blocking collectives  83.2 us
    all_gather x1, waiting for transfers between devices, body(): lax.all_gather(up_weight.astype(jnp.bfloat16), ('wide', 'narrow'), axis=0...  62.2 us
    all_gather x1, waiting for transfers between devices, body(): lax.all_gather(down_weight.astype(jnp.bfloat16), ('wide', 'narrow'), axis...  45.5 us
    all_gather x1, waiting for transfers between devices, body(): lax.all_gather(out_weight.astype(jnp.bfloat16), ('wide', 'narrow'), axis=...  37.6 us
    dot_general x1, matrix products, body(): jnp.dot(normed_two, w_up, preferred_element_type=jnp.float32)  20.3 us
  transfers between devices with their start and end apart: 8, of which 7 were waited for; matrix products, arithmetic and copies ran while one was open for 18% of the time, Pallas kernels for 0%

commit v1 on v0

--- a/solution.py
+++ b/solution.py
@@ -1,8 +1,11 @@
+import functools
 import math
 
 import jax
 import jax.numpy as jnp
 from jax import lax
+from jax.experimental import pallas as pl
+from jax.experimental.pallas import tpu as pltpu
 from jax.sharding import PartitionSpec as P
 
 HEAD = 64
@@ -11,6 +14,8 @@
 
 
 NORM_EPSILON = 1e-05
+VMEM_BYTES = 62 << 20
+AXES = ("wide", "narrow")
 
 
 def normalize(values, gain, shift):
@@ -124,7 +129,15 @@
     )
 
 
-def body(
+def gathered(shard):
+    return lax.all_gather(shard.astype(jnp.bfloat16), AXES, axis=0, tiled=True)
+
+
+def scattered(part):
+    return lax.psum_scatter(part, AXES, scatter_dimension=0, tiled=True)
+
+
+def body_plain(
     tokens,
     band_mask,
     out_grad,
@@ -147,12 +160,12 @@
     key_live = present > 0.5
     column_mask = present[:, None]
     gain_one, shift_one, w_qkv, b_qv, w_out, b_out = (
-        lax.all_gather(norm1_gain.astype(jnp.bfloat16), ("wide", "narrow"), axis=0, tiled=True),
-        lax.all_gather(norm1_shift.astype(jnp.bfloat16), ("wide", "narrow"), axis=0, tiled=True),
-        lax.all_gather(qkv_weight.astype(jnp.bfloat16), ("wide", "narrow"), axis=0, tiled=True),
-        lax.all_gather(qv_bias.astype(jnp.bfloat16), ("wide", "narrow"), axis=0, tiled=True),
-        lax.all_gather(out_weight.astype(jnp.bfloat16), ("wide", "narrow"), axis=0, tiled=True),
-        lax.all_gather(out_bias.astype(jnp.bfloat16), ("wide", "narrow"), axis=0, tiled=True),
+        gathered(norm1_gain),
+        gathered(norm1_shift),
+        gathered(qkv_weight),
+        gathered(qv_bias),
+        gathered(out_weight),
+        gathered(out_bias),
     )
     inputs = tokens.astype(jnp.float32)
     normed_one, unit_one, factor_one = normalize(
@@ -179,12 +192,12 @@
     )
     middle = inputs + column_mask * attention
     gain_two, shift_two, w_up, b_up, w_down, b_down = (
-        lax.all_gather(norm2_gain.astype(jnp.bfloat16), ("wide", "narrow"), axis=0, tiled=True),
-        lax.all_gather(norm2_shift.astype(jnp.bfloat16), ("wide", "narrow"), axis=0, tiled=True),
-        lax.all_gather(up_weight.astype(jnp.bfloat16), ("wide", "narrow"), axis=0, tiled=True),
-        lax.all_gather(up_bias.astype(jnp.bfloat16), ("wide", "narrow"), axis=0, tiled=True),
-        lax.all_gather(down_weight.astype(jnp.bfloat16), ("wide", "narrow"), axis=0, tiled=True),
-        lax.all_gather(down_bias.astype(jnp.bfloat16), ("wide", "narrow"), axis=0, tiled=True),
+        gathered(norm2_gain),
+        gathered(norm2_shift),
+        gathered(up_weight),
+        gathered(up_bias),
+        gathered(down_weight),
+        gathered(down_bias),
     )
     normed_two, unit_two, factor_two = normalize(
         middle, gain_two.astype(jnp.float32), shift_two.astype(jnp.float32)
@@ -198,14 +211,6 @@
         jnp.float32
     )
     output = (middle + column_mask * branch).astype(jnp.bfloat16)
-    back_gain_two, back_shift_two, back_up, back_up_bias, back_down, back_down_bias = (
-        lax.all_gather(norm2_gain.astype(jnp.bfloat16), ("wide", "narrow"), axis=0, tiled=True),
-        lax.all_gather(norm2_shift.astype(jnp.bfloat16), ("wide", "narrow"), axis=0, tiled=True),
-        lax.all_gather(up_weight.astype(jnp.bfloat16), ("wide", "narrow"), axis=0, tiled=True),
-        lax.all_gather(up_bias.astype(jnp.bfloat16), ("wide", "narrow"), axis=0, tiled=True),
-        lax.all_gather(down_weight.astype(jnp.bfloat16), ("wide", "narrow"), axis=0, tiled=True),
-        lax.all_gather(down_bias.astype(jnp.bfloat16), ("wide", "narrow"), axis=0, tiled=True),
-    )
     upstream = out_grad.astype(jnp.float32)
     branch_grad = (column_mask * upstream).astype(jnp.bfloat16)
     down_weight_grad = jnp.einsum(
@@ -213,7 +218,7 @@
     )
     down_bias_grad = jnp.sum(branch_grad.astype(jnp.float32), axis=0)
     active_grad = jnp.einsum(
-        "td,fd->tf", branch_grad, back_down, preferred_element_type=jnp.float32
+        "td,fd->tf", branch_grad, w_down, preferred_element_type=jnp.float32
     )
     hidden_grad = (active_grad * gelu_slope(hidden)).astype(jnp.bfloat16)
     up_weight_grad = jnp.einsum(
@@ -221,10 +226,10 @@
     )
     up_bias_grad = jnp.sum(hidden_grad.astype(jnp.float32), axis=0)
     normed_two_grad = jnp.einsum(
-        "tf,df->td", hidden_grad, back_up, preferred_element_type=jnp.float32
+        "tf,df->td", hidden_grad, w_up, preferred_element_type=jnp.float32
     )
     middle_part, norm2_gain_grad, norm2_shift_grad = normalize_back(
-        normed_two_grad, unit_two, factor_two, back_gain_two.astype(jnp.float32)
+        normed_two_grad, unit_two, factor_two, gain_two.astype(jnp.float32)
     )
     (
         norm2_gain_grad,
@@ -234,29 +239,21 @@
         down_weight_grad,
         down_bias_grad,
     ) = (
-        lax.psum_scatter(norm2_gain_grad, ("wide", "narrow"), scatter_dimension=0, tiled=True),
-        lax.psum_scatter(norm2_shift_grad, ("wide", "narrow"), scatter_dimension=0, tiled=True),
-        lax.psum_scatter(up_weight_grad, ("wide", "narrow"), scatter_dimension=0, tiled=True),
-        lax.psum_scatter(up_bias_grad, ("wide", "narrow"), scatter_dimension=0, tiled=True),
-        lax.psum_scatter(down_weight_grad, ("wide", "narrow"), scatter_dimension=0, tiled=True),
-        lax.psum_scatter(down_bias_grad, ("wide", "narrow"), scatter_dimension=0, tiled=True),
+        scattered(norm2_gain_grad),
+        scattered(norm2_shift_grad),
+        scattered(up_weight_grad),
+        scattered(up_bias_grad),
+        scattered(down_weight_grad),
+        scattered(down_bias_grad),
     )
     middle_grad = upstream + middle_part
-    back_gain_one, back_shift_one, back_qkv, back_qv, back_out, back_out_bias = (
-        lax.all_gather(norm1_gain.astype(jnp.bfloat16), ("wide", "narrow"), axis=0, tiled=True),
-        lax.all_gather(norm1_shift.astype(jnp.bfloat16), ("wide", "narrow"), axis=0, tiled=True),
-        lax.all_gather(qkv_weight.astype(jnp.bfloat16), ("wide", "narrow"), axis=0, tiled=True),
-        lax.all_gather(qv_bias.astype(jnp.bfloat16), ("wide", "narrow"), axis=0, tiled=True),
-        lax.all_gather(out_weight.astype(jnp.bfloat16), ("wide", "narrow"), axis=0, tiled=True),
-        lax.all_gather(out_bias.astype(jnp.bfloat16), ("wide", "narrow"), axis=0, tiled=True),
-    )
     attention_grad = (column_mask * middle_grad).astype(jnp.bfloat16)
     out_weight_grad = jnp.einsum(
         "te,td->ed", mixture, attention_grad, preferred_element_type=jnp.float32
     )
     out_bias_grad = jnp.sum(attention_grad.astype(jnp.float32), axis=0)
     mixture_grad = jnp.einsum(
-        "td,ed->te", attention_grad, back_out, preferred_element_type=jnp.float32
+        "td,ed->te", attention_grad, w_out, preferred_element_type=jnp.float32
     ).astype(jnp.bfloat16)
     grad_groups = to_groups(mixture_grad, group_count)
     query_grad, key_grad, value_grad = lax.map(
@@ -277,10 +274,10 @@
         ]
     )
     normed_one_grad = jnp.einsum(
-        "tc,dc->td", joined_grad, back_qkv, preferred_element_type=jnp.float32
+        "tc,dc->td", joined_grad, w_qkv, preferred_element_type=jnp.float32
     )
     input_part, norm1_gain_grad, norm1_shift_grad = normalize_back(
-        normed_one_grad, unit_one, factor_one, back_gain_one.astype(jnp.float32)
+        normed_one_grad, unit_one, factor_one, gain_one.astype(jnp.float32)
     )
     input_grad = (middle_grad + input_part).astype(jnp.bfloat16)
     (
@@ -291,12 +288,12 @@
         out_weight_grad,
         out_bias_grad,
     ) = (
-        lax.psum_scatter(norm1_gain_grad, ("wide", "narrow"), scatter_dimension=0, tiled=True),
-        lax.psum_scatter(norm1_shift_grad, ("wide", "narrow"), scatter_dimension=0, tiled=True),
-        lax.psum_scatter(qkv_weight_grad, ("wide", "narrow"), scatter_dimension=0, tiled=True),
-        lax.psum_scatter(qv_bias_grad, ("wide", "narrow"), scatter_dimension=0, tiled=True),
-        lax.psum_scatter(out_weight_grad, ("wide", "narrow"), scatter_dimension=0, tiled=True),
-        lax.psum_scatter(out_bias_grad, ("wide", "narrow"), scatter_dimension=0, tiled=True),
+        scattered(norm1_gain_grad),
+        scattered(norm1_shift_grad),
+        scattered(qkv_weight_grad),
+        scattered(qv_bias_grad),
+        scattered(out_weight_grad),
+        scattered(out_bias_grad),
     )
     return (
         output,
@@ -316,43 +313,1142 @@
     )
 
 
+MESH_ID = pl.DeviceIdType.MESH
+VIA_X = (0, 2)
+VIA_Y = (1, 3)
+ORDER = (1, 3, 2)
+SCORE_SCALE = math.log2(math.e) / math.sqrt(HEAD)
+TILE = 384
+
+
+class Place:
+    def __init__(self):
+        wide = lax.axis_index("wide")
+        narrow = lax.axis_index("narrow")
+        z, y = wide // 2, wide % 2
+        x, c = narrow // 2, narrow % 2
+        self.z, self.c = z, c
+        self.zs = (z, z + 1 - 2 * (z % 2), (z + 2) % 4, 3 - z)
+        self.q = y * 2 + x
+        self.qx = y * 2 + (1 - x)
+        self.qy = (1 - y) * 2 + x
+        self.qd = (1 - y) * 2 + (1 - x)
+        self.to_z = tuple((zz * 2 + y, x * 2 + c) for zz in self.zs)
+        self.to_x = (z * 2 + y, (1 - x) * 2 + c)
+        self.to_y = (z * 2 + 1 - y, x * 2 + c)
+        self.to_c = (z * 2 + y, x * 2 + 1 - c)
+
+
+def span(start, size, step):
+    return pl.ds(pl.multiple_of(start, step), size)
+
+
+def meet(place):
+    barrier = pltpu.get_barrier_semaphore()
+    peers = place.to_z[1:] + (place.to_x, place.to_y, place.to_c)
+    for peer in peers:
+        pl.semaphore_signal(barrier, inc=1, device_id=peer, device_id_type=MESH_ID)
+    pl.semaphore_wait(barrier, len(peers))
+
+
+def remote(source, target, send, recv, peer):
+    return pltpu.make_async_remote_copy(
+        src_ref=source,
+        dst_ref=target,
+        send_sem=send,
+        recv_sem=recv,
+        device_id=peer,
+        device_id_type=MESH_ID,
+    )
+
+
+class Piece:
+    COUNT = 19
+
+    def __init__(self, place, send, recv):
+        self.p = place
+        self.send = send
+        self.recv = recv
+        self.sent = []
+
+    def go(self, source, target, index, peer):
+        remote(source(), target(), self.send.at[index], self.recv.at[index], peer).start()
+        self.sent.append((source, target, index, peer))
+
+    def got(self, target, index, peer):
+        remote(target, target, self.send.at[index], self.recv.at[index], peer).wait_recv()
+
+    def finish(self):
+        for source, target, index, peer in self.sent:
+            remote(source(), target(), self.send.at[index], self.recv.at[index], peer).wait_send()
+
+
+class Gather(Piece):
+    def __init__(self, place, own, block, column, other, send, recv):
+        super().__init__(place, send, recv)
+        self.own = own
+        self.block = block
+        self.column = column
+        self.other = other
+
+    def start_z(self):
+        p = self.p
+        for k in ORDER:
+            self.go(self.own, lambda: self.block(p.z, p.q), k - 1, p.to_z[k])
+
+    def start_xy(self):
+        p = self.p
+        self.go(self.own, lambda: self.block(p.z, p.q), 3, p.to_x)
+        self.go(self.own, lambda: self.block(p.z, p.q), 9, p.to_y)
+
+    def z(self, k):
+        p = self.p
+        here = lambda: self.block(p.zs[k], p.q)
+        self.got(here(), k - 1, p.to_z[k])
+        self.go(here, here, 3 + k, p.to_x)
+        self.go(here, here, 9 + k, p.to_y)
+
+    def share(self, index, q):
+        column = lambda: self.column(q)
+        self.go(column, column, index, self.p.to_c)
+
+    def own_column(self):
+        self.share(15, self.p.q)
+
+    def xy(self, k):
+        p = self.p
+        from_x = lambda: self.block(p.zs[k], p.qx)
+        self.got(from_x(), 3 + k, p.to_x)
+        if k in VIA_X:
+            self.go(from_x, from_x, 13 + VIA_X.index(k), p.to_y)
+        from_y = lambda: self.block(p.zs[k], p.qy)
+        self.got(from_y(), 9 + k, p.to_y)
+        if k in VIA_Y:
+            self.go(from_y, from_y, 7 + VIA_Y.index(k), p.to_x)
+
+    def xy_columns(self):
+        self.share(16, self.p.qx)
+        self.share(17, self.p.qy)
+
+    def d(self):
+        p = self.p
+        for i, k in enumerate(VIA_X):
+            self.got(self.block(p.zs[k], p.qd), 13 + i, p.to_y)
+        for i, k in enumerate(VIA_Y):
+            self.got(self.block(p.zs[k], p.qd), 7 + i, p.to_x)
+        self.share(18, p.qd)
+
+    def c(self):
+        p = self.p
+        for i, q in enumerate((p.q, p.qx, p.qy, p.qd)):
+            self.got(self.other(q), 15 + i, p.to_c)
+
+
+class Scatter(Piece):
+    def __init__(self, place, bufs, send, recv):
+        super().__init__(place, send, recv)
+        self.total, self.dx, self.dy, self.xr, self.yr, self.zr = bufs
+        self.columns = (place.qd, place.qx, place.qy, place.q)
+
+    def add(self, target, other):
+        target[...] = (target[...].astype(jnp.float32) + other[...].astype(jnp.float32)).astype(
+            target.dtype
+        )
+
+    def give(self, other):
+        for i, q in enumerate(self.columns):
+            self.go(
+                lambda q=q: other(q), lambda q=q: self.total.at[:, q], 15 + i, self.p.to_c
+            )
+
+    def arrive(self, i):
+        self.got(self.total.at[:, self.columns[i]], 15 + i, self.p.to_c)
+
+    def take(self, i, mine):
+        self.arrive(i)
+        q = self.columns[i]
+        for zz in range(4):
+            self.add(self.total.at[zz, q], mine(zz, q))
+
+    def diagonal(self):
+        p = self.p
+        for i in range(2):
+            self.go(
+                lambda i=i: self.total.at[p.zs[VIA_X[i]], p.qd],
+                lambda i=i: self.dx.at[i],
+                7 + i,
+                p.to_x,
+            )
+            self.go(
+                lambda i=i: self.total.at[p.zs[VIA_Y[i]], p.qd],
+                lambda i=i: self.dy.at[i],
+                13 + i,
+                p.to_y,
+            )
+
+    def cross(self, k):
+        p = self.p
+        on_x = lambda: self.total.at[p.zs[k], p.qx]
+        on_y = lambda: self.total.at[p.zs[k], p.qy]
+        if k in VIA_Y:
+            i = VIA_Y.index(k)
+            self.go(on_y, lambda: self.yr.at[k], 9 + k, p.to_y)
+            self.got(self.dy.at[i], 13 + i, p.to_y)
+            self.add(on_x(), self.dy.at[i])
+            self.go(on_x, lambda: self.xr.at[k], 3 + k, p.to_x)
+        else:
+            i = VIA_X.index(k)
+            self.go(on_x, lambda: self.xr.at[k], 3 + k, p.to_x)
+            self.got(self.dx.at[i], 7 + i, p.to_x)
+            self.add(on_y(), self.dx.at[i])
+            self.go(on_y, lambda: self.yr.at[k], 9 + k, p.to_y)
+
+    def plane(self, k):
+        p = self.p
+        self.got(self.xr.at[k], 3 + k, p.to_x)
+        self.got(self.yr.at[k], 9 + k, p.to_y)
+        here = self.total.at[p.zs[k], p.q]
+        return here, (
+            here[...].astype(jnp.float32)
+            + self.xr[k].astype(jnp.float32)
+            + self.yr[k].astype(jnp.float32)
+        )
+
+    def spread(self, k):
+        here, value = self.plane(k)
+        here[...] = value.astype(here.dtype)
+        self.go(
+            lambda: self.total.at[self.p.zs[k], self.p.q],
+            lambda: self.zr.at[k - 1],
+            k - 1,
+            self.p.to_z[k],
+        )
+
+    def last(self):
+        p = self.p
+        _, value = self.plane(0)
+        for k in ORDER:
+            self.got(self.zr.at[k - 1], k - 1, p.to_z[k])
+            value = value + self.zr[k - 1].astype(jnp.float32)
+        return value
+
+
+def scatter_buffers(tail, kind):
+    return [
+        pltpu.VMEM((4, 4) + tail, kind),
+        pltpu.VMEM((2,) + tail, kind),
+        pltpu.VMEM((2,) + tail, kind),
+        pltpu.VMEM((4,) + tail, kind),
+        pltpu.VMEM((4,) + tail, kind),
+        pltpu.VMEM((3,) + tail, kind),
+    ]
+
+
+WANTED = (
+    "vec",
+    "turned_two",
+    "middle",
+    "up_wide",
+    "mixed_turned",
+    "out_wide",
+    "joined",
+    "logsum",
+    "turned_one",
+    "qkv_wide",
+)
+MATRICES = ("qkv", "out", "up", "down")
+
+
+def triples(**named):
+    return [(name, one, two) for name, (one, two) in named.items()]
+
+
+def pairs_of(**named):
+    return list(named.items())
+
+
+class Named:
+    def __init__(self, names, refs):
+        assert len(names) == len(refs)
+        self.__dict__.update(zip(names, refs))
+
+
+def loop(count, compute, slots=()):
+    def step(i, carry):
+        compute(i)
+        for j, steps in enumerate(slots):
+            if steps:
+
+                @pl.when(i == j)
+                def _(steps=steps):
+                    for one in steps:
+                        one()
+
+        return carry
+
+    lax.fori_loop(0, count, step, 0)
+
+
+def dot(left, right):
+    return jnp.dot(left, right, preferred_element_type=jnp.float32)
+
+
+def dot_nt(left, right):
+    return lax.dot_general(
+        left, right, (((1,), (1,)), ((), ())), preferred_element_type=jnp.float32
+    )
+
+
+def dot_tn(left, right):
+    return lax.dot_general(
+        left, right, (((0,), (0,)), ((), ())), preferred_element_type=jnp.float32
+    )
+
+
+def head_only(values, e):
+    lane = lax.broadcasted_iota(jnp.int32, values.shape, 1)
+    return jnp.where((lane // HEAD) == e, values, jnp.zeros_like(values))
+
+
+def fill_present(present, mask):
+    groups = mask.shape[1]
+    rows = present.shape[0] // groups
+    for g in range(groups):
+        present[g * rows : (g + 1) * rows, :] = jnp.full(
+            (rows, 128), mask[0, g].astype(jnp.float32)
+        )
+
+
+def segments(width):
+    return ((0, width, width // 32), (width, 2 * width, width // 16), (3 * width, 4 * width, width // 8))
+
+
+def selection(width):
+    parts = []
+    for _, size, m in segments(width):
+        lane = lax.broadcasted_iota(jnp.int32, (1, size), 1).astype(jnp.float32)
+        rest = lane - m * jnp.floor((lane + 0.5) * (1.0 / m))
+        row = lax.broadcasted_iota(jnp.int32, (128, size), 0).astype(jnp.float32)
+        parts.append(jnp.where(row == rest, 1.0, 0.0).astype(jnp.bfloat16))
+    return jnp.concatenate(parts, axis=1)
+
+
+def owners(width):
+    parts = []
+    for _, size, m in segments(width):
+        lane = lax.broadcasted_iota(jnp.int32, (1, size), 1).astype(jnp.float32)
+        parts.append(jnp.floor((lane + 0.5) * (1.0 / m)))
+    return jnp.concatenate(parts, axis=1)
+
+
+def unit(values):
+    centred = values - jnp.mean(values, axis=1, keepdims=True)
+    factor = lax.rsqrt(jnp.mean(centred * centred, axis=1, keepdims=True) + NORM_EPSILON)
+    return centred * factor, factor
+
+
+def forward_kernel(names, *refs):
+    r = Named(names, refs)
+    place = Place()
+    tokens, width = r.tokens.shape
+    hidden = r.act.shape[0] * TILE
+    pairs = width // 128
+    shards = (r.qkv_shard, r.out_shard, r.up_shard, r.down_shard)
+    owns = (r.qkv_own, r.out_own, r.up_own, r.down_own)
+    sibs = (r.qkv_sib, r.out_sib, r.up_sib, r.down_sib)
+    wides = (r.qkv_wide, r.out_wide, r.up_wide, r.down_wide)
+    meet(place)
+    first = place.c == 0
+
+    def before(i):
+        half = shards[i].shape[1] // 2
+        return remote(
+            shards[i].at[:, span((1 - place.c) * half, half, 128)],
+            sibs[i],
+            r.pre_send.at[i],
+            r.pre_recv.at[i],
+            place.to_c,
+        )
+
+    for i in range(4):
+        before(i).start()
+    small = Gather(
+        place,
+        lambda: r.small,
+        lambda zz, q: r.small_wide.at[zz, q, place.c],
+        lambda q: r.small_wide.at[:, q, place.c],
+        lambda q: r.small_wide.at[:, q, 1 - place.c],
+        r.send.at[6],
+        r.recv.at[6],
+    )
+    local = [pltpu.make_async_copy(r.small, r.small_wide.at[place.z, place.q, place.c], r.local.at[4])]
+    local[0].start()
+    small.start_z()
+    small.start_xy()
+
+    cuts = (
+        (0, 0, 48, 0, 1152),
+        (1, 0, 48, 0, 384),
+        (2, 0, 48, 0, 768),
+        (2, 0, 48, 768, 768),
+        (3, 0, 96, 0, 384),
+        (3, 96, 96, 0, 384),
+    )
+    pieces = []
+    for j, (i, row, rows, col, cols) in enumerate(cuts):
+        half = shards[i].shape[1] // 2
+
+        def at(c, row=row, rows=rows, col=col, cols=cols, half=half):
+            return (pl.ds(row, rows), span(c * half + col, cols, 128))
+
+        pieces.append(
+            Gather(
+                place,
+                lambda i=i, row=row, rows=rows, col=col, cols=cols: owns[i].at[
+                    pl.ds(row, rows), pl.ds(col, cols)
+                ],
+                lambda zz, q, i=i, at=at: wides[i].at[(zz, q) + at(place.c)],
+                lambda q, i=i, at=at: wides[i].at[(slice(None), q) + at(place.c)],
+                lambda q, i=i, at=at: wides[i].at[(slice(None), q) + at(1 - place.c)],
+                r.send.at[j],
+                r.recv.at[j],
+            )
+        )
+    for i in range(4):
+        half = shards[i].shape[1] // 2
+        cols = span(place.c * half, half, 128)
+        before(i).wait_recv()
+        mine = shards[i][:, cols]
+        theirs = sibs[i][...]
+        owns[i][...] = jnp.concatenate(
+            [jnp.where(first, mine, theirs), jnp.where(first, theirs, mine)], axis=0
+        ).astype(jnp.bfloat16)
+        copy = pltpu.make_async_copy(
+            owns[i], wides[i].at[place.z, place.q, :, cols], r.local.at[i]
+        )
+        copy.start()
+        local.append(copy)
+        for j, cut in enumerate(cuts):
+            if cut[0] == i:
+                pieces[j].start_z()
+        if i == 0:
+            pieces[0].start_xy()
+    fill_present(r.present, r.mask)
+    for copy in local:
+        copy.wait()
+    p0, p1, p2, p3, p4, p5 = pieces
+
+    def z_steps(piece):
+        return [lambda k=k: piece.z(k) for k in ORDER] + [piece.own_column]
+
+    def xy_steps(piece):
+        return [lambda k=k: piece.xy(k) for k in (0, 1, 3, 2)]
+
+    def run(steps):
+        for one in steps:
+            one()
+
+    outgoing = []
+
+    def write(source, target, index):
+        copy = pltpu.make_async_copy(source, target, r.write.at[index])
+        copy.start()
+        outgoing.append(copy)
+
+    run(z_steps(small)[:3])
+    run(z_steps(p0))
+    small.own_column()
+    run(xy_steps(small))
+    small.xy_columns()
+    p1.start_xy()
+    p0.xy(0)
+    small.d()
+    small.c()
+
+    rows = r.small_wide[...].reshape(256, 128).astype(jnp.bfloat16)
+    picked = dot(rows, selection(width))
+    owner = owners(width)
+    total = jnp.zeros((8, 7 * width), jnp.float32)
+    for d in range(32):
+        total = total + jnp.where(owner == d, picked[d * 8 : d * 8 + 8], 0.0)
+    r.vec[...] = total
+    r.bias[:, 0:width] = total[2:3, width : 2 * width]
+    r.bias[:, width : 2 * width] = jnp.zeros((1, width), jnp.float32)
+    r.bias[:, 2 * width : 3 * width] = total[2:3, 2 * width : 3 * width]
+    write(r.vec, r.vec_out, 0)
+
+    def first_norm(t):
+        rows = span(t * 128, 128, 128)
+        normed, _ = unit(r.tokens[rows, :].astype(jnp.float32))
+        value = normed * r.vec[0:1, 0:width] + r.vec[1:2, 0:width]
+        r.normed[rows, :] = value.astype(jnp.bfloat16)
+        r.turned_one[:, rows] = value.T.astype(jnp.bfloat16)
+
+    loop(tokens // 128, first_norm)
+    write(r.turned_one, r.turned_one_out, 1)
+    run(xy_steps(p0)[1:])
+    p0.xy_columns()
+    run(z_steps(p1))
+    p0.d()
+    p2.start_xy()
+    p0.c()
+    write(r.qkv_wide, r.qkv_wide_out, 2)
+
+    def project(t):
+        cols = span(t * width, width, 128)
+        r.joined[:, cols] = (
+            dot(r.normed[...], r.qkv_wide[:, :, :, cols].reshape(width, width)) + r.bias[:, cols]
+        ).astype(jnp.bfloat16)
+
+    xy1 = xy_steps(p1)
+    loop(3, project, [xy1[:2], xy1[2:3], xy1[3:] + [p1.xy_columns]])
+    write(r.joined, r.joined_out, 3)
+
+    def attend(hp):
+        cols = span(hp * 128, 128, 128)
+        query = r.joined[:, cols]
+        key = r.joined[:, span(width + hp * 128, 128, 128)]
+        value = r.joined[:, span(2 * width + hp * 128, 128, 128)].T
+        live = r.present[:, 0:1] > 0.5
+        mixed = []
+        for e in range(2):
+            scores = dot_nt(head_only(key, e), query) * SCORE_SCALE
+            scores = jnp.where(live, scores, -jnp.inf)
+            largest = jnp.max(scores, axis=0, keepdims=True)
+            expo = jnp.exp2(scores - largest)
+            totals = jnp.sum(expo, axis=0, keepdims=True)
+            probs = (expo * (1.0 / totals)).astype(jnp.bfloat16)
+            mixed.append(dot(value[HEAD * e : HEAD * (e + 1)], probs))
+            r.logsum[hp, e : e + 1, :] = largest + jnp.log2(totals)
+        both = jnp.concatenate(mixed, axis=0)
+        r.mixed_turned[cols, :] = both.astype(jnp.bfloat16)
+        r.mixed[:, cols] = both.T.astype(jnp.bfloat16)
+
+    z2 = z_steps(p2)
+    xy2 = xy_steps(p2)
+    loop(
+        pairs,
+        attend,
+        [z2, [p1.d, p3.start_xy], xy2[:1], xy2[1:2], xy2[2:3], xy2[3:] + [p2.xy_columns]],
+    )
+    write(r.logsum, r.logsum_out, 4)
+    write(r.mixed_turned, r.mixed_turned_out, 5)
+    p1.c()
+    run(z_steps(p3))
+    write(r.out_wide, r.out_wide_out, 6)
+    r.middle[...] = dot(r.mixed[...], r.out_wide[...].reshape(width, width))
+
+    def second_norm(t):
+        rows = span(t * 128, 128, 128)
+        present = r.present[rows, 0:1]
+        middle = r.tokens[rows, :].astype(jnp.float32) + present * (
+            r.middle[rows, :] + r.vec[3:4, 0:width]
+        )
+        r.middle[rows, :] = middle
+        normed, _ = unit(middle)
+        value = normed * r.vec[4:5, 0:width] + r.vec[5:6, 0:width]
+        r.normed[rows, :] = value.astype(jnp.bfloat16)
+        r.turned_two[:, rows] = value.T.astype(jnp.bfloat16)
+        r.grad_low[rows, :] = (present * r.out_grad[rows, :].astype(jnp.float32)).astype(
+            jnp.bfloat16
+        )
+
+    loop(tokens // 128, second_norm)
+    write(r.middle, r.middle_out, 7)
+    write(r.turned_two, r.turned_two_out, 8)
+    p2.d()
+    p4.start_xy()
+    p2.c()
+
+    def expand(t):
+        cols = span(t * TILE, TILE, 128)
+        value = (
+            dot(r.normed[...], r.up_wide[:, :, :, cols].reshape(width, TILE))
+            + r.vec[6:7, span(3 * width + t * TILE, TILE, 128)]
+        )
+        cumulative = 0.5 * (1.0 + lax.erf(value * (1.0 / math.sqrt(2.0))))
+        r.act[t] = (value * cumulative).astype(jnp.bfloat16)
+        r.slope[t] = cumulative + value * jnp.exp(-0.5 * value * value) * (
+            1.0 / math.sqrt(2.0 * math.pi)
+        )
+
+    def down_grad(t):
+        grad = dot_tn(r.act[t], r.grad_low[...]).astype(jnp.bfloat16)
+        r.down_grad[t // 2, pl.ds((t % 2) * 2, 2)] = grad.reshape(2, TILE // 2, width)
+
+    xy3 = xy_steps(p3)
+    loop(4, lambda u: expand(u + 2 * (u // 2)), [[s] for s in xy3])
+    p3.xy_columns()
+    run(z_steps(p4))
+    loop(4, lambda u: down_grad(u + 2 * (u // 2)))
+    p3.d()
+    p5.start_xy()
+    p3.c()
+    write(r.up_wide, r.up_wide_out, 9)
+    xy4 = xy_steps(p4)
+    loop(4, lambda u: expand(u + 2 * (u // 2) + 2), [[s] for s in xy4])
+    p4.xy_columns()
+    write(r.act, r.act_out, 10)
+    write(r.slope, r.slope_out, 11)
+    run(z_steps(p5))
+    loop(4, lambda u: down_grad(u + 2 * (u // 2) + 2))
+    write(r.down_grad, r.down_grad_out, 12)
+    p4.d()
+    run(xy_steps(p5))
+    p5.xy_columns()
+    p4.c()
+    p5.d()
+    p5.c()
+    write(r.down_wide, r.down_wide_out, 13)
+    for i in range(4):
+        before(i).wait_send()
+    for piece in [small] + pieces:
+        piece.finish()
+    for copy in outgoing:
+        copy.wait()
+
+
+def forward_call(tokens, band_mask, out_grad, shards, small):
+    bf16, f32 = jnp.bfloat16, jnp.float32
+    count, width = tokens.shape
+    shapes = [s.shape for s in shards]
+    hidden = shapes[2][1]
+    tiles = hidden // TILE
+    vmem = pl.BlockSpec(memory_space=pltpu.VMEM)
+    inputs = triples(
+        tokens=(tokens, vmem),
+        mask=(band_mask, pl.BlockSpec(memory_space=pltpu.SMEM)),
+        out_grad=(out_grad, vmem),
+        qkv_shard=(shards[0], vmem),
+        out_shard=(shards[1], vmem),
+        up_shard=(shards[2], vmem),
+        down_shard=(shards[3], vmem),
+        small=(small, vmem),
+    )
+    kept = triples(
+        vec=((8, 7 * width), f32),
+        turned_one=((width, count), bf16),
+        qkv_wide=((4, 4, 2 * shapes[0][0], shapes[0][1]), bf16),
+        joined=((count, 3 * width), bf16),
+        logsum=((width // 128, 8, count), f32),
+        mixed_turned=((width, count), bf16),
+        out_wide=((4, 4, 2 * shapes[1][0], shapes[1][1]), bf16),
+        middle=((count, width), f32),
+        turned_two=((width, count), bf16),
+        up_wide=((4, 4, 2 * shapes[2][0], shapes[2][1]), bf16),
+        act=((tiles, count, TILE), bf16),
+        slope=((tiles, count, TILE), f32),
+        down_grad=((4, 4, 2 * shapes[3][0], shapes[3][1]), bf16),
+        down_wide=((4, 4, 2 * shapes[3][0], shapes[3][1]), bf16),
+    )
+    scratch = [(name, pltpu.VMEM(shape, kind)) for name, shape, kind in kept]
+    for name, (rows, cols) in zip(MATRICES, shapes):
+        scratch.append((name + "_own", pltpu.VMEM((2 * rows, cols // 2), bf16)))
+        scratch.append((name + "_sib", pltpu.VMEM((rows, cols // 2), f32)))
+    scratch += pairs_of(
+        small_wide=pltpu.VMEM((4, 4, 2, 8, 128), f32),
+        present=pltpu.VMEM((count, 128), f32),
+        bias=pltpu.VMEM((1, 3 * width), f32),
+        normed=pltpu.VMEM((count, width), bf16),
+        mixed=pltpu.VMEM((count, width), bf16),
+        grad_low=pltpu.VMEM((count, width), bf16),
+        send=pltpu.SemaphoreType.DMA((7, Piece.COUNT)),
+        recv=pltpu.SemaphoreType.DMA((7, Piece.COUNT)),
+        pre_send=pltpu.SemaphoreType.DMA((4,)),
+        pre_recv=pltpu.SemaphoreType.DMA((4,)),
+        local=pltpu.SemaphoreType.DMA((5,)),
+        write=pltpu.SemaphoreType.DMA((len(kept),)),
+    )
+    names = (
+        [name for name, _, _ in inputs]
+        + [name + "_out" for name, _, _ in kept]
+        + [name for name, _ in scratch]
+    )
+    results = pl.pallas_call(
+        functools.partial(forward_kernel, names),
+        out_shape=tuple(jax.ShapeDtypeStruct(shape, kind) for _, shape, kind in kept),
+        in_specs=[spec for _, _, spec in inputs],
+        out_specs=(pl.BlockSpec(memory_space=pl.ANY),) * len(kept),
+        scratch_shapes=[kind for _, kind in scratch],
+        compiler_params=pltpu.CompilerParams(
+            collective_id=0, has_side_effects=True, vmem_limit_bytes=VMEM_BYTES
+        ),
+        name="forward",
+    )(*[array for _, array, _ in inputs])
+    return dict(zip([name for name, _, _ in kept], results))
+
+
+def backward_kernel(names, *refs):
+    r = Named(names, refs)
+    place = Place()
+    tokens, width = r.tokens.shape
+    hidden = r.dpre.shape[1]
+    pairs = width // 128
+    tiles = hidden // TILE
+    c = place.c
+
+    def fetch(name, index):
+        return pltpu.make_async_copy(getattr(r, name + "_in"), getattr(r, name), r.load.at[index])
+
+    wanted = WANTED
+
+    def need(*some):
+        for name in some:
+            fetch(name, wanted.index(name)).wait()
+
+    def stream(t, slot):
+        return (
+            pltpu.make_async_copy(r.act_in.at[t], r.act.at[slot], r.tile.at[0, slot]),
+            pltpu.make_async_copy(r.slope_in.at[t], r.slope.at[slot], r.tile.at[1, slot]),
+            pltpu.make_async_copy(
+                r.down_wide_in.at[t // 2, pl.ds((t % 2) * 2, 2)],
+                r.down_tile.at[slot],
+                r.tile.at[2, slot],
+            ),
+        )
+
+    def down_mine(s):
+        return pltpu.make_async_copy(
+            r.down_grad_in.at[:, :, pl.ds(96 * s, 96), span(c * 384, 384, 128)],
+            r.down_mine.at[s],
+            r.mine.at[s],
+        )
+
+    for s in range(2):
+        down_mine(s).start()
+    for copy in stream(0, 0):
+        copy.start()
+    for i, name in enumerate(wanted):
+        fetch(name, i).start()
+    meet(place)
+    pieces = []
+    for j in range(9):
+        bufs = [getattr(r, "piece%d_%d" % (j, b)) for b in range(6)]
+        pieces.append(Scatter(place, bufs, r.send.at[j], r.recv.at[j]))
+    d0, d1, u0, u1, o, q0, q1, q2, small = pieces
+    for s, piece in enumerate((d0, d1)):
+        piece.give(
+            lambda q, s=s: r.down_grad_in.at[
+                :, q, pl.ds(96 * s, 96), span((1 - c) * 384, 384, 128)
+            ]
+        )
+    fill_present(r.present, r.mask)
+    r.sums[...] = jnp.zeros_like(r.sums)
+    r.acc[...] = jnp.zeros_like(r.acc)
+
+    def mask_grad(t):
+        rows = span(t * 128, 128, 128)
+        low = (r.present[rows, 0:1] * r.out_grad[rows, :].astype(jnp.float32)).astype(jnp.bfloat16)
+        r.grad_low[rows, :] = low
+        r.sums[7:8, 0:width] += jnp.sum(low.astype(jnp.float32), axis=0, keepdims=True)
+
+    loop(tokens // 128, mask_grad)
+
+    def take_down(piece, s, i):
+        if i == 0:
+            down_mine(s).wait()
+        piece.take(i, lambda zz, q: r.down_mine.at[s, zz, q])
+
+    def narrow(t):
+        slot = t % 2
+        for copy in stream(t, slot):
+            copy.wait()
+
+        @pl.when(t + 1 < tiles)
+        def _():
+            for copy in stream(t + 1, 1 - slot):
+                copy.start()
+
+        cols = span(t * TILE, TILE, 128)
+        weights = r.down_tile[slot].reshape(TILE, width)
+        r.acc[...] += dot(r.act[slot], weights)
+        grad = (dot_nt(r.grad_low[...], weights) * r.slope[slot]).astype(jnp.bfloat16)
+        r.dpre[:, cols] = grad
+        r.sums[6:7, span(3 * width + t * TILE, TILE, 128)] = jnp.sum(
+            grad.astype(jnp.float32), axis=0, keepdims=True
+        )
+
+    def cross_steps(piece):
+        return [lambda k=k: piece.cross(k) for k in (1, 3, 2, 0)]
+
+    def spread_steps(piece):
+        return [lambda k=k: piece.spread(k) for k in ORDER]
+
+    def run(steps):
+        for one in steps:
+            one()
+
+    xd0, xd1, xu0, xu1, xo = [cross_steps(p) for p in (d0, d1, u0, u1, o)]
+    take_down(d0, 0, 0)
+    d0.diagonal()
+    loop(
+        tiles,
+        narrow,
+        [
+            [lambda: take_down(d0, 0, 1), lambda: take_down(d0, 0, 2)],
+            [lambda: take_down(d1, 1, 0), d1.diagonal],
+            xd0[:1],
+            xd0[1:2] + [lambda: take_down(d1, 1, 1)],
+            xd0[2:3] + [lambda: take_down(d1, 1, 2)],
+            xd0[3:] + [lambda: take_down(d0, 0, 3)],
+            [lambda: take_down(d1, 1, 3)],
+            xd1[:1],
+        ],
+    )
+
+    need("vec", "middle")
+
+    def finish_output(t):
+        rows = span(t * 128, 128, 128)
+        r.output[rows, :] = (
+            r.middle[rows, :]
+            + r.present[rows, 0:1] * (r.acc[rows, :] + r.vec[7:8, 0:width])
+        ).astype(jnp.bfloat16)
+
+    need("turned_two", "up_wide")
+
+    def up_part(side, s):
+        cols = span(side * (hidden // 2) + 768 * s, 768, 128)
+        return dot(r.turned_two[...], r.dpre[:, cols]).reshape(4, 4, 48, 768)
+
+    for s, (piece, part) in enumerate(((u0, r.up_part0), (u1, r.up_part1))):
+        part[...] = up_part(1 - c, s).astype(jnp.bfloat16)
+        piece.give(lambda q, part=part: part.at[:, q])
+    run(xd1[1:2])
+    for s, piece in enumerate((u0, u1)):
+        for i in range(4):
+            piece.arrive(i)
+        piece.total[...] = (
+            piece.total[...].astype(jnp.float32) + up_part(c, s)
+        ).astype(jnp.bfloat16)
+        if s == 0:
+            piece.diagonal()
+            run(xd1[2:])
+    run(spread_steps(d0))
+    u1.diagonal()
+    loop(tokens // 128, finish_output)
+    r.acc[...] = dot_nt(r.dpre[...], r.up_wide[...].reshape(width, hidden))
+
+    def second_back(t):
+        rows = span(t * 128, 128, 128)
+        normed, factor = unit(r.middle[rows, :])
+        up = r.acc[rows, :]
+        r.sums[4:5, 0:width] += jnp.sum(up * normed, axis=0, keepdims=True)
+        r.sums[5:6, 0:width] += jnp.sum(up, axis=0, keepdims=True)
+        scaled = up * r.vec[4:5, 0:width]
+        inner = (
+            scaled
+            - jnp.mean(scaled, axis=1, keepdims=True)
+            - normed * jnp.mean(scaled * normed, axis=1, keepdims=True)
+        )
+        grad = r.out_grad[rows, :].astype(jnp.float32) + factor * inner
+        r.middle[rows, :] = grad
+        low = (r.present[rows, 0:1] * grad).astype(jnp.bfloat16)
+        r.attention_low[rows, :] = low
+        r.sums[3:4, 0:width] += jnp.sum(low.astype(jnp.float32), axis=0, keepdims=True)
+
+    loop(tokens // 128, second_back, [xu0[:1], xu0[1:2], xu0[2:3], xu0[3:]])
+    need("mixed_turned", "out_wide")
+
+    def out_part(side):
+        cols = span(side * (width // 2), width // 2, 128)
+        return dot(r.mixed_turned[...], r.attention_low[:, cols]).reshape(4, 4, 48, width // 2)
+
+    r.out_part[...] = out_part(1 - c).astype(jnp.bfloat16)
+    o.give(lambda q: r.out_part.at[:, q])
+    r.mixed_grad[...] = dot_nt(r.attention_low[...], r.out_wide[...].reshape(width, width)).astype(
+        jnp.bfloat16
+    )
+    for i in range(4):
+        o.arrive(i)
+    o.total[...] = (o.total[...].astype(jnp.float32) + out_part(c)).astype(jnp.bfloat16)
+    o.diagonal()
+    run(spread_steps(d1))
+    need("joined", "logsum")
+
+    def attend_back(hp):
+        cols = span(hp * 128, 128, 128)
+        key_cols = span(width + hp * 128, 128, 128)
+        value_cols = span(2 * width + hp * 128, 128, 128)
+        query = r.joined[:, cols]
+        key = r.joined[:, key_cols]
+        value = r.joined[:, value_cols]
+        grad = r.mixed_grad[:, cols]
+        turned = key.T
+        live = r.present[:, 0:1] > 0.5
+        value_grad = jnp.zeros((tokens, 128), jnp.float32)
+        key_grad = jnp.zeros((tokens, 128), jnp.float32)
+        query_grad = []
+        for e in range(2):
+            scores = dot_nt(head_only(key, e), query) * SCORE_SCALE
+            scores = jnp.where(live, scores, -jnp.inf)
+            probs = jnp.exp2(scores - r.logsum[hp, e : e + 1, :])
+            back = dot_nt(head_only(value, e), grad)
+            inner = jnp.sum(probs * back, axis=0, keepdims=True)
+            score_grad = (probs * (back - inner)).astype(jnp.bfloat16)
+            value_grad = value_grad + dot(probs.astype(jnp.bfloat16), head_only(grad, e))
+            key_grad = key_grad + dot(score_grad, head_only(query, e))
+            query_grad.append(dot(turned[HEAD * e : HEAD * (e + 1)], score_grad))
+        scale = 1.0 / math.sqrt(HEAD)
+        query_low = (jnp.concatenate(query_grad, axis=0).T * scale).astype(jnp.bfloat16)
+        value_low = value_grad.astype(jnp.bfloat16)
+        r.joined_grad[:, cols] = query_low
+        r.joined_grad[:, key_cols] = (key_grad * scale).astype(jnp.bfloat16)
+        r.joined_grad[:, value_cols] = value_low
+        r.sums[2:3, span(width + hp * 128, 128, 128)] = jnp.sum(
+            query_low.astype(jnp.float32), axis=0, keepdims=True
+        )
+        r.sums[2:3, span(2 * width + hp * 128, 128, 128)] = jnp.sum(
+            value_low.astype(jnp.float32), axis=0, keepdims=True
+        )
+
+    loop(
+        pairs,
+        attend_back,
+        [xu1[:1], xu1[1:2], xu1[2:3], xu1[3:] + spread_steps(u0)[:1], spread_steps(u0)[1:], xo],
+    )
+
+    need("turned_one", "qkv_wide")
+
+    def qkv_part(side, s):
+        cols = span(side * (3 * width // 2) + 384 * s, 384, 128)
+        return dot(r.turned_one[...], r.joined_grad[:, cols]).reshape(4, 4, 48, 384)
+
+    qs = (q0, q1, q2)
+    for s, (piece, part) in enumerate(zip(qs, (r.qkv_part0, r.qkv_part1, r.qkv_part2))):
+        part[...] = qkv_part(1 - c, s).astype(jnp.bfloat16)
+        piece.give(lambda q, part=part: part.at[:, q])
+    for s, piece in enumerate(qs):
+        for i in range(4):
+            piece.arrive(i)
+        piece.total[...] = (
+            piece.total[...].astype(jnp.float32) + qkv_part(c, s)
+        ).astype(jnp.bfloat16)
+        piece.diagonal()
+    run(spread_steps(u1))
+    r.acc[...] = dot_nt(r.joined_grad[...], r.qkv_wide[...].reshape(width, 3 * width))
+
+    def first_back(t):
+        rows = span(t * 128, 128, 128)
+        normed, factor = unit(r.tokens[rows, :].astype(jnp.float32))
+        up = r.acc[rows, :]
+        r.sums[0:1, 0:width] += jnp.sum(up * normed, axis=0, keepdims=True)
+        r.sums[1:2, 0:width] += jnp.sum(up, axis=0, keepdims=True)
+        scaled = up * r.vec[0:1, 0:width]
+        inner = (
+            scaled
+            - jnp.mean(scaled, axis=1, keepdims=True)
+            - normed * jnp.mean(scaled * normed, axis=1, keepdims=True)
+        )
+        r.input_grad[rows, :] = (r.middle[rows, :] + factor * inner).astype(jnp.bfloat16)
+
+    loop(tokens // 128, first_back)
+    owner = owners(width)
+    sums = r.sums[...]
+    high = sums.astype(jnp.bfloat16)
+    rest = sums - high.astype(jnp.float32)
+    mid = rest.astype(jnp.bfloat16)
+    low = (rest - mid.astype(jnp.float32)).astype(jnp.bfloat16)
+    chosen = selection(width)
+    tile = jnp.zeros((256, 128), jnp.float32)
+    for part in (high, mid, low):
+        part = part.astype(jnp.float32)
+        spreaded = jnp.concatenate(
+            [jnp.where(owner == d, part, 0.0) for d in range(32)], axis=0
+        ).astype(jnp.bfloat16)
+        tile = tile + dot_nt(spreaded, chosen)
+    r.small_part[...] = tile.reshape(4, 4, 2, 8, 128)
+    small.give(lambda q: r.small_part.at[:, q, 1 - c])
+    run(cross_steps(q0))
+    for i in range(4):
+        small.take(i, lambda zz, q: r.small_part.at[zz, q, c])
+    small.diagonal()
+    run(spread_steps(o))
+    run(cross_steps(q1))
+    run(cross_steps(small))
+    run(spread_steps(q0))
+    run(cross_steps(q2))
+    run(spread_steps(small))
+
+    finals = (r.down_final, r.up_final, r.out_final, r.qkv_final)
+    others = (r.down_other, r.up_other, r.out_other, r.qkv_other)
+    results = (r.down_result, r.up_result, r.out_result, r.qkv_result)
+
+    def swap(i):
+        rows = results[i].shape[0]
+        return remote(
+            finals[i].at[span((1 - c) * rows, rows, 8)],
+            others[i],
+            r.end_send.at[i],
+            r.end_recv.at[i],
+            place.to_c,
+        )
+
+    def close(i):
+        rows, cols = results[i].shape
+        swap(i).start()
+        results[i][:, span(c * (cols // 2), cols // 2, 128)] = finals[i][span(c * rows, rows, 8)]
+
+    def settle(i):
+        cols = results[i].shape[1]
+        swap(i).wait_recv()
+        results[i][:, span((1 - c) * (cols // 2), cols // 2, 128)] = others[i][...]
+
+    r.down_final[0:96, :] = d0.last()
+    r.down_final[96:192, :] = d1.last()
+    close(0)
+    r.up_final[:, 0:768] = u0.last()
+    r.up_final[:, 768:1536] = u1.last()
+    close(1)
+    r.out_final[...] = o.last()
+    close(2)
+    run(spread_steps(q1))
+    r.qkv_final[:, 0:384] = q0.last()
+    run(spread_steps(q2))
+    r.small_result[...] = small.last()
+    r.qkv_final[:, 384:768] = q1.last()
+    settle(0)
+    settle(1)
+    settle(2)
+    r.qkv_final[:, 768:1152] = q2.last()
+    close(3)
+    settle(3)
+    for i in range(4):
+        swap(i).wait_send()
+    for piece in pieces:
+        piece.finish()
+
+
+def backward_call(tokens, band_mask, out_grad, kept, shapes):
+    bf16, f32 = jnp.bfloat16, jnp.float32
+    count, width = tokens.shape
+    hidden = shapes[2][1]
+    vmem = pl.BlockSpec(memory_space=pltpu.VMEM)
+    anywhere = pl.BlockSpec(memory_space=pl.ANY)
+    inputs = triples(
+        tokens=(tokens, vmem),
+        mask=(band_mask, pl.BlockSpec(memory_space=pltpu.SMEM)),
+        out_grad=(out_grad, vmem),
+    ) + [(name + "_in", array, anywhere) for name, array in kept.items()]
+    outs = triples(
+        output=((count, width), bf16),
+        input_grad=((count, width), bf16),
+        qkv_result=(shapes[0], f32),
+        out_result=(shapes[1], f32),
+        up_result=(shapes[2], f32),
+        down_result=(shapes[3], f32),
+        small_result=((8, 128), f32),
+    )
+    tails = (
+        [((96, 384), bf16)] * 2
+        + [((48, 768), bf16)] * 2
+        + [((48, 384), bf16)] * 4
+        + [((8, 128), f32)]
+    )
+    scratch = []
+    for j, (tail, kind) in enumerate(tails):
+        for b, one in enumerate(scatter_buffers(tail, kind)):
+            scratch.append(("piece%d_%d" % (j, b), one))
+    for name in WANTED:
+        scratch.append((name, pltpu.VMEM(kept[name].shape, kept[name].dtype)))
+    for name, (rows, cols) in zip(MATRICES, shapes):
+        scratch.append((name + "_final", pltpu.VMEM((2 * rows, cols // 2), f32)))
+        scratch.append((name + "_other", pltpu.VMEM((rows, cols // 2), f32)))
+    scratch += pairs_of(
+        act=pltpu.VMEM((2, count, TILE), bf16),
+        slope=pltpu.VMEM((2, count, TILE), f32),
+        down_tile=pltpu.VMEM((2, 2, TILE // 2, width), bf16),
+        down_mine=pltpu.VMEM((2, 4, 4, 96, 384), bf16),
+        up_part0=pltpu.VMEM((4, 4, 48, 768), bf16),
+        up_part1=pltpu.VMEM((4, 4, 48, 768), bf16),
+        out_part=pltpu.VMEM((4, 4, 48, 384), bf16),
+        qkv_part0=pltpu.VMEM((4, 4, 48, 384), bf16),
+        qkv_part1=pltpu.VMEM((4, 4, 48, 384), bf16),
+        qkv_part2=pltpu.VMEM((4, 4, 48, 384), bf16),
+        small_part=pltpu.VMEM((4, 4, 2, 8, 128), f32),
+        present=pltpu.VMEM((count, 128), f32),
+        sums=pltpu.VMEM((8, 7 * width), f32),
+        acc=pltpu.VMEM((count, width), f32),
+        grad_low=pltpu.VMEM((count, width), bf16),
+        dpre=pltpu.VMEM((count, hidden), bf16),
+        attention_low=pltpu.VMEM((count, width), bf16),
+        mixed_grad=pltpu.VMEM((count, width), bf16),
+        joined_grad=pltpu.VMEM((count, 3 * width), bf16),
+        send=pltpu.SemaphoreType.DMA((len(tails), Piece.COUNT)),
+        recv=pltpu.SemaphoreType.DMA((len(tails), Piece.COUNT)),
+        end_send=pltpu.SemaphoreType.DMA((4,)),
+        end_recv=pltpu.SemaphoreType.DMA((4,)),
+        load=pltpu.SemaphoreType.DMA((10,)),
+        tile=pltpu.SemaphoreType.DMA((3, 2)),
+        mine=pltpu.SemaphoreType.DMA((2,)),
+    )
+    names = (
+        [name for name, _, _ in inputs] + [name for name, _, _ in outs] + [name for name, _ in scratch]
+    )
+    results = pl.pallas_call(
+        functools.partial(backward_kernel, names),
+        out_shape=tuple(jax.ShapeDtypeStruct(shape, kind) for _, shape, kind in outs),
+        in_specs=[spec for _, _, spec in inputs],
+        out_specs=(vmem,) * len(outs),
+        scratch_shapes=[kind for _, kind in scratch],
+        compiler_params=pltpu.CompilerParams(
+            collective_id=1, has_side_effects=True, vmem_limit_bytes=VMEM_BYTES
+        ),
+        name="backward",
+    )(*[array for _, array, _ in inputs])
+    return dict(zip([name for name, _, _ in outs], results))
+
+
+def body(
+    tokens,
+    band_mask,
+    out_grad,
+    norm1_gain,
+    norm1_shift,
+    qkv_weight,
+    qv_bias,
+    out_weight,
+    out_bias,
+    norm2_gain,
+    norm2_shift,
+    up_weight,
+    up_bias,
+    down_weight,
+    down_bias,
+):
+    smalls = (norm1_gain, norm1_shift, qv_bias, out_bias, norm2_gain, norm2_shift, up_bias, down_bias)
+    shards = (qkv_weight, out_weight, up_weight, down_weight)
+    packed = jnp.stack([jnp.pad(v, (0, 128 - v.shape[0])) for v in smalls])
+    kept = forward_call(tokens, band_mask, out_grad, shards, packed)
+    done = backward_call(tokens, band_mask, out_grad, kept, [s.shape for s in shards])
+    tile = done["small_result"]
+    grads = [tile[i, : v.shape[0]] for i, v in enumerate(smalls)]
+    return (
+        done["output"],
+        done["input_grad"],
+        grads[0],
+        grads[1],
+        done["qkv_result"],
+        grads[2],
+        done["out_result"],
+        grads[3],
+        grads[4],
+        grads[5],
+        done["up_result"],
+        grads[6],
+        done["down_result"],
+        grads[7],
+    )
+
+
 def solution(mesh):
-    placed = (
-        P(("wide", "narrow"), None),
-        P(("wide", "narrow"), None),
-        P(("wide", "narrow"), None),
-        P(("wide", "narrow")),
-        P(("wide", "narrow")),
-        P(("wide", "narrow"), None),
-        P(("wide", "narrow")),
-        P(("wide", "narrow"), None),
-        P(("wide", "narrow")),
-        P(("wide", "narrow")),
-        P(("wide", "narrow")),
-        P(("wide", "narrow"), None),
-        P(("wide", "narrow")),
-        P(("wide", "narrow"), None),
-        P(("wide", "narrow")),
-    )
+    rows, flat = P(AXES, None), P(AXES)
+    params = (flat, flat, rows, flat, rows, flat, flat, flat, rows, flat, rows, flat)
+    fitted = tuple(mesh.shape[axis] for axis in AXES) == (8, 4)
     return jax.shard_map(
-        body,
+        body if fitted else body_plain,
         mesh=mesh,
-        in_specs=placed,
-        out_specs=(
-            P(("wide", "narrow"), None),
-            P(("wide", "narrow"), None),
-            P(("wide", "narrow")),
-            P(("wide", "narrow")),
-            P(("wide", "narrow"), None),
-            P(("wide", "narrow")),
-            P(("wide", "narrow"), None),
-            P(("wide", "narrow")),
-            P(("wide", "narrow")),
-            P(("wide", "narrow")),
-            P(("wide", "narrow"), None),
-            P(("wide", "narrow")),
-            P(("wide", "narrow"), None),
-            P(("wide", "narrow")),
-        ),
+        in_specs=(rows, rows, rows) + params,
+        out_specs=(rows, rows) + params,
         check_vma=False,
     )

time: 806 us -> 186 us (0.23); the launches traced: 797 us -> 186 us
  waiting for transfers between devices: 529 us -> 0 us
  Pallas kernels: 0 us -> 170 us
  matrix products: 111 us -> 0 us
  blocking collectives: 83.2 us -> 0 us
  other arithmetic: 29.4 us -> 0 us
  between operations: 14.9 us -> 0.69 us
  local copies, waits for them, and re-layouts: 28.6 us -> 15 us
    reduce_scatter x4 -> x0, waiting for transfers between devices: 376 us -> none  [the longest x1 142 us: body(): lax.psum_scatter(down_weight_grad, ('wide', 'narrow'), scatter_dimension=...]
    pallas_call x0 -> x2, Pallas kernels: none -> 170 us  [the longest x1 85.8 us: forward_call(): pl.pallas_call(functools.partial(forward_kernel, names), out_shape=tuple(...]
    all_gather x4 -> x0, waiting for transfers between devices: 153 us -> none  [the longest x1 62.2 us: body(): lax.all_gather(up_weight.astype(jnp.bfloat16), ('wide', 'narrow'), axis=0...]
    dot_general x33 -> x0, matrix products: 111 us -> none  [the longest x1 20.3 us: body(): jnp.dot(normed_two, w_up, preferred_element_type=jnp.float32)]
    unnamed x2 -> x0, blocking collectives: 83.2 us -> none
    convert_element_type x24 -> x0, other arithmetic: 20 us -> none  [the longest x3 4.21 us: one_block(): score_grad = (probs * (prob_grad - inner)).astype(jnp.bfloat16)]
    reduce_sum x9 -> x0, other arithmetic: 9.29 us -> none  [the longest x3 2.72 us: one_block(): totals = jnp.sum(expo, axis=2, keepdims=True)]
  transfers between devices with their start and end apart: 8 -> 0, of which waited for: 7 -> 0; matrix products, arithmetic and copies ran while one was open for 18% -> 0% of each run, Pallas kernels for 0% -> 0%
where the time goes in v1:
time: 186 us
  Pallas kernels  170 us (91%)
  local copies, waits for them, and re-layouts  15 us (8%)
    pallas_call x1, Pallas kernels, forward_call(): pl.pallas_call(functools.partial(forward_kernel, names), out_shape=tuple(...  85.8 us
    pallas_call x1, Pallas kernels, backward_call(): pl.pallas_call(functools.partial(backward_kernel, names), out_shape=tuple...  84.4 us
    unnamed x12, local copies, waits for them, and re-layouts  7.83 us
    squeeze x3, local copies, waits for them, and re-layouts, body(): grads = [tile[i, :v.shape[0]] for i, v in enumerate(smalls)]  3.89 us

profile of v1, /device:TPU:0, one launch (start us, length us, event | category | flops | bytes accessed | tf_op | source)
XLA Modules:
  0.0 185.9 jit_solution(10165877995811487371)
XLA Ops:
  0.6 0.7 pad_bitcast_fusion.6
  1.3 0.7 pad_bitcast_fusion.4
  2.0 0.7 pad_bitcast_fusion.2
  2.7 0.7 pad_bitcast_fusion
  3.3 0.6 stack.35.refs_7_
  4.0 85.8 %forward.1 = (f32[8,5376]{1,0:T(8,128)}, bf16[768,512]{1,0:T(8,128)(2,1)}, bf16[4,4,48,2304]{3,2,1,0:T(8,128)(2,1)}, bf16[512,2304]{1,0:T(8,128)(2,1)}, f32[6,8,...) custom-call(bf16[512,768]{1,0:T(8,128)(2,1)} %refs_0_.3, ...), custom_call_target="tpu_custom_call" | custom-call | tf_op jit(solution)/shard_map/forward/pallas_call | solution.py:967
  89.7 84.4 %backward.1 = (bf16[512,768]{1,0:T(8,128)(2,1)}, bf16[512,768]{1,0:T(8,128)(2,1)}, f32[24,2304]{1,0:T(8,128)}, f32[24,768]{1,0:T(8,128)}, f32[24,3072]{1,0:T(8,1...) custom-call(bf16[512,768]{1,0:T(8,128)(2,1)} %refs_0_.3, s32[1,8]{1,0:T(1,128)} %refs_1_.3, bf16[512,768]{1,0:T(8,128)(2,1)} %refs_2_.3, ...), custom_call_target="tpu_custom_call" | custom-call | tf_op jit(solution)/shard_map/backward/pallas_call | solution.py:1388
  174.1 0.0 copy-start.2
  174.1 0.0 copy-start.1
  174.1 0.0 copy-start
  174.1 1.3 slice_bitcast_fusion.5
  175.4 1.2 slice_bitcast_fusion.1
  176.6 1.4 slice_bitcast_fusion
  178.0 2.1 %copy.35 = bf16[512,768]{1,0:T(8,128)(2,1)} copy(bf16[512,768]{1,0:T(8,128)(2,1)} %get-tuple-element.84) | data formatting | bytes 1572864
  180.1 2.1 %copy.36 = bf16[512,768]{1,0:T(8,128)(2,1)} copy(bf16[512,768]{1,0:T(8,128)(2,1)} %get-tuple-element.85) | data formatting | bytes 1572864
  182.2 1.6 copy.37
  183.8 0.0 copy-done.2
  183.8 0.6 copy.38
  184.4 0.0 copy-done.1
  184.4 0.7 copy.39
  185.1 0.0 copy-done
  185.1 0.7 copy.40
Async XLA Ops:
  174.1 9.7 %copy-start.2 = (f32[24,768]{1,0:T(8,128)S(1)}, f32[24,768]{1,0:T(8,128)}, u32[]{:S(2)}) copy-start(f32[24,768]{1,0:T(8,128)} %get-tuple-element.90) | copy-start | bytes 221188
  174.1 10.3 %copy-start.1 = (f32[24,3072]{1,0:T(8,128)S(1)}, f32[24,3072]{1,0:T(8,128)}, u32[]{:S(2)}) copy-start(f32[24,3072]{1,0:T(8,128)} %get-tuple-element.94) | copy-start | bytes 884740
  174.1 11.0 %copy-start = (f32[96,768]{1,0:T(8,128)S(1)}, f32[96,768]{1,0:T(8,128)}, u32[]{:S(2)}) copy-start(f32[96,768]{1,0:T(8,128)} %get-tuple-element.96) | copy-start | bytes 884740

commit v2 on v1

--- a/solution.py
+++ b/solution.py
@@ -672,6 +672,10 @@
 
     for i in range(4):
         before(i).start()
+    r.small[...] = jnp.zeros_like(r.small)
+    for i in range(8):
+        vector = getattr(r, "vector%d" % i)
+        r.small[i : i + 1, 0 : vector.shape[0]] = vector[...].reshape(1, -1)
     small = Gather(
         place,
         lambda: r.small,
@@ -908,7 +912,7 @@
         copy.wait()
 
 
-def forward_call(tokens, band_mask, out_grad, shards, small):
+def forward_call(tokens, band_mask, out_grad, shards, smalls):
     bf16, f32 = jnp.bfloat16, jnp.float32
     count, width = tokens.shape
     shapes = [s.shape for s in shards]
@@ -923,8 +927,7 @@
         out_shard=(shards[1], vmem),
         up_shard=(shards[2], vmem),
         down_shard=(shards[3], vmem),
-        small=(small, vmem),
-    )
+    ) + [("vector%d" % i, v, vmem) for i, v in enumerate(smalls)]
     kept = triples(
         vec=((8, 7 * width), f32),
         turned_one=((width, count), bf16),
@@ -946,6 +949,7 @@
         scratch.append((name + "_own", pltpu.VMEM((2 * rows, cols // 2), bf16)))
         scratch.append((name + "_sib", pltpu.VMEM((rows, cols // 2), f32)))
     scratch += pairs_of(
+        small=pltpu.VMEM((8, 128), f32),
         small_wide=pltpu.VMEM((4, 4, 2, 8, 128), f32),
         present=pltpu.VMEM((count, 128), f32),
         bias=pltpu.VMEM((1, 3 * width), f32),
@@ -1396,7 +1400,38 @@
         ),
         name="backward",
     )(*[array for _, array, _ in inputs])
-    return dict(zip([name for name, _, _ in outs], results))
+    return results
+
+
+def deliver_kernel(count, *refs):
+    sources, tile = refs[:count], refs[count]
+    targets = refs[count + 1 : 2 * count + 1]
+    vectors = refs[2 * count + 1 : -1]
+    copies = [
+        pltpu.make_async_copy(source, target, refs[-1].at[i])
+        for i, (source, target) in enumerate(zip(sources, targets))
+    ]
+    for copy in copies:
+        copy.start()
+    for i, vector in enumerate(vectors):
+        vector[...] = tile[i, 0 : vector.shape[0]]
+    for copy in copies:
+        copy.wait()
+
+
+def deliver(whole, tile, sizes):
+    count = len(whole)
+    anywhere = pl.BlockSpec(memory_space=pl.ANY)
+    vmem = pl.BlockSpec(memory_space=pltpu.VMEM)
+    return pl.pallas_call(
+        functools.partial(deliver_kernel, count),
+        out_shape=[jax.ShapeDtypeStruct(a.shape, a.dtype) for a in whole]
+        + [jax.ShapeDtypeStruct((m,), jnp.float32) for m in sizes],
+        in_specs=[anywhere] * count + [vmem],
+        out_specs=[anywhere] * count + [vmem] * len(sizes),
+        scratch_shapes=[pltpu.SemaphoreType.DMA((count,))],
+        name="deliver",
+    )(*whole, tile)
 
 
 def body(
@@ -1418,25 +1453,25 @@
 ):
     smalls = (norm1_gain, norm1_shift, qv_bias, out_bias, norm2_gain, norm2_shift, up_bias, down_bias)
     shards = (qkv_weight, out_weight, up_weight, down_weight)
-    packed = jnp.stack([jnp.pad(v, (0, 128 - v.shape[0])) for v in smalls])
-    kept = forward_call(tokens, band_mask, out_grad, shards, packed)
-    done = backward_call(tokens, band_mask, out_grad, kept, [s.shape for s in shards])
-    tile = done["small_result"]
-    grads = [tile[i, : v.shape[0]] for i, v in enumerate(smalls)]
+    kept = forward_call(tokens, band_mask, out_grad, shards, smalls)
+    *whole, tile = backward_call(tokens, band_mask, out_grad, kept, [s.shape for s in shards])
+    output, input_grad, qkv, out, up, down, *grads = deliver(
+        whole, tile, [v.shape[0] for v in smalls]
+    )
     return (
-        done["output"],
-        done["input_grad"],
+        output,
+        input_grad,
         grads[0],
         grads[1],
-        done["qkv_result"],
+        qkv,
         grads[2],
-        done["out_result"],
+        out,
         grads[3],
         grads[4],
         grads[5],
-        done["up_result"],
+        up,
         grads[6],
-        done["down_result"],
+        down,
         grads[7],
     )
 

time: 186 us -> 248 us (1.33)
  Pallas kernels: 170 us -> 247 us
  local copies, waits for them, and re-layouts: 15 us -> 0 us
    pallas_call x0 -> x1, Pallas kernels: none -> 76.8 us  [deliver(): pl.pallas_call(functools.partial(deliver_kernel, count), out_shape=[jax.S...]
    unnamed x12 -> x0, local copies, waits for them, and re-layouts: 7.83 us -> none
    squeeze x3 -> x0, local copies, waits for them, and re-layouts: 3.89 us -> none  [body(): grads = [tile[i, :v.shape[0]] for i, v in enumerate(smalls)]]
    another operation x5 -> x0, local copies, waits for them, and re-layouts: 3.31 us -> none  [body(): packed = jnp.stack([jnp.pad(v, (0, 128 - v.shape[0])) for v in smalls])]
where the time goes in v2:
time: 248 us
  Pallas kernels  247 us (100%)
    pallas_call x1, Pallas kernels, forward_call(): pl.pallas_call(functools.partial(forward_kernel, names), out_shape=tuple(...  85.8 us
    pallas_call x1, Pallas kernels, backward_call(): pl.pallas_call(functools.partial(backward_kernel, names), out_shape=tuple...  84.4 us
    pallas_call x1, Pallas kernels, deliver(): pl.pallas_call(functools.partial(deliver_kernel, count), out_shape=[jax.S...  76.8 us

profile of v2, /device:TPU:0, one launch (start us, length us, event | category | flops | bytes accessed | tf_op | source)
XLA Modules:
  0.0 247.9 jit_solution(17108541581060114128)
XLA Ops:
  0.6 85.8 %forward.1 = (f32[8,5376]{1,0:T(8,128)}, bf16[768,512]{1,0:T(8,128)(2,1)}, bf16[4,4,48,2304]{3,2,1,0:T(8,128)(2,1)}, bf16[512,2304]{1,0:T(8,128)(2,1)}, f32[6,8,...) custom-call(bf16[512,768]{1,0:T(8,128)(2,1)} %refs_0_.3, ...), custom_call_target="tpu_custom_call" | custom-call | tf_op jit(solution)/shard_map/forward/pallas_call | solution.py:971
  86.5 84.4 %backward.1 = (bf16[512,768]{1,0:T(8,128)(2,1)}, bf16[512,768]{1,0:T(8,128)(2,1)}, f32[24,2304]{1,0:T(8,128)}, f32[24,768]{1,0:T(8,128)}, f32[24,3072]{1,0:T(8,1...) custom-call(bf16[512,768]{1,0:T(8,128)(2,1)} %refs_0_.3, s32[1,8]{1,0:T(1,128)} %refs_1_.3, bf16[512,768]{1,0:T(8,128)(2,1)} %refs_2_.3, ...), custom_call_target="tpu_custom_call" | custom-call | tf_op jit(solution)/shard_map/backward/pallas_call | solution.py:1392
  170.9 76.8 %deliver.1 = (bf16[512,768]{1,0:T(8,128)(2,1)}, bf16[512,768]{1,0:T(8,128)(2,1)}, f32[24,2304]{1,0:T(8,128)}, f32[24,768]{1,0:T(8,128)}, f32[24,3072]{1,0:T(8,12...) custom-call(bf16[512,768]{1,0:T(8,128)(2,1)} %get-tuple-element.63.r, ...), custom_call_target="tpu_custom_call" | custom-call | tf_op jit(solution)/shard_map/deliver/pallas_call | solution.py:1426

commit v3 on v2

--- a/solution.py
+++ b/solution.py
@@ -14,7 +14,7 @@
 
 
 NORM_EPSILON = 1e-05
-VMEM_BYTES = 62 << 20
+VMEM_BYTES = 127 << 19
 AXES = ("wide", "narrow")
 
 
@@ -378,9 +378,12 @@
     def got(self, target, index, peer):
         remote(target, target, self.send.at[index], self.recv.at[index], peer).wait_recv()
 
+    def left(self, source, target, index, peer):
+        remote(source(), target(), self.send.at[index], self.recv.at[index], peer).wait_send()
+
     def finish(self):
-        for source, target, index, peer in self.sent:
-            remote(source(), target(), self.send.at[index], self.recv.at[index], peer).wait_send()
+        for one in self.sent:
+            self.left(*one)
 
 
 class Gather(Piece):
@@ -445,9 +448,10 @@
 
 
 class Scatter(Piece):
-    def __init__(self, place, bufs, send, recv):
+    def __init__(self, place, block, column, bufs, send, recv):
         super().__init__(place, send, recv)
-        self.total, self.dx, self.dy, self.xr, self.yr, self.zr = bufs
+        self.block, self.column = block, column
+        self.dx, self.dy, self.xr, self.yr, self.zr = bufs
         self.columns = (place.qd, place.qx, place.qy, place.q)
 
     def add(self, target, other):
@@ -458,29 +462,35 @@
     def give(self, other):
         for i, q in enumerate(self.columns):
             self.go(
-                lambda q=q: other(q), lambda q=q: self.total.at[:, q], 15 + i, self.p.to_c
+                lambda q=q: other(q), lambda q=q: self.column(q), 15 + i, self.p.to_c
             )
 
+    def given(self):
+        for source, target, index, peer in self.sent:
+            if index >= 15:
+                self.left(source, target, index, peer)
+        self.sent = [one for one in self.sent if one[2] < 15]
+
     def arrive(self, i):
-        self.got(self.total.at[:, self.columns[i]], 15 + i, self.p.to_c)
+        self.got(self.column(self.columns[i]), 15 + i, self.p.to_c)
 
     def take(self, i, mine):
         self.arrive(i)
         q = self.columns[i]
         for zz in range(4):
-            self.add(self.total.at[zz, q], mine(zz, q))
+            self.add(self.block(zz, q), mine(zz, q))
 
     def diagonal(self):
         p = self.p
         for i in range(2):
             self.go(
-                lambda i=i: self.total.at[p.zs[VIA_X[i]], p.qd],
+                lambda i=i: self.block(p.zs[VIA_X[i]], p.qd),
                 lambda i=i: self.dx.at[i],
                 7 + i,
                 p.to_x,
             )
             self.go(
-                lambda i=i: self.total.at[p.zs[VIA_Y[i]], p.qd],
+                lambda i=i: self.block(p.zs[VIA_Y[i]], p.qd),
                 lambda i=i: self.dy.at[i],
                 13 + i,
                 p.to_y,
@@ -488,8 +498,8 @@
 
     def cross(self, k):
         p = self.p
-        on_x = lambda: self.total.at[p.zs[k], p.qx]
-        on_y = lambda: self.total.at[p.zs[k], p.qy]
+        on_x = lambda: self.block(p.zs[k], p.qx)
+        on_y = lambda: self.block(p.zs[k], p.qy)
         if k in VIA_Y:
             i = VIA_Y.index(k)
             self.go(on_y, lambda: self.yr.at[k], 9 + k, p.to_y)
@@ -507,7 +517,7 @@
         p = self.p
         self.got(self.xr.at[k], 3 + k, p.to_x)
         self.got(self.yr.at[k], 9 + k, p.to_y)
-        here = self.total.at[p.zs[k], p.q]
+        here = self.block(p.zs[k], p.q)
         return here, (
             here[...].astype(jnp.float32)
             + self.xr[k].astype(jnp.float32)
@@ -518,7 +528,7 @@
         here, value = self.plane(k)
         here[...] = value.astype(here.dtype)
         self.go(
-            lambda: self.total.at[self.p.zs[k], self.p.q],
+            lambda: self.block(self.p.zs[k], self.p.q),
             lambda: self.zr.at[k - 1],
             k - 1,
             self.p.to_z[k],
@@ -535,7 +545,6 @@
 
 def scatter_buffers(tail, kind):
     return [
-        pltpu.VMEM((4, 4) + tail, kind),
         pltpu.VMEM((2,) + tail, kind),
         pltpu.VMEM((2,) + tail, kind),
         pltpu.VMEM((4,) + tail, kind),
@@ -544,18 +553,6 @@
     ]
 
 
-WANTED = (
-    "vec",
-    "turned_two",
-    "middle",
-    "up_wide",
-    "mixed_turned",
-    "out_wide",
-    "joined",
-    "logsum",
-    "turned_one",
-    "qkv_wide",
-)
 MATRICES = ("qkv", "out", "up", "down")
 
 
@@ -647,23 +644,28 @@
     return centred * factor, factor
 
 
-def forward_kernel(names, *refs):
+def run(steps):
+    for one in steps:
+        one()
+
+
+def layer_kernel(names, *refs):
     r = Named(names, refs)
     place = Place()
+    c = place.c
     tokens, width = r.tokens.shape
-    hidden = r.act.shape[0] * TILE
+    hidden = r.act.shape[1]
     pairs = width // 128
+    tiles = hidden // TILE
     shards = (r.qkv_shard, r.out_shard, r.up_shard, r.down_shard)
-    owns = (r.qkv_own, r.out_own, r.up_own, r.down_own)
     sibs = (r.qkv_sib, r.out_sib, r.up_sib, r.down_sib)
     wides = (r.qkv_wide, r.out_wide, r.up_wide, r.down_wide)
     meet(place)
-    first = place.c == 0
 
     def before(i):
         half = shards[i].shape[1] // 2
         return remote(
-            shards[i].at[:, span((1 - place.c) * half, half, 128)],
+            shards[i].at[:, span((1 - c) * half, half, 128)],
             sibs[i],
             r.pre_send.at[i],
             r.pre_recv.at[i],
@@ -672,26 +674,26 @@
 
     for i in range(4):
         before(i).start()
-    r.small[...] = jnp.zeros_like(r.small)
+    r.small_wide[place.z, place.q, c] = jnp.zeros((8, 128), jnp.float32)
     for i in range(8):
         vector = getattr(r, "vector%d" % i)
-        r.small[i : i + 1, 0 : vector.shape[0]] = vector[...].reshape(1, -1)
-    small = Gather(
+        r.small_wide[place.z, place.q, c, i : i + 1, 0 : vector.shape[0]] = vector[...].reshape(1, -1)
+    gather_small = Gather(
         place,
-        lambda: r.small,
-        lambda zz, q: r.small_wide.at[zz, q, place.c],
-        lambda q: r.small_wide.at[:, q, place.c],
-        lambda q: r.small_wide.at[:, q, 1 - place.c],
-        r.send.at[6],
-        r.recv.at[6],
-    )
-    local = [pltpu.make_async_copy(r.small, r.small_wide.at[place.z, place.q, place.c], r.local.at[4])]
-    local[0].start()
-    small.start_z()
-    small.start_xy()
+        lambda: r.small_wide.at[place.z, place.q, c],
+        lambda zz, q: r.small_wide.at[zz, q, c],
+        lambda q: r.small_wide.at[:, q, c],
+        lambda q: r.small_wide.at[:, q, 1 - c],
+        r.gather_send.at[8],
+        r.gather_recv.at[8],
+    )
+    gather_small.start_z()
+    gather_small.start_xy()
 
     cuts = (
-        (0, 0, 48, 0, 1152),
+        (0, 0, 48, 0, 384),
+        (0, 0, 48, 384, 384),
+        (0, 0, 48, 768, 384),
         (1, 0, 48, 0, 384),
         (2, 0, 48, 0, 768),
         (2, 0, 48, 768, 768),
@@ -702,84 +704,85 @@
     for j, (i, row, rows, col, cols) in enumerate(cuts):
         half = shards[i].shape[1] // 2
 
-        def at(c, row=row, rows=rows, col=col, cols=cols, half=half):
-            return (pl.ds(row, rows), span(c * half + col, cols, 128))
-
+        def at(side, row=row, rows=rows, col=col, cols=cols, half=half):
+            return (pl.ds(row, rows), span(side * half + col, cols, 128))
+
+        block = lambda zz, q, i=i, at=at: wides[i].at[(zz, q) + at(c)]
         pieces.append(
             Gather(
                 place,
-                lambda i=i, row=row, rows=rows, col=col, cols=cols: owns[i].at[
-                    pl.ds(row, rows), pl.ds(col, cols)
-                ],
-                lambda zz, q, i=i, at=at: wides[i].at[(zz, q) + at(place.c)],
-                lambda q, i=i, at=at: wides[i].at[(slice(None), q) + at(place.c)],
-                lambda q, i=i, at=at: wides[i].at[(slice(None), q) + at(1 - place.c)],
-                r.send.at[j],
-                r.recv.at[j],
+                lambda block=block: block(place.z, place.q),
+                block,
+                lambda q, i=i, at=at: wides[i].at[(slice(None), q) + at(c)],
+                lambda q, i=i, at=at: wides[i].at[(slice(None), q) + at(1 - c)],
+                r.gather_send.at[j],
+                r.gather_recv.at[j],
             )
         )
     for i in range(4):
         half = shards[i].shape[1] // 2
-        cols = span(place.c * half, half, 128)
+        cols = span(c * half, half, 128)
         before(i).wait_recv()
         mine = shards[i][:, cols]
         theirs = sibs[i][...]
-        owns[i][...] = jnp.concatenate(
-            [jnp.where(first, mine, theirs), jnp.where(first, theirs, mine)], axis=0
+        wides[i][place.z, place.q, :, cols] = jnp.concatenate(
+            [jnp.where(c == 0, mine, theirs), jnp.where(c == 0, theirs, mine)], axis=0
         ).astype(jnp.bfloat16)
-        copy = pltpu.make_async_copy(
-            owns[i], wides[i].at[place.z, place.q, :, cols], r.local.at[i]
-        )
-        copy.start()
-        local.append(copy)
         for j, cut in enumerate(cuts):
             if cut[0] == i:
                 pieces[j].start_z()
-        if i == 0:
-            pieces[0].start_xy()
+                if j == 0:
+                    pieces[0].start_xy()
     fill_present(r.present, r.mask)
-    for copy in local:
-        copy.wait()
-    p0, p1, p2, p3, p4, p5 = pieces
-
-    def z_steps(piece):
-        return [lambda k=k: piece.z(k) for k in ORDER] + [piece.own_column]
-
-    def xy_steps(piece):
-        return [lambda k=k: piece.xy(k) for k in (0, 1, 3, 2)]
-
-    def run(steps):
-        for one in steps:
-            one()
-
-    outgoing = []
-
-    def write(source, target, index):
-        copy = pltpu.make_async_copy(source, target, r.write.at[index])
-        copy.start()
-        outgoing.append(copy)
-
-    run(z_steps(small)[:3])
-    run(z_steps(p0))
-    small.own_column()
-    run(xy_steps(small))
-    small.xy_columns()
-    p1.start_xy()
-    p0.xy(0)
-    small.d()
-    small.c()
-
-    rows = r.small_wide[...].reshape(256, 128).astype(jnp.bfloat16)
-    picked = dot(rows, selection(width))
-    owner = owners(width)
-    total = jnp.zeros((8, 7 * width), jnp.float32)
-    for d in range(32):
-        total = total + jnp.where(owner == d, picked[d * 8 : d * 8 + 8], 0.0)
-    r.vec[...] = total
-    r.bias[:, 0:width] = total[2:3, width : 2 * width]
+    r.sums[...] = jnp.zeros_like(r.sums)
+
+    def z_steps(j):
+        piece = pieces[j]
+        return (
+            ([piece.start_xy] if j else [])
+            + [lambda k=k: piece.z(k) for k in ORDER]
+            + [piece.own_column]
+        )
+
+    def xy_steps(j):
+        piece = pieces[j]
+        return [lambda k=k: piece.xy(k) for k in (0, 1, 3, 2)] + [piece.xy_columns]
+
+    def period(j):
+        return (
+            (z_steps(j + 1) if j + 1 < len(pieces) else [])
+            + xy_steps(j)
+            + ([pieces[j - 1].d] if j else [])
+        )
+
+    run([lambda k=k: gather_small.z(k) for k in ORDER])
+    run(z_steps(0))
+    gather_small.own_column()
+    run([lambda k=k: gather_small.xy(k) for k in range(4)])
+    gather_small.xy_columns()
+    run(z_steps(1))
+    run(xy_steps(0)[:2])
+    gather_small.d()
+    gather_small.c()
+
+    r.chosen[...] = selection(width)
+    r.owner[...] = owners(width)
+    r.vec[...] = jnp.zeros_like(r.vec)
+
+    def unpack(zz):
+        rows = r.small_wide[zz].reshape(64, 128).astype(jnp.bfloat16)
+        picked = dot(rows, r.chosen[...])
+        owner = r.owner[...] - (zz * 8).astype(jnp.float32)
+        total = r.vec[...]
+        for d in range(8):
+            total = total + jnp.where(owner == d, picked[d * 8 : d * 8 + 8], 0.0)
+        r.vec[...] = total
+
+    loop(4, unpack)
+    run(xy_steps(0)[2:])
+    r.bias[:, 0:width] = r.vec[2:3, width : 2 * width]
     r.bias[:, width : 2 * width] = jnp.zeros((1, width), jnp.float32)
-    r.bias[:, 2 * width : 3 * width] = total[2:3, 2 * width : 3 * width]
-    write(r.vec, r.vec_out, 0)
+    r.bias[:, 2 * width : 3 * width] = r.vec[2:3, 2 * width : 3 * width]
 
     def first_norm(t):
         rows = span(t * 128, 128, 128)
@@ -788,15 +791,24 @@
         r.normed[rows, :] = value.astype(jnp.bfloat16)
         r.turned_one[:, rows] = value.T.astype(jnp.bfloat16)
 
-    loop(tokens // 128, first_norm)
-    write(r.turned_one, r.turned_one_out, 1)
-    run(xy_steps(p0)[1:])
-    p0.xy_columns()
-    run(z_steps(p1))
-    p0.d()
-    p2.start_xy()
-    p0.c()
-    write(r.qkv_wide, r.qkv_wide_out, 2)
+    def mask_grad(t):
+        rows = span(t * 128, 128, 128)
+        low = (r.present[rows, 0:1] * r.out_grad[rows, :].astype(jnp.float32)).astype(jnp.bfloat16)
+        r.grad_low[rows, :] = low
+        r.sums[7:8, 0:width] += jnp.sum(low.astype(jnp.float32), axis=0, keepdims=True)
+
+    steps = period(1)
+    loop(tokens // 128, first_norm, [steps[0:2], steps[2:3], steps[3:4], steps[4:5]])
+    run(steps[5:])
+    steps = period(2)
+    loop(tokens // 128, mask_grad, [steps[0:2], steps[2:3], steps[3:4], steps[4:5]])
+    run(steps[5:])
+    steps = period(3)
+    run(steps[:4])
+    pieces[2].d()
+    run(steps[4:-1])
+    for j in range(3):
+        pieces[j].c()
 
     def project(t):
         cols = span(t * width, width, 128)
@@ -804,9 +816,8 @@
             dot(r.normed[...], r.qkv_wide[:, :, :, cols].reshape(width, width)) + r.bias[:, cols]
         ).astype(jnp.bfloat16)
 
-    xy1 = xy_steps(p1)
-    loop(3, project, [xy1[:2], xy1[2:3], xy1[3:] + [p1.xy_columns]])
-    write(r.joined, r.joined_out, 3)
+    steps = period(4)
+    loop(3, project, [steps[0:2], steps[2:4], steps[4:5]])
 
     def attend(hp):
         cols = span(hp * 128, 128, 128)
@@ -828,18 +839,13 @@
         r.mixed_turned[cols, :] = both.astype(jnp.bfloat16)
         r.mixed[:, cols] = both.T.astype(jnp.bfloat16)
 
-    z2 = z_steps(p2)
-    xy2 = xy_steps(p2)
+    later = period(5)
     loop(
         pairs,
         attend,
-        [z2, [p1.d, p3.start_xy], xy2[:1], xy2[1:2], xy2[2:3], xy2[3:] + [p2.xy_columns]],
-    )
-    write(r.logsum, r.logsum_out, 4)
-    write(r.mixed_turned, r.mixed_turned_out, 5)
-    p1.c()
-    run(z_steps(p3))
-    write(r.out_wide, r.out_wide_out, 6)
+        [steps[5:6], steps[6:7], steps[7:8], steps[8:], later[0:3], later[3:5]],
+    )
+    pieces[3].c()
     r.middle[...] = dot(r.mixed[...], r.out_wide[...].reshape(width, width))
 
     def second_norm(t):
@@ -853,254 +859,141 @@
         value = normed * r.vec[4:5, 0:width] + r.vec[5:6, 0:width]
         r.normed[rows, :] = value.astype(jnp.bfloat16)
         r.turned_two[:, rows] = value.T.astype(jnp.bfloat16)
-        r.grad_low[rows, :] = (present * r.out_grad[rows, :].astype(jnp.float32)).astype(
-            jnp.bfloat16
-        )
-
-    loop(tokens // 128, second_norm)
-    write(r.middle, r.middle_out, 7)
-    write(r.turned_two, r.turned_two_out, 8)
-    p2.d()
-    p4.start_xy()
-    p2.c()
-
-    def expand(t):
+
+    loop(tokens // 128, second_norm, [later[5:6], later[6:7], later[7:8], later[8:9]])
+    run(later[9:])
+    pieces[4].c()
+
+    def slope_out(t, slot):
+        return pltpu.make_async_copy(r.slope.at[slot], r.slope_far.at[t], r.slope_send.at[slot])
+
+    def slope_in(t, slot):
+        return pltpu.make_async_copy(r.slope_far.at[t], r.slope.at[slot], r.slope_recv.at[slot])
+
+    def expand(t, u):
+        slot = u % 2
+
+        @pl.when(u >= 2)
+        def _():
+            slope_out(t, slot).wait()
+
         cols = span(t * TILE, TILE, 128)
         value = (
             dot(r.normed[...], r.up_wide[:, :, :, cols].reshape(width, TILE))
             + r.vec[6:7, span(3 * width + t * TILE, TILE, 128)]
         )
         cumulative = 0.5 * (1.0 + lax.erf(value * (1.0 / math.sqrt(2.0))))
-        r.act[t] = (value * cumulative).astype(jnp.bfloat16)
-        r.slope[t] = cumulative + value * jnp.exp(-0.5 * value * value) * (
+        r.act[:, cols] = (value * cumulative).astype(jnp.bfloat16)
+        r.slope[slot] = cumulative + value * jnp.exp(-0.5 * value * value) * (
             1.0 / math.sqrt(2.0 * math.pi)
         )
+        slope_out(t, slot).start()
 
     def down_grad(t):
-        grad = dot_tn(r.act[t], r.grad_low[...]).astype(jnp.bfloat16)
-        r.down_grad[t // 2, pl.ds((t % 2) * 2, 2)] = grad.reshape(2, TILE // 2, width)
-
-    xy3 = xy_steps(p3)
-    loop(4, lambda u: expand(u + 2 * (u // 2)), [[s] for s in xy3])
-    p3.xy_columns()
-    run(z_steps(p4))
-    loop(4, lambda u: down_grad(u + 2 * (u // 2)))
-    p3.d()
-    p5.start_xy()
-    p3.c()
-    write(r.up_wide, r.up_wide_out, 9)
-    xy4 = xy_steps(p4)
-    loop(4, lambda u: expand(u + 2 * (u // 2) + 2), [[s] for s in xy4])
-    p4.xy_columns()
-    write(r.act, r.act_out, 10)
-    write(r.slope, r.slope_out, 11)
-    run(z_steps(p5))
-    loop(4, lambda u: down_grad(u + 2 * (u // 2) + 2))
-    write(r.down_grad, r.down_grad_out, 12)
-    p4.d()
-    run(xy_steps(p5))
-    p5.xy_columns()
-    p4.c()
-    p5.d()
-    p5.c()
-    write(r.down_wide, r.down_wide_out, 13)
-    for i in range(4):
-        before(i).wait_send()
-    for piece in [small] + pieces:
-        piece.finish()
-    for copy in outgoing:
-        copy.wait()
-
-
-def forward_call(tokens, band_mask, out_grad, shards, smalls):
-    bf16, f32 = jnp.bfloat16, jnp.float32
-    count, width = tokens.shape
-    shapes = [s.shape for s in shards]
-    hidden = shapes[2][1]
-    tiles = hidden // TILE
-    vmem = pl.BlockSpec(memory_space=pltpu.VMEM)
-    inputs = triples(
-        tokens=(tokens, vmem),
-        mask=(band_mask, pl.BlockSpec(memory_space=pltpu.SMEM)),
-        out_grad=(out_grad, vmem),
-        qkv_shard=(shards[0], vmem),
-        out_shard=(shards[1], vmem),
-        up_shard=(shards[2], vmem),
-        down_shard=(shards[3], vmem),
-    ) + [("vector%d" % i, v, vmem) for i, v in enumerate(smalls)]
-    kept = triples(
-        vec=((8, 7 * width), f32),
-        turned_one=((width, count), bf16),
-        qkv_wide=((4, 4, 2 * shapes[0][0], shapes[0][1]), bf16),
-        joined=((count, 3 * width), bf16),
-        logsum=((width // 128, 8, count), f32),
-        mixed_turned=((width, count), bf16),
-        out_wide=((4, 4, 2 * shapes[1][0], shapes[1][1]), bf16),
-        middle=((count, width), f32),
-        turned_two=((width, count), bf16),
-        up_wide=((4, 4, 2 * shapes[2][0], shapes[2][1]), bf16),
-        act=((tiles, count, TILE), bf16),
-        slope=((tiles, count, TILE), f32),
-        down_grad=((4, 4, 2 * shapes[3][0], shapes[3][1]), bf16),
-        down_wide=((4, 4, 2 * shapes[3][0], shapes[3][1]), bf16),
-    )
-    scratch = [(name, pltpu.VMEM(shape, kind)) for name, shape, kind in kept]
-    for name, (rows, cols) in zip(MATRICES, shapes):
-        scratch.append((name + "_own", pltpu.VMEM((2 * rows, cols // 2), bf16)))
-        scratch.append((name + "_sib", pltpu.VMEM((rows, cols // 2), f32)))
-    scratch += pairs_of(
-        small=pltpu.VMEM((8, 128), f32),
-        small_wide=pltpu.VMEM((4, 4, 2, 8, 128), f32),
-        present=pltpu.VMEM((count, 128), f32),
-        bias=pltpu.VMEM((1, 3 * width), f32),
-        normed=pltpu.VMEM((count, width), bf16),
-        mixed=pltpu.VMEM((count, width), bf16),
-        grad_low=pltpu.VMEM((count, width), bf16),
-        send=pltpu.SemaphoreType.DMA((7, Piece.COUNT)),
-        recv=pltpu.SemaphoreType.DMA((7, Piece.COUNT)),
-        pre_send=pltpu.SemaphoreType.DMA((4,)),
-        pre_recv=pltpu.SemaphoreType.DMA((4,)),
-        local=pltpu.SemaphoreType.DMA((5,)),
-        write=pltpu.SemaphoreType.DMA((len(kept),)),
-    )
-    names = (
-        [name for name, _, _ in inputs]
-        + [name + "_out" for name, _, _ in kept]
-        + [name for name, _ in scratch]
-    )
-    results = pl.pallas_call(
-        functools.partial(forward_kernel, names),
-        out_shape=tuple(jax.ShapeDtypeStruct(shape, kind) for _, shape, kind in kept),
-        in_specs=[spec for _, _, spec in inputs],
-        out_specs=(pl.BlockSpec(memory_space=pl.ANY),) * len(kept),
-        scratch_shapes=[kind for _, kind in scratch],
-        compiler_params=pltpu.CompilerParams(
-            collective_id=0, has_side_effects=True, vmem_limit_bytes=VMEM_BYTES
-        ),
-        name="forward",
-    )(*[array for _, array, _ in inputs])
-    return dict(zip([name for name, _, _ in kept], results))
-
-
-def backward_kernel(names, *refs):
-    r = Named(names, refs)
-    place = Place()
-    tokens, width = r.tokens.shape
-    hidden = r.dpre.shape[1]
-    pairs = width // 128
-    tiles = hidden // TILE
-    c = place.c
-
-    def fetch(name, index):
-        return pltpu.make_async_copy(getattr(r, name + "_in"), getattr(r, name), r.load.at[index])
-
-    wanted = WANTED
-
-    def need(*some):
-        for name in some:
-            fetch(name, wanted.index(name)).wait()
-
-    def stream(t, slot):
-        return (
-            pltpu.make_async_copy(r.act_in.at[t], r.act.at[slot], r.tile.at[0, slot]),
-            pltpu.make_async_copy(r.slope_in.at[t], r.slope.at[slot], r.tile.at[1, slot]),
-            pltpu.make_async_copy(
-                r.down_wide_in.at[t // 2, pl.ds((t % 2) * 2, 2)],
-                r.down_tile.at[slot],
-                r.tile.at[2, slot],
-            ),
-        )
-
-    def down_mine(s):
-        return pltpu.make_async_copy(
-            r.down_grad_in.at[:, :, pl.ds(96 * s, 96), span(c * 384, 384, 128)],
-            r.down_mine.at[s],
-            r.mine.at[s],
-        )
-
-    for s in range(2):
-        down_mine(s).start()
-    for copy in stream(0, 0):
-        copy.start()
-    for i, name in enumerate(wanted):
-        fetch(name, i).start()
-    meet(place)
-    pieces = []
-    for j in range(9):
-        bufs = [getattr(r, "piece%d_%d" % (j, b)) for b in range(6)]
-        pieces.append(Scatter(place, bufs, r.send.at[j], r.recv.at[j]))
-    d0, d1, u0, u1, o, q0, q1, q2, small = pieces
+        cols = span(t * TILE, TILE, 128)
+        grad = dot_tn(r.act[:, cols], r.grad_low[...]).astype(jnp.bfloat16)
+        r.down_part[t // 2, pl.ds((t % 2) * 2, 2)] = grad.reshape(2, TILE // 2, width)
+
+    steps = period(6)
+    loop(4, lambda u: expand(u + 2 * (u // 2), u), [steps[0:2], steps[2:4], steps[4:5], steps[5:6]])
+    loop(4, lambda u: down_grad(u + 2 * (u // 2)), [steps[6:7], steps[7:8], steps[8:9], steps[9:]])
+    pieces[5].c()
+    steps = period(7)
+    loop(4, lambda u: expand(u + 2 * (u // 2) + 2, u + 4), [[s] for s in steps[0:4]])
+    loop(4, lambda u: down_grad(u + 2 * (u // 2) + 2), [steps[4:5], steps[5:6]])
+    for u in (6, 7):
+        slope_out(0, u % 2).wait()
+    slope_in(0, 0).start()
+
+    def scatter(j, block, column):
+        bufs = [getattr(r, "piece%d_%d" % (j, b)) for b in range(5)]
+        return Scatter(place, block, column, bufs, r.scatter_send.at[j], r.scatter_recv.at[j])
+
+    d0, d1 = [
+        scatter(
+            s,
+            lambda zz, q, s=s: r.down_total.at[zz, q, pl.ds(96 * s, 96)],
+            lambda q, s=s: r.down_total.at[:, q, pl.ds(96 * s, 96)],
+        )
+        for s in range(2)
+    ]
+    u0, u1 = [
+        scatter(
+            2 + s,
+            lambda zz, q, s=s: r.up_total.at[s, zz, q],
+            lambda q, s=s: r.up_total.at[s, :, q],
+        )
+        for s in range(2)
+    ]
+    o = scatter(4, lambda zz, q: r.out_total.at[zz, q], lambda q: r.out_total.at[:, q])
+    qs = [
+        scatter(
+            5 + s,
+            lambda zz, q, s=s: r.qkv_total.at[s, zz, q],
+            lambda q, s=s: r.qkv_total.at[s, :, q],
+        )
+        for s in range(3)
+    ]
+    small = scatter(8, lambda zz, q: r.small_total.at[zz, q], lambda q: r.small_total.at[:, q])
+
+    def take_down(piece, s, i):
+        piece.take(
+            i, lambda zz, q: r.down_part.at[zz, q, pl.ds(96 * s, 96), span(c * 384, 384, 128)]
+        )
+
+    def cross_steps(piece):
+        return [lambda k=k: piece.cross(k) for k in (1, 3, 2, 0)]
+
+    def spread_steps(piece):
+        return [lambda k=k: piece.spread(k) for k in ORDER]
+
     for s, piece in enumerate((d0, d1)):
         piece.give(
-            lambda q, s=s: r.down_grad_in.at[
+            lambda q, s=s: r.down_part.at[
                 :, q, pl.ds(96 * s, 96), span((1 - c) * 384, 384, 128)
             ]
         )
-    fill_present(r.present, r.mask)
-    r.sums[...] = jnp.zeros_like(r.sums)
+    pieces[7].d()
+    take_down(d0, 0, 0)
+    d0.diagonal()
+    take_down(d1, 1, 0)
+    d1.diagonal()
+    pieces[6].c()
+    pieces[7].c()
     r.acc[...] = jnp.zeros_like(r.acc)
-
-    def mask_grad(t):
-        rows = span(t * 128, 128, 128)
-        low = (r.present[rows, 0:1] * r.out_grad[rows, :].astype(jnp.float32)).astype(jnp.bfloat16)
-        r.grad_low[rows, :] = low
-        r.sums[7:8, 0:width] += jnp.sum(low.astype(jnp.float32), axis=0, keepdims=True)
-
-    loop(tokens // 128, mask_grad)
-
-    def take_down(piece, s, i):
-        if i == 0:
-            down_mine(s).wait()
-        piece.take(i, lambda zz, q: r.down_mine.at[s, zz, q])
 
     def narrow(t):
         slot = t % 2
-        for copy in stream(t, slot):
-            copy.wait()
+        slope_in(t, slot).wait()
 
         @pl.when(t + 1 < tiles)
         def _():
-            for copy in stream(t + 1, 1 - slot):
-                copy.start()
+            slope_in(t + 1, 1 - slot).start()
 
         cols = span(t * TILE, TILE, 128)
-        weights = r.down_tile[slot].reshape(TILE, width)
-        r.acc[...] += dot(r.act[slot], weights)
+        weights = r.down_wide[t // 2, pl.ds((t % 2) * 2, 2)].reshape(TILE, width)
+        r.acc[...] += dot(r.act[:, cols], weights)
         grad = (dot_nt(r.grad_low[...], weights) * r.slope[slot]).astype(jnp.bfloat16)
-        r.dpre[:, cols] = grad
+        r.act[:, cols] = grad
         r.sums[6:7, span(3 * width + t * TILE, TILE, 128)] = jnp.sum(
             grad.astype(jnp.float32), axis=0, keepdims=True
         )
 
-    def cross_steps(piece):
-        return [lambda k=k: piece.cross(k) for k in (1, 3, 2, 0)]
-
-    def spread_steps(piece):
-        return [lambda k=k: piece.spread(k) for k in ORDER]
-
-    def run(steps):
-        for one in steps:
-            one()
-
     xd0, xd1, xu0, xu1, xo = [cross_steps(p) for p in (d0, d1, u0, u1, o)]
-    take_down(d0, 0, 0)
-    d0.diagonal()
     loop(
         tiles,
         narrow,
         [
             [lambda: take_down(d0, 0, 1), lambda: take_down(d0, 0, 2)],
-            [lambda: take_down(d1, 1, 0), d1.diagonal],
             xd0[:1],
-            xd0[1:2] + [lambda: take_down(d1, 1, 1)],
-            xd0[2:3] + [lambda: take_down(d1, 1, 2)],
-            xd0[3:] + [lambda: take_down(d0, 0, 3)],
+            xd0[1:2],
+            xd0[2:3] + [lambda: take_down(d1, 1, 1)],
+            xd0[3:] + [lambda: take_down(d1, 1, 2)],
+            xd1[:1] + [lambda: take_down(d0, 0, 3)],
+            xd1[1:2],
             [lambda: take_down(d1, 1, 3)],
-            xd1[:1],
         ],
     )
-
-    need("vec", "middle")
 
     def finish_output(t):
         rows = span(t * 128, 128, 128)
@@ -1109,66 +1002,61 @@
             + r.present[rows, 0:1] * (r.acc[rows, :] + r.vec[7:8, 0:width])
         ).astype(jnp.bfloat16)
 
-    need("turned_two", "up_wide")
-
     def up_part(side, s):
         cols = span(side * (hidden // 2) + 768 * s, 768, 128)
-        return dot(r.turned_two[...], r.dpre[:, cols]).reshape(4, 4, 48, 768)
-
-    for s, (piece, part) in enumerate(((u0, r.up_part0), (u1, r.up_part1))):
-        part[...] = up_part(1 - c, s).astype(jnp.bfloat16)
-        piece.give(lambda q, part=part: part.at[:, q])
-    run(xd1[1:2])
+        return dot(r.turned_two[...], r.act[:, cols]).reshape(4, 4, 48, 768)
+
+    for s, piece in enumerate((u0, u1)):
+        r.up_part[s] = up_part(1 - c, s).astype(jnp.bfloat16)
+        piece.give(lambda q, s=s: r.up_part.at[s, :, q])
+    run(xd1[2:3])
     for s, piece in enumerate((u0, u1)):
         for i in range(4):
             piece.arrive(i)
-        piece.total[...] = (
-            piece.total[...].astype(jnp.float32) + up_part(c, s)
-        ).astype(jnp.bfloat16)
+        r.up_total[s] = (r.up_total[s].astype(jnp.float32) + up_part(c, s)).astype(jnp.bfloat16)
         if s == 0:
             piece.diagonal()
-            run(xd1[2:])
+            run(xd1[3:])
     run(spread_steps(d0))
     u1.diagonal()
     loop(tokens // 128, finish_output)
-    r.acc[...] = dot_nt(r.dpre[...], r.up_wide[...].reshape(width, hidden))
+    r.acc[...] = dot_nt(r.act[...], r.up_wide[...].reshape(width, hidden))
+
+    def norm_back(up, normed, factor, index):
+        r.sums[index : index + 1, 0:width] += jnp.sum(up * normed, axis=0, keepdims=True)
+        r.sums[index + 1 : index + 2, 0:width] += jnp.sum(up, axis=0, keepdims=True)
+        scaled = up * r.vec[index : index + 1, 0:width]
+        return factor * (
+            scaled
+            - jnp.mean(scaled, axis=1, keepdims=True)
+            - normed * jnp.mean(scaled * normed, axis=1, keepdims=True)
+        )
 
     def second_back(t):
         rows = span(t * 128, 128, 128)
         normed, factor = unit(r.middle[rows, :])
-        up = r.acc[rows, :]
-        r.sums[4:5, 0:width] += jnp.sum(up * normed, axis=0, keepdims=True)
-        r.sums[5:6, 0:width] += jnp.sum(up, axis=0, keepdims=True)
-        scaled = up * r.vec[4:5, 0:width]
-        inner = (
-            scaled
-            - jnp.mean(scaled, axis=1, keepdims=True)
-            - normed * jnp.mean(scaled * normed, axis=1, keepdims=True)
-        )
-        grad = r.out_grad[rows, :].astype(jnp.float32) + factor * inner
+        grad = r.out_grad[rows, :].astype(jnp.float32) + norm_back(
+            r.acc[rows, :], normed, factor, 4
+        )
         r.middle[rows, :] = grad
         low = (r.present[rows, 0:1] * grad).astype(jnp.bfloat16)
-        r.attention_low[rows, :] = low
+        r.normed[rows, :] = low
         r.sums[3:4, 0:width] += jnp.sum(low.astype(jnp.float32), axis=0, keepdims=True)
 
     loop(tokens // 128, second_back, [xu0[:1], xu0[1:2], xu0[2:3], xu0[3:]])
-    need("mixed_turned", "out_wide")
 
     def out_part(side):
         cols = span(side * (width // 2), width // 2, 128)
-        return dot(r.mixed_turned[...], r.attention_low[:, cols]).reshape(4, 4, 48, width // 2)
+        return dot(r.mixed_turned[...], r.normed[:, cols]).reshape(4, 4, 48, width // 2)
 
     r.out_part[...] = out_part(1 - c).astype(jnp.bfloat16)
     o.give(lambda q: r.out_part.at[:, q])
-    r.mixed_grad[...] = dot_nt(r.attention_low[...], r.out_wide[...].reshape(width, width)).astype(
-        jnp.bfloat16
-    )
+    r.mixed[...] = dot_nt(r.normed[...], r.out_wide[...].reshape(width, width)).astype(jnp.bfloat16)
     for i in range(4):
         o.arrive(i)
-    o.total[...] = (o.total[...].astype(jnp.float32) + out_part(c)).astype(jnp.bfloat16)
+    r.out_total[...] = (r.out_total[...].astype(jnp.float32) + out_part(c)).astype(jnp.bfloat16)
     o.diagonal()
     run(spread_steps(d1))
-    need("joined", "logsum")
 
     def attend_back(hp):
         cols = span(hp * 128, 128, 128)
@@ -1177,7 +1065,7 @@
         query = r.joined[:, cols]
         key = r.joined[:, key_cols]
         value = r.joined[:, value_cols]
-        grad = r.mixed_grad[:, cols]
+        grad = r.mixed[:, cols]
         turned = key.T
         live = r.present[:, 0:1] > 0.5
         value_grad = jnp.zeros((tokens, 128), jnp.float32)
@@ -1196,9 +1084,9 @@
         scale = 1.0 / math.sqrt(HEAD)
         query_low = (jnp.concatenate(query_grad, axis=0).T * scale).astype(jnp.bfloat16)
         value_low = value_grad.astype(jnp.bfloat16)
-        r.joined_grad[:, cols] = query_low
-        r.joined_grad[:, key_cols] = (key_grad * scale).astype(jnp.bfloat16)
-        r.joined_grad[:, value_cols] = value_low
+        r.joined[:, cols] = query_low
+        r.joined[:, key_cols] = (key_grad * scale).astype(jnp.bfloat16)
+        r.joined[:, value_cols] = value_low
         r.sums[2:3, span(width + hp * 128, 128, 128)] = jnp.sum(
             query_low.astype(jnp.float32), axis=0, keepdims=True
         )
@@ -1212,77 +1100,66 @@
         [xu1[:1], xu1[1:2], xu1[2:3], xu1[3:] + spread_steps(u0)[:1], spread_steps(u0)[1:], xo],
     )
 
-    need("turned_one", "qkv_wide")
-
     def qkv_part(side, s):
         cols = span(side * (3 * width // 2) + 384 * s, 384, 128)
-        return dot(r.turned_one[...], r.joined_grad[:, cols]).reshape(4, 4, 48, 384)
-
-    qs = (q0, q1, q2)
-    for s, (piece, part) in enumerate(zip(qs, (r.qkv_part0, r.qkv_part1, r.qkv_part2))):
-        part[...] = qkv_part(1 - c, s).astype(jnp.bfloat16)
-        piece.give(lambda q, part=part: part.at[:, q])
+        return dot(r.turned_one[...], r.joined[:, cols]).reshape(4, 4, 48, 384)
+
+    u0.given()
+    u1.given()
+    for s, piece in enumerate(qs):
+        cols = pl.ds(384 * (s % 2), 384)
+        r.up_part[s // 2, :, :, :, cols] = qkv_part(1 - c, s).astype(jnp.bfloat16)
+        piece.give(lambda q, s=s, cols=cols: r.up_part.at[s // 2, :, q, :, cols])
     for s, piece in enumerate(qs):
         for i in range(4):
             piece.arrive(i)
-        piece.total[...] = (
-            piece.total[...].astype(jnp.float32) + qkv_part(c, s)
-        ).astype(jnp.bfloat16)
+        r.qkv_total[s] = (r.qkv_total[s].astype(jnp.float32) + qkv_part(c, s)).astype(jnp.bfloat16)
         piece.diagonal()
     run(spread_steps(u1))
-    r.acc[...] = dot_nt(r.joined_grad[...], r.qkv_wide[...].reshape(width, 3 * width))
+    r.acc[...] = dot_nt(r.joined[...], r.qkv_wide[...].reshape(width, 3 * width))
 
     def first_back(t):
         rows = span(t * 128, 128, 128)
         normed, factor = unit(r.tokens[rows, :].astype(jnp.float32))
-        up = r.acc[rows, :]
-        r.sums[0:1, 0:width] += jnp.sum(up * normed, axis=0, keepdims=True)
-        r.sums[1:2, 0:width] += jnp.sum(up, axis=0, keepdims=True)
-        scaled = up * r.vec[0:1, 0:width]
-        inner = (
-            scaled
-            - jnp.mean(scaled, axis=1, keepdims=True)
-            - normed * jnp.mean(scaled * normed, axis=1, keepdims=True)
-        )
-        r.input_grad[rows, :] = (r.middle[rows, :] + factor * inner).astype(jnp.bfloat16)
+        part = norm_back(r.acc[rows, :], normed, factor, 0)
+        r.input_grad[rows, :] = (r.middle[rows, :] + part).astype(jnp.bfloat16)
 
     loop(tokens // 128, first_back)
-    owner = owners(width)
-    sums = r.sums[...]
-    high = sums.astype(jnp.bfloat16)
-    rest = sums - high.astype(jnp.float32)
-    mid = rest.astype(jnp.bfloat16)
-    low = (rest - mid.astype(jnp.float32)).astype(jnp.bfloat16)
-    chosen = selection(width)
-    tile = jnp.zeros((256, 128), jnp.float32)
-    for part in (high, mid, low):
-        part = part.astype(jnp.float32)
-        spreaded = jnp.concatenate(
-            [jnp.where(owner == d, part, 0.0) for d in range(32)], axis=0
-        ).astype(jnp.bfloat16)
-        tile = tile + dot_nt(spreaded, chosen)
-    r.small_part[...] = tile.reshape(4, 4, 2, 8, 128)
+
+    def pack(zz):
+        sums = r.sums[...]
+        owner = r.owner[...] - (zz * 8).astype(jnp.float32)
+        tile = jnp.zeros((64, 128), jnp.float32)
+        for _ in range(3):
+            part = sums.astype(jnp.bfloat16).astype(jnp.float32)
+            sums = sums - part
+            rows = jnp.concatenate(
+                [jnp.where(owner == d, part, 0.0) for d in range(8)], axis=0
+            ).astype(jnp.bfloat16)
+            tile = tile + dot_nt(rows, r.chosen[...])
+        r.small_part[zz] = tile.reshape(4, 2, 8, 128)
+
+    loop(4, pack)
     small.give(lambda q: r.small_part.at[:, q, 1 - c])
-    run(cross_steps(q0))
+    run(cross_steps(qs[0]))
     for i in range(4):
         small.take(i, lambda zz, q: r.small_part.at[zz, q, c])
     small.diagonal()
     run(spread_steps(o))
-    run(cross_steps(q1))
+    run(cross_steps(qs[1]))
     run(cross_steps(small))
-    run(spread_steps(q0))
-    run(cross_steps(q2))
+    run(spread_steps(qs[0]))
+    run(cross_steps(qs[2]))
     run(spread_steps(small))
 
     finals = (r.down_final, r.up_final, r.out_final, r.qkv_final)
-    others = (r.down_other, r.up_other, r.out_other, r.qkv_other)
     results = (r.down_result, r.up_result, r.out_result, r.qkv_result)
 
-    def swap(i):
-        rows = results[i].shape[0]
+    def swap(i, side):
+        rows, cols = results[i].shape
         return remote(
             finals[i].at[span((1 - c) * rows, rows, 8)],
-            others[i],
+            results[i].at[:, span(side * (cols // 2), cols // 2, 128)],
             r.end_send.at[i],
             r.end_recv.at[i],
             place.to_c,
@@ -1290,13 +1167,8 @@
 
     def close(i):
         rows, cols = results[i].shape
-        swap(i).start()
+        swap(i, c).start()
         results[i][:, span(c * (cols // 2), cols // 2, 128)] = finals[i][span(c * rows, rows, 8)]
-
-    def settle(i):
-        cols = results[i].shape[1]
-        swap(i).wait_recv()
-        results[i][:, span((1 - c) * (cols // 2), cols // 2, 128)] = others[i][...]
 
     r.down_final[0:96, :] = d0.last()
     r.down_final[96:192, :] = d1.last()
@@ -1306,35 +1178,41 @@
     close(1)
     r.out_final[...] = o.last()
     close(2)
-    run(spread_steps(q1))
-    r.qkv_final[:, 0:384] = q0.last()
-    run(spread_steps(q2))
+    run(spread_steps(qs[1]))
+    r.qkv_final[:, 0:384] = qs[0].last()
+    run(spread_steps(qs[2]))
     r.small_result[...] = small.last()
-    r.qkv_final[:, 384:768] = q1.last()
-    settle(0)
-    settle(1)
-    settle(2)
-    r.qkv_final[:, 768:1152] = q2.last()
+    r.qkv_final[:, 384:768] = qs[1].last()
+    r.qkv_final[:, 768:1152] = qs[2].last()
     close(3)
-    settle(3)
     for i in range(4):
-        swap(i).wait_send()
-    for piece in pieces:
+        swap(i, 1 - c).wait_recv()
+    for i in range(4):
+        before(i).wait_send()
+        swap(i, c).wait_send()
+    for piece in [gather_small] + pieces + [d0, d1, u0, u1, o] + qs + [small]:
         piece.finish()
 
 
-def backward_call(tokens, band_mask, out_grad, kept, shapes):
+def layer_call(tokens, band_mask, out_grad, shards, smalls):
     bf16, f32 = jnp.bfloat16, jnp.float32
     count, width = tokens.shape
+    shapes = [s.shape for s in shards]
     hidden = shapes[2][1]
+    tiles = hidden // TILE
     vmem = pl.BlockSpec(memory_space=pltpu.VMEM)
     anywhere = pl.BlockSpec(memory_space=pl.ANY)
     inputs = triples(
         tokens=(tokens, vmem),
         mask=(band_mask, pl.BlockSpec(memory_space=pltpu.SMEM)),
         out_grad=(out_grad, vmem),
-    ) + [(name + "_in", array, anywhere) for name, array in kept.items()]
+        qkv_shard=(shards[0], vmem),
+        out_shard=(shards[1], vmem),
+        up_shard=(shards[2], vmem),
+        down_shard=(shards[3], vmem),
+    ) + [("vector%d" % i, v, vmem) for i, v in enumerate(smalls)]
     outs = triples(
+        slope_far=((tiles, count, TILE), f32),
         output=((count, width), bf16),
         input_grad=((count, width), bf16),
         qkv_result=(shapes[0], f32),
@@ -1353,69 +1231,85 @@
     for j, (tail, kind) in enumerate(tails):
         for b, one in enumerate(scatter_buffers(tail, kind)):
             scratch.append(("piece%d_%d" % (j, b), one))
-    for name in WANTED:
-        scratch.append((name, pltpu.VMEM(kept[name].shape, kept[name].dtype)))
     for name, (rows, cols) in zip(MATRICES, shapes):
+        scratch.append((name + "_wide", pltpu.VMEM((4, 4, 2 * rows, cols), bf16)))
+        scratch.append((name + "_sib", pltpu.VMEM((rows, cols // 2), f32)))
         scratch.append((name + "_final", pltpu.VMEM((2 * rows, cols // 2), f32)))
-        scratch.append((name + "_other", pltpu.VMEM((rows, cols // 2), f32)))
     scratch += pairs_of(
-        act=pltpu.VMEM((2, count, TILE), bf16),
+        small_wide=pltpu.VMEM((4, 4, 2, 8, 128), f32),
+        small_part=pltpu.VMEM((4, 4, 2, 8, 128), f32),
+        small_total=pltpu.VMEM((4, 4, 8, 128), f32),
+        down_part=pltpu.VMEM((4, 4, 192, width), bf16),
+        down_total=pltpu.VMEM((4, 4, 192, 384), bf16),
+        up_part=pltpu.VMEM((2, 4, 4, 48, 768), bf16),
+        up_total=pltpu.VMEM((2, 4, 4, 48, 768), bf16),
+        out_part=pltpu.VMEM((4, 4, 48, 384), bf16),
+        out_total=pltpu.VMEM((4, 4, 48, 384), bf16),
+        qkv_total=pltpu.VMEM((3, 4, 4, 48, 384), bf16),
+        present=pltpu.VMEM((count, 128), f32),
+        vec=pltpu.VMEM((8, 7 * width), f32),
+        sums=pltpu.VMEM((8, 7 * width), f32),
+        bias=pltpu.VMEM((1, 3 * width), f32),
+        chosen=pltpu.VMEM((128, 7 * width), bf16),
+        owner=pltpu.VMEM((1, 7 * width), f32),
+        logsum=pltpu.VMEM((width // 128, 8, count), f32),
+        turned_one=pltpu.VMEM((width, count), bf16),
+        turned_two=pltpu.VMEM((width, count), bf16),
+        mixed_turned=pltpu.VMEM((width, count), bf16),
+        normed=pltpu.VMEM((count, width), bf16),
+        mixed=pltpu.VMEM((count, width), bf16),
+        grad_low=pltpu.VMEM((count, width), bf16),
+        joined=pltpu.VMEM((count, 3 * width), bf16),
+        middle=pltpu.VMEM((count, width), f32),
+        acc=pltpu.VMEM((count, width), f32),
+        act=pltpu.VMEM((count, hidden), bf16),
         slope=pltpu.VMEM((2, count, TILE), f32),
-        down_tile=pltpu.VMEM((2, 2, TILE // 2, width), bf16),
-        down_mine=pltpu.VMEM((2, 4, 4, 96, 384), bf16),
-        up_part0=pltpu.VMEM((4, 4, 48, 768), bf16),
-        up_part1=pltpu.VMEM((4, 4, 48, 768), bf16),
-        out_part=pltpu.VMEM((4, 4, 48, 384), bf16),
-        qkv_part0=pltpu.VMEM((4, 4, 48, 384), bf16),
-        qkv_part1=pltpu.VMEM((4, 4, 48, 384), bf16),
-        qkv_part2=pltpu.VMEM((4, 4, 48, 384), bf16),
-        small_part=pltpu.VMEM((4, 4, 2, 8, 128), f32),
-        present=pltpu.VMEM((count, 128), f32),
-        sums=pltpu.VMEM((8, 7 * width), f32),
-        acc=pltpu.VMEM((count, width), f32),
-        grad_low=pltpu.VMEM((count, width), bf16),
-        dpre=pltpu.VMEM((count, hidden), bf16),
-        attention_low=pltpu.VMEM((count, width), bf16),
-        mixed_grad=pltpu.VMEM((count, width), bf16),
-        joined_grad=pltpu.VMEM((count, 3 * width), bf16),
-        send=pltpu.SemaphoreType.DMA((len(tails), Piece.COUNT)),
-        recv=pltpu.SemaphoreType.DMA((len(tails), Piece.COUNT)),
+        gather_send=pltpu.SemaphoreType.DMA((9, Piece.COUNT)),
+        gather_recv=pltpu.SemaphoreType.DMA((9, Piece.COUNT)),
+        scatter_send=pltpu.SemaphoreType.DMA((9, Piece.COUNT)),
+        scatter_recv=pltpu.SemaphoreType.DMA((9, Piece.COUNT)),
+        pre_send=pltpu.SemaphoreType.DMA((4,)),
+        pre_recv=pltpu.SemaphoreType.DMA((4,)),
         end_send=pltpu.SemaphoreType.DMA((4,)),
         end_recv=pltpu.SemaphoreType.DMA((4,)),
-        load=pltpu.SemaphoreType.DMA((10,)),
-        tile=pltpu.SemaphoreType.DMA((3, 2)),
-        mine=pltpu.SemaphoreType.DMA((2,)),
+        slope_send=pltpu.SemaphoreType.DMA((2,)),
+        slope_recv=pltpu.SemaphoreType.DMA((2,)),
     )
     names = (
         [name for name, _, _ in inputs] + [name for name, _, _ in outs] + [name for name, _ in scratch]
     )
     results = pl.pallas_call(
-        functools.partial(backward_kernel, names),
+        functools.partial(layer_kernel, names),
         out_shape=tuple(jax.ShapeDtypeStruct(shape, kind) for _, shape, kind in outs),
         in_specs=[spec for _, _, spec in inputs],
-        out_specs=(vmem,) * len(outs),
+        out_specs=(anywhere,) + (vmem,) * (len(outs) - 1),
         scratch_shapes=[kind for _, kind in scratch],
         compiler_params=pltpu.CompilerParams(
-            collective_id=1, has_side_effects=True, vmem_limit_bytes=VMEM_BYTES
+            collective_id=0, has_side_effects=True, vmem_limit_bytes=VMEM_BYTES
         ),
-        name="backward",
+        name="layer",
     )(*[array for _, array, _ in inputs])
-    return results
+    return results[1:]
 
 
 def deliver_kernel(count, *refs):
     sources, tile = refs[:count], refs[count]
     targets = refs[count + 1 : 2 * count + 1]
-    vectors = refs[2 * count + 1 : -1]
-    copies = [
-        pltpu.make_async_copy(source, target, refs[-1].at[i])
-        for i, (source, target) in enumerate(zip(sources, targets))
+    vectors = refs[2 * count + 1 : -count - 2]
+    stages = refs[-count - 2 : -2]
+    get, put = refs[-2:]
+    arriving = [
+        pltpu.make_async_copy(sources[i], stages[i], get.at[i]) for i in range(count)
     ]
-    for copy in copies:
+    leaving = [pltpu.make_async_copy(stages[i], targets[i], put.at[i]) for i in range(count)]
+    for copy in arriving:
         copy.start()
     for i, vector in enumerate(vectors):
         vector[...] = tile[i, 0 : vector.shape[0]]
-    for copy in copies:
+    for first, second in zip(arriving, leaving):
+        first.wait()
+        second.start()
+    for copy in leaving:
         copy.wait()
 
 
@@ -1429,7 +1323,9 @@
         + [jax.ShapeDtypeStruct((m,), jnp.float32) for m in sizes],
         in_specs=[anywhere] * count + [vmem],
         out_specs=[anywhere] * count + [vmem] * len(sizes),
-        scratch_shapes=[pltpu.SemaphoreType.DMA((count,))],
+        scratch_shapes=[pltpu.VMEM(a.shape, a.dtype) for a in whole]
+        + [pltpu.SemaphoreType.DMA((count,))] * 2,
+        compiler_params=pltpu.CompilerParams(vmem_limit_bytes=VMEM_BYTES),
         name="deliver",
     )(*whole, tile)
 
@@ -1453,8 +1349,7 @@
 ):
     smalls = (norm1_gain, norm1_shift, qv_bias, out_bias, norm2_gain, norm2_shift, up_bias, down_bias)
     shards = (qkv_weight, out_weight, up_weight, down_weight)
-    kept = forward_call(tokens, band_mask, out_grad, shards, smalls)
-    *whole, tile = backward_call(tokens, band_mask, out_grad, kept, [s.shape for s in shards])
+    *whole, tile = layer_call(tokens, band_mask, out_grad, shards, smalls)
     output, input_grad, qkv, out, up, down, *grads = deliver(
         whole, tile, [v.shape[0] for v in smalls]
     )

time: 248 us -> 162 us (0.65)
  Pallas kernels: 247 us -> 161 us
    pallas_call x1, Pallas kernels: 76.8 us -> 3.9 us  [deliver(): pl.pallas_call(functools.partial(deliver_kernel, count), out_shape=[jax.S...]
    pallas_call x2 -> x1, Pallas kernels: 170 us -> 157 us  [layer_call(): pl.pallas_call(functools.partial(layer_kernel, names), out_shape=tuple((j...]
where the time goes in v3:
time: 162 us
  Pallas kernels  161 us (99%)
    pallas_call x1, Pallas kernels, layer_call(): pl.pallas_call(functools.partial(layer_kernel, names), out_shape=tuple((j...  157 us
    pallas_call x1, Pallas kernels, deliver(): pl.pallas_call(functools.partial(deliver_kernel, count), out_shape=[jax.S...  3.9 us

profile of v3, /device:TPU:0, one launch (start us, length us, event | category | flops | bytes accessed | tf_op | source)
XLA Modules:
  0.0 161.8 jit_solution(9200436911593094540)
XLA Ops:
  0.7 157.1 %layer.1 = (f32[8,512,384]{2,1,0:T(8,128)}, bf16[512,768]{1,0:T(8,128)(2,1)}, bf16[512,768]{1,0:T(8,128)(2,1)}, f32[24,2304]{1,0:T(8,128)}, f32[24,768]{1,0:T(8,...) custom-call(bf16[512,768]{1,0:T(8,128)(2,1)} %refs_0_.1, s32[1,8]{1,0:T(1,128)} %refs_1_.1, ...), custom_call_target="tpu_custom_call" | custom-call | tf_op jit(solution)/shard_map/layer/pallas_call | solution.py:1281
  157.7 3.9 %deliver.1 = (bf16[512,768]{1,0:T(8,128)(2,1)}, bf16[512,768]{1,0:T(8,128)(2,1)}, f32[24,2304]{1,0:T(8,128)}, f32[24,768]{1,0:T(8,128)}, f32[24,3072]{1,0:T(8,12...) custom-call(bf16[512,768]{1,0:T(8,128)(2,1)} %get-tuple-element.35.r, ...), custom_call_target="tpu_custom_call" | custom-call | tf_op jit(solution)/shard_map/deliver/pallas_call | solution.py:1320

commit v4 on v3

--- a/solution.py
+++ b/solution.py
@@ -14,7 +14,7 @@
 
 
 NORM_EPSILON = 1e-05
-VMEM_BYTES = 127 << 19
+VMEM_BYTES = 62 << 20
 AXES = ("wide", "narrow")
 
 
@@ -365,44 +365,47 @@
 class Piece:
     COUNT = 19
 
-    def __init__(self, place, send, recv):
+    def __init__(self, place, send, recv, slots, z_send=None):
         self.p = place
-        self.send = send
-        self.recv = recv
+        self.send, self.recv, self.slots, self.z_send = send, recv, slots, z_send
         self.sent = []
 
+    def pair(self, index):
+        own = self.send if index >= 3 or self.z_send is None else self.z_send
+        return own.at[index], self.recv.at[self.slots[index]]
+
     def go(self, source, target, index, peer):
-        remote(source(), target(), self.send.at[index], self.recv.at[index], peer).start()
+        remote(source(), target(), *self.pair(index), peer).start()
         self.sent.append((source, target, index, peer))
 
     def got(self, target, index, peer):
-        remote(target, target, self.send.at[index], self.recv.at[index], peer).wait_recv()
-
-    def left(self, source, target, index, peer):
-        remote(source(), target(), self.send.at[index], self.recv.at[index], peer).wait_send()
+        remote(target, target, *self.pair(index), peer).wait_recv()
 
     def finish(self):
-        for one in self.sent:
-            self.left(*one)
+        for source, target, index, peer in self.sent:
+            remote(source(), target(), *self.pair(index), peer).wait_send()
+        self.sent = []
 
 
 class Gather(Piece):
-    def __init__(self, place, own, block, column, other, send, recv):
-        super().__init__(place, send, recv)
-        self.own = own
-        self.block = block
-        self.column = column
-        self.other = other
+    SLOTS = (0, 1, 2, 3, 4, 5, 6, 11, 11, 7, 8, 9, 10, 11, 11, 12, 12, 12, 12)
+
+    def __init__(self, place, block, column, others, send, recv, z_send):
+        super().__init__(place, send, recv, self.SLOTS, z_send)
+        self.block, self.column, self.others = block, column, others
+
+    def own(self):
+        return self.block(self.p.z, self.p.q)
 
     def start_z(self):
         p = self.p
         for k in ORDER:
-            self.go(self.own, lambda: self.block(p.z, p.q), k - 1, p.to_z[k])
+            self.go(self.own, self.own, k - 1, p.to_z[k])
 
     def start_xy(self):
         p = self.p
-        self.go(self.own, lambda: self.block(p.z, p.q), 3, p.to_x)
-        self.go(self.own, lambda: self.block(p.z, p.q), 9, p.to_y)
+        self.go(self.own, self.own, 3, p.to_x)
+        self.go(self.own, self.own, 9, p.to_y)
 
     def z(self, k):
         p = self.p
@@ -435,24 +438,20 @@
 
     def d(self):
         p = self.p
-        for i, k in enumerate(VIA_X):
-            self.got(self.block(p.zs[k], p.qd), 13 + i, p.to_y)
-        for i, k in enumerate(VIA_Y):
-            self.got(self.block(p.zs[k], p.qd), 7 + i, p.to_x)
+        self.got(self.column(p.qd), 13, p.to_y)
         self.share(18, p.qd)
 
     def c(self):
-        p = self.p
-        for i, q in enumerate((p.q, p.qx, p.qy, p.qd)):
-            self.got(self.other(q), 15 + i, p.to_c)
+        self.got(self.others(), 15, self.p.to_c)
 
 
 class Scatter(Piece):
-    def __init__(self, place, block, column, bufs, send, recv):
-        super().__init__(place, send, recv)
-        self.block, self.column = block, column
+    SLOTS = (13, 13, 13, 5, 6, 7, 8, 1, 2, 9, 10, 11, 12, 3, 4, 0, 0, 0, 0)
+
+    def __init__(self, place, block, column, whole, bufs, send, recv):
+        super().__init__(place, send, recv, self.SLOTS)
+        self.block, self.column, self.whole = block, column, whole
         self.dx, self.dy, self.xr, self.yr, self.zr = bufs
-        self.columns = (place.qd, place.qx, place.qy, place.q)
 
     def add(self, target, other):
         target[...] = (target[...].astype(jnp.float32) + other[...].astype(jnp.float32)).astype(
@@ -460,40 +459,21 @@
         )
 
     def give(self, other):
-        for i, q in enumerate(self.columns):
-            self.go(
-                lambda q=q: other(q), lambda q=q: self.column(q), 15 + i, self.p.to_c
-            )
-
-    def given(self):
-        for source, target, index, peer in self.sent:
-            if index >= 15:
-                self.left(source, target, index, peer)
-        self.sent = [one for one in self.sent if one[2] < 15]
-
-    def arrive(self, i):
-        self.got(self.column(self.columns[i]), 15 + i, self.p.to_c)
-
-    def take(self, i, mine):
-        self.arrive(i)
-        q = self.columns[i]
-        for zz in range(4):
-            self.add(self.block(zz, q), mine(zz, q))
+        p = self.p
+        for i, q in enumerate((p.qd, p.qx, p.qy, p.q)):
+            self.go(lambda q=q: other(q), lambda q=q: self.column(q), 15 + i, p.to_c)
+
+    def arrive(self):
+        self.got(self.whole(), 15, self.p.to_c)
 
     def diagonal(self):
         p = self.p
         for i in range(2):
             self.go(
-                lambda i=i: self.block(p.zs[VIA_X[i]], p.qd),
-                lambda i=i: self.dx.at[i],
-                7 + i,
-                p.to_x,
+                lambda i=i: self.block(p.zs[VIA_X[i]], p.qd), lambda i=i: self.dx.at[i], 7 + i, p.to_x
             )
             self.go(
-                lambda i=i: self.block(p.zs[VIA_Y[i]], p.qd),
-                lambda i=i: self.dy.at[i],
-                13 + i,
-                p.to_y,
+                lambda i=i: self.block(p.zs[VIA_Y[i]], p.qd), lambda i=i: self.dy.at[i], 13 + i, p.to_y
             )
 
     def cross(self, k):
@@ -525,20 +505,15 @@
         )
 
     def spread(self, k):
+        p = self.p
         here, value = self.plane(k)
         here[...] = value.astype(here.dtype)
-        self.go(
-            lambda: self.block(self.p.zs[k], self.p.q),
-            lambda: self.zr.at[k - 1],
-            k - 1,
-            self.p.to_z[k],
-        )
+        self.go(lambda: self.block(p.zs[k], p.q), lambda: self.zr.at[k - 1], k - 1, p.to_z[k])
 
     def last(self):
-        p = self.p
         _, value = self.plane(0)
+        self.got(self.zr, 0, self.p.to_z[1])
         for k in ORDER:
-            self.got(self.zr.at[k - 1], k - 1, p.to_z[k])
             value = value + self.zr[k - 1].astype(jnp.float32)
         return value
 
@@ -570,20 +545,46 @@
         self.__dict__.update(zip(names, refs))
 
 
-def loop(count, compute, slots=()):
+def loop(first, count, compute, slots=()):
     def step(i, carry):
         compute(i)
         for j, steps in enumerate(slots):
             if steps:
 
-                @pl.when(i == j)
+                @pl.when(i == first + j)
                 def _(steps=steps):
                     for one in steps:
                         one()
 
         return carry
 
-    lax.fori_loop(0, count, step, 0)
+    lax.fori_loop(first, first + count, step, 0)
+
+
+def follow(order, steps, loops):
+    at = 0
+    while at < len(order):
+        kind = order[at][0]
+        if kind not in loops:
+            steps[order[at]]()
+            at += 1
+            continue
+        first, slots, end = order[at][1], [[]], at + 1
+        held = []
+        while end < len(order) and (order[end][0] not in loops or order[end][0] == kind):
+            if order[end][0] == kind:
+                slots[-1] += held
+                held = []
+                slots.append([])
+                at = end
+            else:
+                held.append(steps[order[end]])
+            end += 1
+        if len(slots) == 1:
+            loops[kind](jnp.int32(first))
+        else:
+            loop(first, len(slots), loops[kind], slots)
+        at += 1
 
 
 def dot(left, right):
@@ -620,14 +621,11 @@
     return ((0, width, width // 32), (width, 2 * width, width // 16), (3 * width, 4 * width, width // 8))
 
 
-def selection(width):
-    parts = []
-    for _, size, m in segments(width):
-        lane = lax.broadcasted_iota(jnp.int32, (1, size), 1).astype(jnp.float32)
-        rest = lane - m * jnp.floor((lane + 0.5) * (1.0 / m))
-        row = lax.broadcasted_iota(jnp.int32, (128, size), 0).astype(jnp.float32)
-        parts.append(jnp.where(row == rest, 1.0, 0.0).astype(jnp.bfloat16))
-    return jnp.concatenate(parts, axis=1)
+def selection(size, m):
+    lane = lax.broadcasted_iota(jnp.int32, (1, size), 1).astype(jnp.float32)
+    rest = lane - m * jnp.floor((lane + 0.5) * (1.0 / m))
+    row = lax.broadcasted_iota(jnp.int32, (128, size), 0).astype(jnp.float32)
+    return jnp.where(row == rest, 1.0, 0.0).astype(jnp.bfloat16)
 
 
 def owners(width):
@@ -644,9 +642,345 @@
     return centred * factor, factor
 
 
-def run(steps):
-    for one in steps:
-        one()
+(
+    ATTENTION,
+    CLOSE,
+    CROSS,
+    C_GOT,
+    DIAGONAL,
+    DOWN_HIGH,
+    DOWN_LOW,
+    DRAIN,
+    D_GOT,
+    EXPAND_HIGH,
+    EXPAND_LOW,
+    FINISH,
+    FIRST_BACK,
+    FIRST_NORM,
+    FORM,
+    GIVE,
+    HEADS,
+    HEADS_BACK,
+    LAST,
+    MASK_GRAD,
+    NARROW,
+    OUT_BACK,
+    OWN_COLUMN,
+    OWN_PART,
+    PACK,
+    QKV_BACK,
+    SECOND_BACK,
+    SECOND_NORM,
+    SETTLE,
+    SPREAD,
+    START_XY,
+    START_Z,
+    UNPACK,
+    UP_BACK,
+    XY_COLUMNS,
+    XY_GOT,
+    Z_GOT,
+) = range(37)
+SEQUENCE = (
+    (START_Z, 8),
+    (START_XY, 8),
+    (FORM, 0),
+    (FORM, 1),
+    (FORM, 2),
+    (FORM, 3),
+    (START_Z, 0),
+    (START_Z, 1),
+    (START_Z, 2),
+    (START_Z, 3),
+    (START_Z, 4),
+    (START_Z, 5),
+    (START_Z, 6),
+    (START_Z, 7),
+    (XY_GOT, 8, 0),
+    (Z_GOT, 8, 1),
+    (Z_GOT, 8, 3),
+    (Z_GOT, 8, 2),
+    (OWN_COLUMN, 8),
+    (START_XY, 0),
+    (START_XY, 1),
+    (START_XY, 2),
+    (MASK_GRAD, 0),
+    (MASK_GRAD, 1),
+    (START_XY, 3),
+    (MASK_GRAD, 2),
+    (XY_GOT, 8, 1),
+    (XY_GOT, 8, 3),
+    (XY_GOT, 8, 2),
+    (XY_COLUMNS, 8),
+    (MASK_GRAD, 3),
+    (XY_GOT, 0, 0),
+    (Z_GOT, 0, 3),
+    (XY_GOT, 1, 0),
+    (Z_GOT, 0, 2),
+    (XY_GOT, 2, 0),
+    (Z_GOT, 0, 1),
+    (OWN_COLUMN, 0),
+    (XY_GOT, 3, 0),
+    (D_GOT, 8),
+    (C_GOT, 8),
+    (UNPACK,),
+    (XY_GOT, 0, 2),
+    (XY_GOT, 0, 3),
+    (Z_GOT, 1, 3),
+    (Z_GOT, 1, 2),
+    (Z_GOT, 1, 1),
+    (OWN_COLUMN, 1),
+    (FIRST_NORM, 0),
+    (FIRST_NORM, 1),
+    (XY_GOT, 0, 1),
+    (XY_COLUMNS, 0),
+    (FIRST_NORM, 2),
+    (FIRST_NORM, 3),
+    (Z_GOT, 2, 3),
+    (XY_GOT, 1, 3),
+    (Z_GOT, 2, 2),
+    (XY_GOT, 1, 2),
+    (Z_GOT, 2, 1),
+    (OWN_COLUMN, 2),
+    (XY_GOT, 1, 1),
+    (D_GOT, 0),
+    (XY_COLUMNS, 1),
+    (START_XY, 4),
+    (XY_GOT, 2, 3),
+    (C_GOT, 0),
+    (HEADS, 0),
+    (D_GOT, 1),
+    (XY_GOT, 2, 1),
+    (XY_GOT, 2, 2),
+    (XY_COLUMNS, 2),
+    (Z_GOT, 3, 1),
+    (Z_GOT, 3, 3),
+    (Z_GOT, 3, 2),
+    (OWN_COLUMN, 3),
+    (HEADS, 1),
+    (C_GOT, 1),
+    (XY_GOT, 4, 0),
+    (START_XY, 5),
+    (D_GOT, 2),
+    (HEADS, 2),
+    (C_GOT, 2),
+    (XY_GOT, 3, 1),
+    (XY_GOT, 3, 2),
+    (XY_GOT, 3, 3),
+    (XY_COLUMNS, 3),
+    (Z_GOT, 4, 3),
+    (HEADS, 3),
+    (Z_GOT, 4, 1),
+    (Z_GOT, 4, 2),
+    (OWN_COLUMN, 4),
+    (XY_GOT, 5, 0),
+    (HEADS, 4),
+    (D_GOT, 3),
+    (XY_GOT, 4, 3),
+    (HEADS, 5),
+    (C_GOT, 3),
+    (XY_GOT, 4, 1),
+    (Z_GOT, 5, 3),
+    (ATTENTION,),
+    (XY_GOT, 4, 2),
+    (XY_COLUMNS, 4),
+    (SECOND_NORM, 0),
+    (Z_GOT, 5, 2),
+    (SECOND_NORM, 1),
+    (SECOND_NORM, 2),
+    (SECOND_NORM, 3),
+    (Z_GOT, 5, 1),
+    (OWN_COLUMN, 5),
+    (XY_GOT, 5, 3),
+    (D_GOT, 4),
+    (START_XY, 6),
+    (XY_GOT, 5, 2),
+    (C_GOT, 4),
+    (EXPAND_LOW, 0),
+    (EXPAND_LOW, 1),
+    (XY_GOT, 5, 1),
+    (XY_COLUMNS, 5),
+    (Z_GOT, 6, 3),
+    (EXPAND_LOW, 2),
+    (Z_GOT, 6, 2),
+    (EXPAND_LOW, 3),
+    (XY_GOT, 6, 0),
+    (Z_GOT, 6, 1),
+    (OWN_COLUMN, 6),
+    (DOWN_LOW, 0),
+    (DOWN_LOW, 1),
+    (D_GOT, 5),
+    (DOWN_LOW, 2),
+    (DOWN_LOW, 3),
+    (XY_GOT, 6, 3),
+    (START_XY, 7),
+    (C_GOT, 5),
+    (EXPAND_HIGH, 0),
+    (XY_GOT, 6, 2),
+    (EXPAND_HIGH, 1),
+    (Z_GOT, 7, 3),
+    (EXPAND_HIGH, 2),
+    (XY_GOT, 6, 1),
+    (XY_COLUMNS, 6),
+    (EXPAND_HIGH, 3),
+    (Z_GOT, 7, 2),
+    (DRAIN,),
+    (DOWN_HIGH, 0),
+    (Z_GOT, 7, 1),
+    (XY_GOT, 7, 0),
+    (OWN_COLUMN, 7),
+    (DOWN_HIGH, 1),
+    (DOWN_HIGH, 2),
+    (XY_GOT, 7, 3),
+    (DOWN_HIGH, 3),
+    (GIVE, 0),
+    (GIVE, 1),
+    (D_GOT, 6),
+    (XY_GOT, 7, 2),
+    (XY_GOT, 7, 1),
+    (XY_COLUMNS, 7),
+    (OWN_PART, 0),
+    (DIAGONAL, 0),
+    (OWN_PART, 1),
+    (D_GOT, 7),
+    (DIAGONAL, 1),
+    (C_GOT, 6),
+    (CROSS, 0, 1),
+    (CROSS, 0, 0),
+    (CROSS, 0, 3),
+    (C_GOT, 7),
+    (NARROW, 0),
+    (CROSS, 0, 2),
+    (CROSS, 1, 1),
+    (NARROW, 1),
+    (CROSS, 1, 0),
+    (CROSS, 1, 3),
+    (NARROW, 2),
+    (CROSS, 1, 2),
+    (NARROW, 3),
+    (SPREAD, 0, 1),
+    (NARROW, 4),
+    (NARROW, 5),
+    (NARROW, 6),
+    (SPREAD, 0, 3),
+    (NARROW, 7),
+    (SPREAD, 0, 2),
+    (GIVE, 2),
+    (SPREAD, 1, 1),
+    (GIVE, 3),
+    (SPREAD, 1, 3),
+    (OWN_PART, 2),
+    (SPREAD, 1, 2),
+    (DIAGONAL, 2),
+    (FINISH, 0),
+    (FINISH, 1),
+    (FINISH, 2),
+    (FINISH, 3),
+    (UP_BACK,),
+    (CROSS, 2, 0),
+    (CROSS, 2, 1),
+    (LAST, 0),
+    (OWN_PART, 3),
+    (CROSS, 2, 2),
+    (CROSS, 2, 3),
+    (DIAGONAL, 3),
+    (SECOND_BACK, 0),
+    (SECOND_BACK, 1),
+    (SECOND_BACK, 2),
+    (SECOND_BACK, 3),
+    (GIVE, 4),
+    (OUT_BACK,),
+    (SPREAD, 2, 1),
+    (HEADS_BACK, 0),
+    (SPREAD, 2, 3),
+    (SPREAD, 2, 2),
+    (LAST, 1),
+    (CLOSE, 3),
+    (OWN_PART, 4),
+    (CROSS, 3, 0),
+    (CROSS, 3, 1),
+    (DIAGONAL, 4),
+    (HEADS_BACK, 1),
+    (CROSS, 3, 2),
+    (CROSS, 3, 3),
+    (SETTLE, 3),
+    (GIVE, 5),
+    (HEADS_BACK, 2),
+    (SPREAD, 3, 1),
+    (CROSS, 4, 0),
+    (CROSS, 4, 1),
+    (CROSS, 4, 2),
+    (CROSS, 4, 3),
+    (OWN_PART, 5),
+    (DIAGONAL, 5),
+    (SPREAD, 3, 2),
+    (LAST, 2),
+    (HEADS_BACK, 3),
+    (SPREAD, 3, 3),
+    (GIVE, 6),
+    (SPREAD, 4, 1),
+    (HEADS_BACK, 4),
+    (SPREAD, 4, 3),
+    (SPREAD, 4, 2),
+    (CROSS, 5, 0),
+    (CROSS, 5, 1),
+    (CROSS, 5, 2),
+    (CROSS, 5, 3),
+    (OWN_PART, 6),
+    (DIAGONAL, 6),
+    (HEADS_BACK, 5),
+    (SPREAD, 5, 1),
+    (LAST, 3),
+    (SPREAD, 5, 2),
+    (CLOSE, 2),
+    (GIVE, 7),
+    (SPREAD, 5, 3),
+    (CROSS, 6, 0),
+    (CROSS, 6, 1),
+    (SETTLE, 2),
+    (LAST, 4),
+    (CROSS, 6, 2),
+    (CROSS, 6, 3),
+    (CLOSE, 1),
+    (OWN_PART, 7),
+    (DIAGONAL, 7),
+    (SETTLE, 1),
+    (QKV_BACK,),
+    (SPREAD, 6, 1),
+    (SPREAD, 6, 3),
+    (SPREAD, 6, 2),
+    (CROSS, 7, 0),
+    (CROSS, 7, 1),
+    (LAST, 5),
+    (CROSS, 7, 2),
+    (CROSS, 7, 3),
+    (FIRST_BACK, 0),
+    (FIRST_BACK, 1),
+    (FIRST_BACK, 2),
+    (FIRST_BACK, 3),
+    (PACK, 0),
+    (SPREAD, 7, 1),
+    (PACK, 1),
+    (PACK, 2),
+    (SPREAD, 7, 2),
+    (PACK, 3),
+    (GIVE, 8),
+    (SPREAD, 7, 3),
+    (LAST, 6),
+    (OWN_PART, 8),
+    (DIAGONAL, 8),
+    (CROSS, 8, 0),
+    (CROSS, 8, 1),
+    (CROSS, 8, 2),
+    (CROSS, 8, 3),
+    (LAST, 7),
+    (SPREAD, 8, 1),
+    (SPREAD, 8, 2),
+    (SPREAD, 8, 3),
+    (CLOSE, 0),
+    (SETTLE, 0),
+    (LAST, 8),
+)
 
 
 def layer_kernel(names, *refs):
@@ -655,134 +989,113 @@
     c = place.c
     tokens, width = r.tokens.shape
     hidden = r.act.shape[1]
-    pairs = width // 128
+    third = width // 2
     tiles = hidden // TILE
     shards = (r.qkv_shard, r.out_shard, r.up_shard, r.down_shard)
+    meet(place)
+
+    moves = [(0, g * width, third, (g,)) for g in range(3)] + [
+        (i, 0, shards[i].shape[1] // 2, ()) for i in (1, 2, 3)
+    ]
     sibs = (r.qkv_sib, r.out_sib, r.up_sib, r.down_sib)
     wides = (r.qkv_wide, r.out_wide, r.up_wide, r.down_wide)
-    meet(place)
-
-    def before(i):
-        half = shards[i].shape[1] // 2
-        return remote(
-            shards[i].at[:, span((1 - c) * half, half, 128)],
-            sibs[i],
-            r.pre_send.at[i],
-            r.pre_recv.at[i],
-            place.to_c,
-        )
-
-    for i in range(4):
-        before(i).start()
+
+    def before(m):
+        i, start, cols, at = moves[m]
+        source = shards[i].at[:, span(start + (1 - c) * cols, cols, 128)]
+        target = sibs[i].at[at] if at else sibs[i]
+        return remote(source, target, r.pre_send.at[m], r.pre_recv.at[m], place.to_c)
+
+    for m in range(6):
+        before(m).start()
     r.small_wide[place.z, place.q, c] = jnp.zeros((8, 128), jnp.float32)
     for i in range(8):
         vector = getattr(r, "vector%d" % i)
         r.small_wide[place.z, place.q, c, i : i + 1, 0 : vector.shape[0]] = vector[...].reshape(1, -1)
-    gather_small = Gather(
-        place,
-        lambda: r.small_wide.at[place.z, place.q, c],
-        lambda zz, q: r.small_wide.at[zz, q, c],
-        lambda q: r.small_wide.at[:, q, c],
-        lambda q: r.small_wide.at[:, q, 1 - c],
-        r.gather_send.at[8],
-        r.gather_recv.at[8],
-    )
-    gather_small.start_z()
-    gather_small.start_xy()
-
+
+    def gather(j, block, column, others):
+        lane = 4 if j == 8 else j % 4
+        return Gather(
+            place, block, column, others, r.send.at[lane], r.gather_recv.at[j], r.gather_z.at[j]
+        )
+
+    every = slice(None)
+    pieces = []
+    for s in range(3):
+        cols = lambda side, s=s: span(side * third + 128 * s, 128, 128)
+        pieces.append(
+            gather(
+                s,
+                lambda zz, q, cols=cols: r.qkv_wide.at[:, zz, q, :, cols(c)],
+                lambda q, cols=cols: r.qkv_wide.at[:, :, q, :, cols(c)],
+                lambda cols=cols: r.qkv_wide.at[:, :, :, :, cols(1 - c)],
+            )
+        )
     cuts = (
-        (0, 0, 48, 0, 384),
-        (0, 0, 48, 384, 384),
-        (0, 0, 48, 768, 384),
         (1, 0, 48, 0, 384),
         (2, 0, 48, 0, 768),
         (2, 0, 48, 768, 768),
         (3, 0, 96, 0, 384),
         (3, 96, 96, 0, 384),
     )
-    pieces = []
     for j, (i, row, rows, col, cols) in enumerate(cuts):
         half = shards[i].shape[1] // 2
 
         def at(side, row=row, rows=rows, col=col, cols=cols, half=half):
             return (pl.ds(row, rows), span(side * half + col, cols, 128))
 
-        block = lambda zz, q, i=i, at=at: wides[i].at[(zz, q) + at(c)]
         pieces.append(
-            Gather(
-                place,
-                lambda block=block: block(place.z, place.q),
-                block,
-                lambda q, i=i, at=at: wides[i].at[(slice(None), q) + at(c)],
-                lambda q, i=i, at=at: wides[i].at[(slice(None), q) + at(1 - c)],
-                r.gather_send.at[j],
-                r.gather_recv.at[j],
+            gather(
+                3 + j,
+                lambda zz, q, i=i, at=at: wides[i].at[(zz, q) + at(c)],
+                lambda q, i=i, at=at: wides[i].at[(every, q) + at(c)],
+                lambda i=i, at=at: wides[i].at[(every, every) + at(1 - c)],
             )
         )
-    for i in range(4):
-        half = shards[i].shape[1] // 2
-        cols = span(c * half, half, 128)
-        before(i).wait_recv()
-        mine = shards[i][:, cols]
-        theirs = sibs[i][...]
-        wides[i][place.z, place.q, :, cols] = jnp.concatenate(
-            [jnp.where(c == 0, mine, theirs), jnp.where(c == 0, theirs, mine)], axis=0
-        ).astype(jnp.bfloat16)
-        for j, cut in enumerate(cuts):
-            if cut[0] == i:
-                pieces[j].start_z()
-                if j == 0:
-                    pieces[0].start_xy()
+    pieces.append(
+        gather(
+            8,
+            lambda zz, q: r.small_wide.at[zz, q, c],
+            lambda q: r.small_wide.at[:, q, c],
+            lambda: r.small_wide.at[:, :, 1 - c],
+        )
+    )
+
+    def form(i):
+        for m, (weight, start, cols, at) in enumerate(moves):
+            if weight == i:
+                before(m).wait_recv()
+                mine = shards[i][:, span(start + c * cols, cols, 128)]
+                theirs = sibs[i][at] if at else sibs[i][...]
+                wides[i][at + (place.z, place.q, every, span(c * cols, cols, 128))] = jnp.concatenate(
+                    [jnp.where(c == 0, mine, theirs), jnp.where(c == 0, theirs, mine)], axis=0
+                ).astype(jnp.bfloat16)
+
     fill_present(r.present, r.mask)
     r.sums[...] = jnp.zeros_like(r.sums)
-
-    def z_steps(j):
-        piece = pieces[j]
-        return (
-            ([piece.start_xy] if j else [])
-            + [lambda k=k: piece.z(k) for k in ORDER]
-            + [piece.own_column]
-        )
-
-    def xy_steps(j):
-        piece = pieces[j]
-        return [lambda k=k: piece.xy(k) for k in (0, 1, 3, 2)] + [piece.xy_columns]
-
-    def period(j):
-        return (
-            (z_steps(j + 1) if j + 1 < len(pieces) else [])
-            + xy_steps(j)
-            + ([pieces[j - 1].d] if j else [])
-        )
-
-    run([lambda k=k: gather_small.z(k) for k in ORDER])
-    run(z_steps(0))
-    gather_small.own_column()
-    run([lambda k=k: gather_small.xy(k) for k in range(4)])
-    gather_small.xy_columns()
-    run(z_steps(1))
-    run(xy_steps(0)[:2])
-    gather_small.d()
-    gather_small.c()
-
-    r.chosen[...] = selection(width)
     r.owner[...] = owners(width)
     r.vec[...] = jnp.zeros_like(r.vec)
 
-    def unpack(zz):
-        rows = r.small_wide[zz].reshape(64, 128).astype(jnp.bfloat16)
-        picked = dot(rows, r.chosen[...])
-        owner = r.owner[...] - (zz * 8).astype(jnp.float32)
-        total = r.vec[...]
-        for d in range(8):
-            total = total + jnp.where(owner == d, picked[d * 8 : d * 8 + 8], 0.0)
-        r.vec[...] = total
-
-    loop(4, unpack)
-    run(xy_steps(0)[2:])
-    r.bias[:, 0:width] = r.vec[2:3, width : 2 * width]
-    r.bias[:, width : 2 * width] = jnp.zeros((1, width), jnp.float32)
-    r.bias[:, 2 * width : 3 * width] = r.vec[2:3, 2 * width : 3 * width]
+    def unpack():
+        for zz in range(4):
+            rows = r.small_wide[zz].reshape(64, 128).astype(jnp.bfloat16)
+            for start, size, m in segments(width):
+                lanes = slice(start, start + size)
+                picked = dot(rows, selection(size, m))
+                total = r.vec[:, lanes]
+                for d in range(8):
+                    total = total + jnp.where(
+                        r.owner[:, lanes] == zz * 8 + d, picked[d * 8 : d * 8 + 8], 0.0
+                    )
+                r.vec[:, lanes] = total
+        for s in range(3):
+            r.bias[s] = jnp.zeros((8, 6 * 128), jnp.float32)
+            for e in range(2):
+                at = 128 * s + third * e
+                r.bias[s, 0:1, 128 * e : 128 * e + 128] = r.vec[2:3, width + at : width + at + 128]
+                r.bias[s, 0:1, 512 + 128 * e : 640 + 128 * e] = r.vec[
+                    2:3, 2 * width + at : 2 * width + at + 128
+                ]
 
     def first_norm(t):
         rows = span(t * 128, 128, 128)
@@ -797,33 +1110,26 @@
         r.grad_low[rows, :] = low
         r.sums[7:8, 0:width] += jnp.sum(low.astype(jnp.float32), axis=0, keepdims=True)
 
-    steps = period(1)
-    loop(tokens // 128, first_norm, [steps[0:2], steps[2:3], steps[3:4], steps[4:5]])
-    run(steps[5:])
-    steps = period(2)
-    loop(tokens // 128, mask_grad, [steps[0:2], steps[2:3], steps[3:4], steps[4:5]])
-    run(steps[5:])
-    steps = period(3)
-    run(steps[:4])
-    pieces[2].d()
-    run(steps[4:-1])
-    for j in range(3):
-        pieces[j].c()
-
-    def project(t):
-        cols = span(t * width, width, 128)
-        r.joined[:, cols] = (
-            dot(r.normed[...], r.qkv_wide[:, :, :, cols].reshape(width, width)) + r.bias[:, cols]
-        ).astype(jnp.bfloat16)
-
-    steps = period(4)
-    loop(3, project, [steps[0:2], steps[2:4], steps[4:5]])
-
-    def attend(hp):
+    def heads(i):
+        s, e = i // 2, i % 2
+
+        @pl.when(e == 0)
+        def _():
+            weights = [
+                r.qkv_wide[g, :, :, :, span(half * third + s * 128, 128, 128)].reshape(width, 128)
+                for g in range(3)
+                for half in range(2)
+            ]
+            value = dot(r.normed[...], jnp.concatenate(weights, axis=1)) + r.bias[s, 0:1, :]
+            value = value.astype(jnp.bfloat16)
+            for g in range(3):
+                for half in range(2):
+                    at = (2 * g + half) * 128
+                    r.joined[s + 3 * half, g] = value[:, at : at + 128]
+
+        hp = s + 3 * e
         cols = span(hp * 128, 128, 128)
-        query = r.joined[:, cols]
-        key = r.joined[:, span(width + hp * 128, 128, 128)]
-        value = r.joined[:, span(2 * width + hp * 128, 128, 128)].T
+        query, key, value = r.joined[hp, 0], r.joined[hp, 1], r.joined[hp, 2].T
         live = r.present[:, 0:1] > 0.5
         mixed = []
         for e in range(2):
@@ -839,14 +1145,8 @@
         r.mixed_turned[cols, :] = both.astype(jnp.bfloat16)
         r.mixed[:, cols] = both.T.astype(jnp.bfloat16)
 
-    later = period(5)
-    loop(
-        pairs,
-        attend,
-        [steps[5:6], steps[6:7], steps[7:8], steps[8:], later[0:3], later[3:5]],
-    )
-    pieces[3].c()
-    r.middle[...] = dot(r.mixed[...], r.out_wide[...].reshape(width, width))
+    def attention():
+        r.middle[...] = dot(r.mixed[...], r.out_wide[...].reshape(width, width))
 
     def second_norm(t):
         rows = span(t * 128, 128, 128)
@@ -860,10 +1160,6 @@
         r.normed[rows, :] = value.astype(jnp.bfloat16)
         r.turned_two[:, rows] = value.T.astype(jnp.bfloat16)
 
-    loop(tokens // 128, second_norm, [later[5:6], later[6:7], later[7:8], later[8:9]])
-    run(later[9:])
-    pieces[4].c()
-
     def slope_out(t, slot):
         return pltpu.make_async_copy(r.slope.at[slot], r.slope_far.at[t], r.slope_send.at[slot])
 
@@ -894,76 +1190,132 @@
         grad = dot_tn(r.act[:, cols], r.grad_low[...]).astype(jnp.bfloat16)
         r.down_part[t // 2, pl.ds((t % 2) * 2, 2)] = grad.reshape(2, TILE // 2, width)
 
-    steps = period(6)
-    loop(4, lambda u: expand(u + 2 * (u // 2), u), [steps[0:2], steps[2:4], steps[4:5], steps[5:6]])
-    loop(4, lambda u: down_grad(u + 2 * (u // 2)), [steps[6:7], steps[7:8], steps[8:9], steps[9:]])
-    pieces[5].c()
-    steps = period(7)
-    loop(4, lambda u: expand(u + 2 * (u // 2) + 2, u + 4), [[s] for s in steps[0:4]])
-    loop(4, lambda u: down_grad(u + 2 * (u // 2) + 2), [steps[4:5], steps[5:6]])
-    for u in (6, 7):
-        slope_out(0, u % 2).wait()
-    slope_in(0, 0).start()
-
-    def scatter(j, block, column):
+    low_tile = lambda u: u + 2 * (u // 2)
+    high_tile = lambda u: u + 2 * (u // 2) + 2
+
+    def scatter(j, block, column, whole):
         bufs = [getattr(r, "piece%d_%d" % (j, b)) for b in range(5)]
-        return Scatter(place, block, column, bufs, r.scatter_send.at[j], r.scatter_recv.at[j])
-
-    d0, d1 = [
+        lane = 4 if j == 8 else j % 4
+        return Scatter(
+            place, block, column, whole, bufs, r.send.at[lane], r.scatter_recv.at[j]
+        )
+
+    sums = []
+    for s in range(2):
+        rows = pl.ds(96 * s, 96)
+        sums.append(
+            scatter(
+                s,
+                lambda zz, q, rows=rows: r.down_total.at[zz, q, rows],
+                lambda q, rows=rows: r.down_total.at[:, q, rows],
+                lambda rows=rows: r.down_total.at[:, :, rows],
+            )
+        )
+    for s in range(2):
+        sums.append(
+            scatter(
+                2 + s,
+                lambda zz, q, s=s: r.up_total.at[s, zz, q],
+                lambda q, s=s: r.up_total.at[s, :, q],
+                lambda s=s: r.up_total.at[s],
+            )
+        )
+    sums.append(
         scatter(
-            s,
-            lambda zz, q, s=s: r.down_total.at[zz, q, pl.ds(96 * s, 96)],
-            lambda q, s=s: r.down_total.at[:, q, pl.ds(96 * s, 96)],
-        )
-        for s in range(2)
-    ]
-    u0, u1 = [
+            4,
+            lambda zz, q: r.out_total.at[zz, q],
+            lambda q: r.out_total.at[:, q],
+            lambda: r.out_total,
+        )
+    )
+    for s in range(3):
+        sums.append(
+            scatter(
+                5 + s,
+                lambda zz, q, s=s: r.qkv_total.at[s, zz, q],
+                lambda q, s=s: r.qkv_total.at[s, :, q],
+                lambda s=s: r.qkv_total.at[s],
+            )
+        )
+    sums.append(
         scatter(
-            2 + s,
-            lambda zz, q, s=s: r.up_total.at[s, zz, q],
-            lambda q, s=s: r.up_total.at[s, :, q],
-        )
-        for s in range(2)
-    ]
-    o = scatter(4, lambda zz, q: r.out_total.at[zz, q], lambda q: r.out_total.at[:, q])
-    qs = [
-        scatter(
-            5 + s,
-            lambda zz, q, s=s: r.qkv_total.at[s, zz, q],
-            lambda q, s=s: r.qkv_total.at[s, :, q],
-        )
-        for s in range(3)
-    ]
-    small = scatter(8, lambda zz, q: r.small_total.at[zz, q], lambda q: r.small_total.at[:, q])
-
-    def take_down(piece, s, i):
-        piece.take(
-            i, lambda zz, q: r.down_part.at[zz, q, pl.ds(96 * s, 96), span(c * 384, 384, 128)]
-        )
-
-    def cross_steps(piece):
-        return [lambda k=k: piece.cross(k) for k in (1, 3, 2, 0)]
-
-    def spread_steps(piece):
-        return [lambda k=k: piece.spread(k) for k in ORDER]
-
-    for s, piece in enumerate((d0, d1)):
-        piece.give(
-            lambda q, s=s: r.down_part.at[
-                :, q, pl.ds(96 * s, 96), span((1 - c) * 384, 384, 128)
-            ]
-        )
-    pieces[7].d()
-    take_down(d0, 0, 0)
-    d0.diagonal()
-    take_down(d1, 1, 0)
-    d1.diagonal()
-    pieces[6].c()
-    pieces[7].c()
-    r.acc[...] = jnp.zeros_like(r.acc)
+            8,
+            lambda zz, q: r.small_total.at[zz, q],
+            lambda q: r.small_total.at[:, q],
+            lambda: r.small_total,
+        )
+    )
+
+    def up_part(side, s):
+        cols = span(side * (hidden // 2) + 768 * s, 768, 128)
+        return dot(r.turned_two[...], r.act[:, cols]).reshape(4, 4, 48, 768)
+
+    def out_part(side):
+        cols = span(side * third, third, 128)
+        return dot(r.mixed_turned[...], r.normed[:, cols]).reshape(4, 4, 48, third)
+
+    def qkv_part(side, s):
+        hp = side * 3 + s
+        grads = jnp.concatenate([r.joined[hp, g] for g in range(3)], axis=1)
+        return dot(r.turned_one[...], grads)
+
+    def other_part(p):
+        if p in (2, 3):
+            r.down_wide[:, :, 48 * (p - 2) : 48 * (p - 1), :] = up_part(1 - c, p - 2).astype(
+                jnp.bfloat16
+            )
+        elif p == 4:
+            r.down_wide[:, :, 96:144, 0:384] = out_part(1 - c).astype(jnp.bfloat16)
+        else:
+            value = qkv_part(1 - c, p - 5).astype(jnp.bfloat16)
+            for g in range(3):
+                r.down_part[:, :, 48 * g : 48 * g + 48, 128 * (p - 5) : 128 * (p - 4)] = value[
+                    :, 128 * g : 128 * g + 128
+                ].reshape(4, 4, 48, 128)
+
+    def given(p):
+        if p < 2:
+            rows, cols = pl.ds(96 * p, 96), span((1 - c) * 384, 384, 128)
+            return lambda q: r.down_part.at[:, q, rows, cols]
+        if p < 4:
+            return lambda q: r.down_wide.at[:, q, pl.ds(48 * (p - 2), 48)]
+        if p == 4:
+            return lambda q: r.down_wide.at[:, q, pl.ds(96, 48), pl.ds(0, 384)]
+        if p < 8:
+            return lambda q: r.down_part.at[:, q, pl.ds(0, 144), pl.ds(128 * (p - 5), 128)]
+        return lambda q: r.small_part.at[:, q, 1 - c]
+
+    def wide_sum(total, value):
+        total[...] = (total[...].astype(jnp.float32) + value).astype(total.dtype)
+
+    def own_part(p):
+        sums[p].arrive()
+        if p < 2:
+            rows = pl.ds(96 * p, 96)
+            mine = r.down_part[:, :, rows, span(c * 384, 384, 128)].astype(jnp.float32)
+            wide_sum(r.down_total.at[:, :, rows], mine)
+        elif p < 4:
+            wide_sum(r.up_total.at[p - 2], up_part(c, p - 2))
+        elif p == 4:
+            wide_sum(r.out_total, out_part(c))
+        elif p < 8:
+            value = qkv_part(c, p - 5)
+            for g in range(3):
+                wide_sum(
+                    r.qkv_total.at[p - 5, :, :, pl.ds(48 * g, 48)],
+                    value[:, 128 * g : 128 * g + 128].reshape(4, 4, 48, 128),
+                )
+        else:
+            wide_sum(r.small_total, r.small_part[:, :, c])
 
     def narrow(t):
         slot = t % 2
+
+        @pl.when(t == 0)
+        def _():
+            slope_in(0, 0).start()
+            r.acc[...] = jnp.zeros_like(r.acc)
+
         slope_in(t, slot).wait()
 
         @pl.when(t + 1 < tiles)
@@ -979,21 +1331,9 @@
             grad.astype(jnp.float32), axis=0, keepdims=True
         )
 
-    xd0, xd1, xu0, xu1, xo = [cross_steps(p) for p in (d0, d1, u0, u1, o)]
-    loop(
-        tiles,
-        narrow,
-        [
-            [lambda: take_down(d0, 0, 1), lambda: take_down(d0, 0, 2)],
-            xd0[:1],
-            xd0[1:2],
-            xd0[2:3] + [lambda: take_down(d1, 1, 1)],
-            xd0[3:] + [lambda: take_down(d1, 1, 2)],
-            xd1[:1] + [lambda: take_down(d0, 0, 3)],
-            xd1[1:2],
-            [lambda: take_down(d1, 1, 3)],
-        ],
-    )
+    def drain_slope():
+        for slot in range(2):
+            slope_out(0, slot).wait()
 
     def finish_output(t):
         rows = span(t * 128, 128, 128)
@@ -1002,25 +1342,8 @@
             + r.present[rows, 0:1] * (r.acc[rows, :] + r.vec[7:8, 0:width])
         ).astype(jnp.bfloat16)
 
-    def up_part(side, s):
-        cols = span(side * (hidden // 2) + 768 * s, 768, 128)
-        return dot(r.turned_two[...], r.act[:, cols]).reshape(4, 4, 48, 768)
-
-    for s, piece in enumerate((u0, u1)):
-        r.up_part[s] = up_part(1 - c, s).astype(jnp.bfloat16)
-        piece.give(lambda q, s=s: r.up_part.at[s, :, q])
-    run(xd1[2:3])
-    for s, piece in enumerate((u0, u1)):
-        for i in range(4):
-            piece.arrive(i)
-        r.up_total[s] = (r.up_total[s].astype(jnp.float32) + up_part(c, s)).astype(jnp.bfloat16)
-        if s == 0:
-            piece.diagonal()
-            run(xd1[3:])
-    run(spread_steps(d0))
-    u1.diagonal()
-    loop(tokens // 128, finish_output)
-    r.acc[...] = dot_nt(r.act[...], r.up_wide[...].reshape(width, hidden))
+    def up_back():
+        r.acc[...] = dot_nt(r.act[...], r.up_wide[...].reshape(width, hidden))
 
     def norm_back(up, normed, factor, index):
         r.sums[index : index + 1, 0:width] += jnp.sum(up * normed, axis=0, keepdims=True)
@@ -1043,28 +1366,15 @@
         r.normed[rows, :] = low
         r.sums[3:4, 0:width] += jnp.sum(low.astype(jnp.float32), axis=0, keepdims=True)
 
-    loop(tokens // 128, second_back, [xu0[:1], xu0[1:2], xu0[2:3], xu0[3:]])
-
-    def out_part(side):
-        cols = span(side * (width // 2), width // 2, 128)
-        return dot(r.mixed_turned[...], r.normed[:, cols]).reshape(4, 4, 48, width // 2)
-
-    r.out_part[...] = out_part(1 - c).astype(jnp.bfloat16)
-    o.give(lambda q: r.out_part.at[:, q])
-    r.mixed[...] = dot_nt(r.normed[...], r.out_wide[...].reshape(width, width)).astype(jnp.bfloat16)
-    for i in range(4):
-        o.arrive(i)
-    r.out_total[...] = (r.out_total[...].astype(jnp.float32) + out_part(c)).astype(jnp.bfloat16)
-    o.diagonal()
-    run(spread_steps(d1))
-
-    def attend_back(hp):
+    def out_back():
+        r.mixed[...] = dot_nt(r.normed[...], r.out_wide[...].reshape(width, width)).astype(
+            jnp.bfloat16
+        )
+
+    def heads_back(i):
+        hp = i // 2 + 3 * (i % 2)
         cols = span(hp * 128, 128, 128)
-        key_cols = span(width + hp * 128, 128, 128)
-        value_cols = span(2 * width + hp * 128, 128, 128)
-        query = r.joined[:, cols]
-        key = r.joined[:, key_cols]
-        value = r.joined[:, value_cols]
+        query, key, value = r.joined[hp, 0], r.joined[hp, 1], r.joined[hp, 2]
         grad = r.mixed[:, cols]
         turned = key.T
         live = r.present[:, 0:1] > 0.5
@@ -1084,9 +1394,9 @@
         scale = 1.0 / math.sqrt(HEAD)
         query_low = (jnp.concatenate(query_grad, axis=0).T * scale).astype(jnp.bfloat16)
         value_low = value_grad.astype(jnp.bfloat16)
-        r.joined[:, cols] = query_low
-        r.joined[:, key_cols] = (key_grad * scale).astype(jnp.bfloat16)
-        r.joined[:, value_cols] = value_low
+        r.joined[hp, 0] = query_low
+        r.joined[hp, 1] = (key_grad * scale).astype(jnp.bfloat16)
+        r.joined[hp, 2] = value_low
         r.sums[2:3, span(width + hp * 128, 128, 128)] = jnp.sum(
             query_low.astype(jnp.float32), axis=0, keepdims=True
         )
@@ -1094,29 +1404,12 @@
             value_low.astype(jnp.float32), axis=0, keepdims=True
         )
 
-    loop(
-        pairs,
-        attend_back,
-        [xu1[:1], xu1[1:2], xu1[2:3], xu1[3:] + spread_steps(u0)[:1], spread_steps(u0)[1:], xo],
-    )
-
-    def qkv_part(side, s):
-        cols = span(side * (3 * width // 2) + 384 * s, 384, 128)
-        return dot(r.turned_one[...], r.joined[:, cols]).reshape(4, 4, 48, 384)
-
-    u0.given()
-    u1.given()
-    for s, piece in enumerate(qs):
-        cols = pl.ds(384 * (s % 2), 384)
-        r.up_part[s // 2, :, :, :, cols] = qkv_part(1 - c, s).astype(jnp.bfloat16)
-        piece.give(lambda q, s=s, cols=cols: r.up_part.at[s // 2, :, q, :, cols])
-    for s, piece in enumerate(qs):
-        for i in range(4):
-            piece.arrive(i)
-        r.qkv_total[s] = (r.qkv_total[s].astype(jnp.float32) + qkv_part(c, s)).astype(jnp.bfloat16)
-        piece.diagonal()
-    run(spread_steps(u1))
-    r.acc[...] = dot_nt(r.joined[...], r.qkv_wide[...].reshape(width, 3 * width))
+    def qkv_back():
+        total = jnp.zeros((tokens, width), jnp.float32)
+        for g in range(3):
+            grads = jnp.concatenate([r.joined[hp, g] for hp in range(6)], axis=1)
+            total = total + dot_nt(grads, r.qkv_wide[g].reshape(width, width))
+        r.acc[...] = total
 
     def first_back(t):
         rows = span(t * 128, 128, 128)
@@ -1124,73 +1417,125 @@
         part = norm_back(r.acc[rows, :], normed, factor, 0)
         r.input_grad[rows, :] = (r.middle[rows, :] + part).astype(jnp.bfloat16)
 
-    loop(tokens // 128, first_back)
-
     def pack(zz):
-        sums = r.sums[...]
-        owner = r.owner[...] - (zz * 8).astype(jnp.float32)
-        tile = jnp.zeros((64, 128), jnp.float32)
-        for _ in range(3):
-            part = sums.astype(jnp.bfloat16).astype(jnp.float32)
-            sums = sums - part
-            rows = jnp.concatenate(
-                [jnp.where(owner == d, part, 0.0) for d in range(8)], axis=0
-            ).astype(jnp.bfloat16)
-            tile = tile + dot_nt(rows, r.chosen[...])
-        r.small_part[zz] = tile.reshape(4, 2, 8, 128)
-
-    loop(4, pack)
-    small.give(lambda q: r.small_part.at[:, q, 1 - c])
-    run(cross_steps(qs[0]))
+        first = (zz * 8).astype(jnp.float32)
+        for index, (start, size, m) in zip((None, 2, 6), segments(width)):
+            lanes = slice(start, start + size)
+            left = r.sums[:, lanes] if index is None else r.sums[index : index + 1, lanes]
+            owner = r.owner[:, lanes] - first
+            chosen = selection(size, m)
+            tile = 0.0
+            for _ in range(2):
+                part = left.astype(jnp.bfloat16).astype(jnp.float32)
+                left = left - part
+                rows = jnp.concatenate(
+                    [jnp.where(owner == d, part, 0.0) for d in range(8)], axis=0
+                ).astype(jnp.bfloat16)
+                tile = tile + dot_nt(rows, chosen)
+            if index is None:
+                r.small_part[zz] = tile.reshape(4, 2, 8, 128)
+            else:
+                for d in range(8):
+                    r.small_part[zz, d // 2, d % 2, index : index + 1, :] = tile[d : d + 1, :]
+
+    results = (r.qkv_result, r.out_result, r.up_result, r.down_result)
+    finals = (r.qkv_final, r.out_final, r.up_final, r.down_final)
+
+    def swap(m, side):
+        i, start, cols, at = moves[m]
+        rows = results[i].shape[0]
+        return remote(
+            finals[i].at[at + (span((1 - c) * rows, rows, 8),)],
+            results[i].at[:, span(start + side * cols, cols, 128)],
+            r.end_send.at[m],
+            r.end_recv.at[m],
+            place.to_c,
+        )
+
+    def close(i):
+        for m, (weight, start, cols, at) in enumerate(moves):
+            if weight == i:
+                rows = results[i].shape[0]
+                swap(m, c).start()
+                results[i][:, span(start + c * cols, cols, 128)] = finals[i][
+                    at + (span(c * rows, rows, 8),)
+                ]
+
+    def settle(i):
+        for m, move in enumerate(moves):
+            if move[0] == i:
+                swap(m, 1 - c).wait_recv()
+
+    def last(p):
+        value = sums[p].last()
+        if p < 2:
+            r.down_final[96 * p : 96 * p + 96, :] = value
+        elif p < 4:
+            r.up_final[:, 768 * (p - 2) : 768 * (p - 1)] = value
+        elif p == 4:
+            r.out_final[...] = value
+        elif p < 8:
+            for g in range(3):
+                r.qkv_final[g, :, 128 * (p - 5) : 128 * (p - 4)] = value[48 * g : 48 * g + 48]
+        else:
+            r.small_result[...] = value
+
+    def start_xy(j):
+        if 4 <= j < 8:
+            pieces[j - 4].finish()
+        pieces[j].start_xy()
+
+    def give(p):
+        before_it = pieces[8] if p == 8 else (sums[p - 4] if p >= 4 else pieces[p + 4])
+        before_it.finish()
+        if 2 <= p < 8:
+            other_part(p)
+        sums[p].give(given(p))
+
+    steps = {(UNPACK,): unpack, (ATTENTION,): attention, (DRAIN,): drain_slope}
+    steps.update({(UP_BACK,): up_back, (OUT_BACK,): out_back, (QKV_BACK,): qkv_back})
     for i in range(4):
-        small.take(i, lambda zz, q: r.small_part.at[zz, q, c])
-    small.diagonal()
-    run(spread_steps(o))
-    run(cross_steps(qs[1]))
-    run(cross_steps(small))
-    run(spread_steps(qs[0]))
-    run(cross_steps(qs[2]))
-    run(spread_steps(small))
-
-    finals = (r.down_final, r.up_final, r.out_final, r.qkv_final)
-    results = (r.down_result, r.up_result, r.out_result, r.qkv_result)
-
-    def swap(i, side):
-        rows, cols = results[i].shape
-        return remote(
-            finals[i].at[span((1 - c) * rows, rows, 8)],
-            results[i].at[:, span(side * (cols // 2), cols // 2, 128)],
-            r.end_send.at[i],
-            r.end_recv.at[i],
-            place.to_c,
-        )
-
-    def close(i):
-        rows, cols = results[i].shape
-        swap(i, c).start()
-        results[i][:, span(c * (cols // 2), cols // 2, 128)] = finals[i][span(c * rows, rows, 8)]
-
-    r.down_final[0:96, :] = d0.last()
-    r.down_final[96:192, :] = d1.last()
-    close(0)
-    r.up_final[:, 0:768] = u0.last()
-    r.up_final[:, 768:1536] = u1.last()
-    close(1)
-    r.out_final[...] = o.last()
-    close(2)
-    run(spread_steps(qs[1]))
-    r.qkv_final[:, 0:384] = qs[0].last()
-    run(spread_steps(qs[2]))
-    r.small_result[...] = small.last()
-    r.qkv_final[:, 384:768] = qs[1].last()
-    r.qkv_final[:, 768:1152] = qs[2].last()
-    close(3)
-    for i in range(4):
-        swap(i, 1 - c).wait_recv()
-    for i in range(4):
-        before(i).wait_send()
-        swap(i, c).wait_send()
-    for piece in [gather_small] + pieces + [d0, d1, u0, u1, o] + qs + [small]:
+        steps[FORM, i] = functools.partial(form, i)
+        steps[CLOSE, i] = functools.partial(close, i)
+        steps[SETTLE, i] = functools.partial(settle, i)
+    for j in range(9):
+        piece, total = pieces[j], sums[j]
+        steps[START_Z, j] = piece.start_z
+        steps[START_XY, j] = functools.partial(start_xy, j)
+        steps[OWN_COLUMN, j] = piece.own_column
+        steps[XY_COLUMNS, j] = piece.xy_columns
+        steps[D_GOT, j] = piece.d
+        steps[C_GOT, j] = piece.c
+        steps[GIVE, j] = functools.partial(give, j)
+        steps[OWN_PART, j] = functools.partial(own_part, j)
+        steps[DIAGONAL, j] = total.diagonal
+        steps[LAST, j] = functools.partial(last, j)
+        for k in range(4):
+            steps[Z_GOT, j, k] = functools.partial(piece.z, k)
+            steps[XY_GOT, j, k] = functools.partial(piece.xy, k)
+            steps[CROSS, j, k] = functools.partial(total.cross, k)
+            steps[SPREAD, j, k] = functools.partial(total.spread, k)
+    loops = {
+        FIRST_NORM: first_norm,
+        MASK_GRAD: mask_grad,
+        HEADS: heads,
+        SECOND_NORM: second_norm,
+        EXPAND_LOW: lambda u: expand(low_tile(u), u),
+        EXPAND_HIGH: lambda u: expand(high_tile(u), u + 4),
+        DOWN_LOW: lambda u: down_grad(low_tile(u)),
+        DOWN_HIGH: lambda u: down_grad(high_tile(u)),
+        NARROW: narrow,
+        FINISH: finish_output,
+        SECOND_BACK: second_back,
+        HEADS_BACK: heads_back,
+        FIRST_BACK: first_back,
+        PACK: pack,
+    }
+    follow(SEQUENCE, steps, loops)
+    for m in range(6):
+        before(m).wait_send()
+        swap(m, c).wait_send()
+    for piece in pieces + sums:
         piece.finish()
 
 
@@ -1224,33 +1569,39 @@
     tails = (
         [((96, 384), bf16)] * 2
         + [((48, 768), bf16)] * 2
-        + [((48, 384), bf16)] * 4
+        + [((48, 384), bf16)]
+        + [((144, 128), bf16)] * 3
         + [((8, 128), f32)]
     )
     scratch = []
     for j, (tail, kind) in enumerate(tails):
         for b, one in enumerate(scatter_buffers(tail, kind)):
             scratch.append(("piece%d_%d" % (j, b), one))
-    for name, (rows, cols) in zip(MATRICES, shapes):
-        scratch.append((name + "_wide", pltpu.VMEM((4, 4, 2 * rows, cols), bf16)))
-        scratch.append((name + "_sib", pltpu.VMEM((rows, cols // 2), f32)))
-        scratch.append((name + "_final", pltpu.VMEM((2 * rows, cols // 2), f32)))
     scratch += pairs_of(
+        qkv_wide=pltpu.VMEM((3, 4, 4, 48, width), bf16),
+        out_wide=pltpu.VMEM((4, 4, 48, width), bf16),
+        up_wide=pltpu.VMEM((4, 4, 48, hidden), bf16),
+        down_wide=pltpu.VMEM((4, 4, 192, width), bf16),
+        qkv_sib=pltpu.VMEM((3, 24, width // 2), f32),
+        out_sib=pltpu.VMEM((24, width // 2), f32),
+        up_sib=pltpu.VMEM((24, hidden // 2), f32),
+        down_sib=pltpu.VMEM((96, width // 2), f32),
+        qkv_final=pltpu.VMEM((3, 48, width // 2), f32),
+        out_final=pltpu.VMEM((48, width // 2), f32),
+        up_final=pltpu.VMEM((48, hidden // 2), f32),
+        down_final=pltpu.VMEM((192, width // 2), f32),
         small_wide=pltpu.VMEM((4, 4, 2, 8, 128), f32),
         small_part=pltpu.VMEM((4, 4, 2, 8, 128), f32),
         small_total=pltpu.VMEM((4, 4, 8, 128), f32),
         down_part=pltpu.VMEM((4, 4, 192, width), bf16),
         down_total=pltpu.VMEM((4, 4, 192, 384), bf16),
-        up_part=pltpu.VMEM((2, 4, 4, 48, 768), bf16),
         up_total=pltpu.VMEM((2, 4, 4, 48, 768), bf16),
-        out_part=pltpu.VMEM((4, 4, 48, 384), bf16),
         out_total=pltpu.VMEM((4, 4, 48, 384), bf16),
-        qkv_total=pltpu.VMEM((3, 4, 4, 48, 384), bf16),
+        qkv_total=pltpu.VMEM((3, 4, 4, 144, 128), bf16),
         present=pltpu.VMEM((count, 128), f32),
         vec=pltpu.VMEM((8, 7 * width), f32),
         sums=pltpu.VMEM((8, 7 * width), f32),
-        bias=pltpu.VMEM((1, 3 * width), f32),
-        chosen=pltpu.VMEM((128, 7 * width), bf16),
+        bias=pltpu.VMEM((3, 8, width), f32),
         owner=pltpu.VMEM((1, 7 * width), f32),
         logsum=pltpu.VMEM((width // 128, 8, count), f32),
         turned_one=pltpu.VMEM((width, count), bf16),
@@ -1259,19 +1610,19 @@
         normed=pltpu.VMEM((count, width), bf16),
         mixed=pltpu.VMEM((count, width), bf16),
         grad_low=pltpu.VMEM((count, width), bf16),
-        joined=pltpu.VMEM((count, 3 * width), bf16),
+        joined=pltpu.VMEM((width // 128, 3, count, 128), bf16),
         middle=pltpu.VMEM((count, width), f32),
         acc=pltpu.VMEM((count, width), f32),
         act=pltpu.VMEM((count, hidden), bf16),
         slope=pltpu.VMEM((2, count, TILE), f32),
-        gather_send=pltpu.SemaphoreType.DMA((9, Piece.COUNT)),
-        gather_recv=pltpu.SemaphoreType.DMA((9, Piece.COUNT)),
-        scatter_send=pltpu.SemaphoreType.DMA((9, Piece.COUNT)),
-        scatter_recv=pltpu.SemaphoreType.DMA((9, Piece.COUNT)),
-        pre_send=pltpu.SemaphoreType.DMA((4,)),
-        pre_recv=pltpu.SemaphoreType.DMA((4,)),
-        end_send=pltpu.SemaphoreType.DMA((4,)),
-        end_recv=pltpu.SemaphoreType.DMA((4,)),
+        send=pltpu.SemaphoreType.DMA((5, Piece.COUNT)),
+        gather_z=pltpu.SemaphoreType.DMA((9, 3)),
+        gather_recv=pltpu.SemaphoreType.DMA((9, 13)),
+        scatter_recv=pltpu.SemaphoreType.DMA((9, 14)),
+        pre_send=pltpu.SemaphoreType.DMA((6,)),
+        pre_recv=pltpu.SemaphoreType.DMA((6,)),
+        end_send=pltpu.SemaphoreType.DMA((6,)),
+        end_recv=pltpu.SemaphoreType.DMA((6,)),
         slope_send=pltpu.SemaphoreType.DMA((2,)),
         slope_recv=pltpu.SemaphoreType.DMA((2,)),
     )

time: 162 us -> 158 us (0.975)
  Pallas kernels: 161 us -> 156 us
    pallas_call x1, Pallas kernels: 157 us -> 153 us  [layer_call(): pl.pallas_call(functools.partial(layer_kernel, names), out_shape=tuple((j...]
where the time goes in v4:
time: 158 us; the launch traced here: 157 us
  Pallas kernels  156 us (99%)
    pallas_call x1, Pallas kernels, layer_call(): pl.pallas_call(functools.partial(layer_kernel, names), out_shape=tuple((j...  153 us
    pallas_call x1, Pallas kernels, deliver(): pl.pallas_call(functools.partial(deliver_kernel, count), out_shape=[jax.S...  3.9 us

profile of v4, /device:TPU:0, one launch (start us, length us, event | category | flops | bytes accessed | tf_op | source)
XLA Modules:
  0.0 157.3 jit_solution(11157911751398037991)
XLA Ops:
  0.7 152.6 %layer.1 = (f32[8,512,384]{2,1,0:T(8,128)}, bf16[512,768]{1,0:T(8,128)(2,1)}, bf16[512,768]{1,0:T(8,128)(2,1)}, f32[24,2304]{1,0:T(8,128)}, f32[24,768]{1,0:T(8,...) custom-call(bf16[512,768]{1,0:T(8,128)(2,1)} %refs_0_.1, s32[1,8]{1,0:T(1,128)} %refs_1_.1, ...), custom_call_target="tpu_custom_call" | custom-call | tf_op jit(solution)/shard_map/layer/pallas_call | solution.py:1632
  153.3 3.9 %deliver.1 = (bf16[512,768]{1,0:T(8,128)(2,1)}, bf16[512,768]{1,0:T(8,128)(2,1)}, f32[24,2304]{1,0:T(8,128)}, f32[24,768]{1,0:T(8,128)}, f32[24,3072]{1,0:T(8,12...) custom-call(bf16[512,768]{1,0:T(8,128)(2,1)} %get-tuple-element.35.r, ...), custom_call_target="tpu_custom_call" | custom-call | tf_op jit(solution)/shard_map/deliver/pallas_call | solution.py:1671

commit v5 on v4

--- a/solution.py
+++ b/solution.py
@@ -318,7 +318,7 @@
 VIA_Y = (1, 3)
 ORDER = (1, 3, 2)
 SCORE_SCALE = math.log2(math.e) / math.sqrt(HEAD)
-TILE = 384
+TILE = 768
 
 
 class Place:
@@ -337,6 +337,7 @@
         self.to_x = (z * 2 + y, (1 - x) * 2 + c)
         self.to_y = (z * 2 + 1 - y, x * 2 + c)
         self.to_c = (z * 2 + y, x * 2 + 1 - c)
+        self.to_d = (z * 2 + 1 - y, (1 - x) * 2 + c)
 
 
 def span(start, size, step):
@@ -345,7 +346,7 @@
 
 def meet(place):
     barrier = pltpu.get_barrier_semaphore()
-    peers = place.to_z[1:] + (place.to_x, place.to_y, place.to_c)
+    peers = place.to_z[1:] + (place.to_x, place.to_y, place.to_d, place.to_c)
     for peer in peers:
         pl.semaphore_signal(barrier, inc=1, device_id=peer, device_id_type=MESH_ID)
     pl.semaphore_wait(barrier, len(peers))
@@ -518,6 +519,51 @@
         return value
 
 
+class SmallScatter(Piece):
+    SLOTS = (4, 4, 4, 1, 2, 3, 0, 0, 0, 0, 0, 0, 0, 0, 0, 0, 0, 0, 0)
+
+    def __init__(self, place, total, arrived, send, recv):
+        super().__init__(place, send, recv, self.SLOTS)
+        self.total, self.arrived = total, arrived
+
+    def give(self, other):
+        self.go(other, lambda: self.total, 15, self.p.to_c)
+
+    def arrive(self):
+        self.got(self.total, 15, self.p.to_c)
+
+    def neighbours(self):
+        p = self.p
+        return ((0, p.qx, p.to_x), (1, p.qy, p.to_y), (2, p.qd, p.to_d))
+
+    def plane(self):
+        for i, q, peer in self.neighbours():
+            self.go(lambda q=q: self.total.at[:, q], lambda i=i: self.arrived.at[i], 3 + i, peer)
+
+    def spread(self):
+        p = self.p
+        value = self.total[:, p.q]
+        for i, _, peer in self.neighbours():
+            self.got(self.arrived.at[i], 3 + i, peer)
+            value = value + self.arrived[i]
+        self.total[:, p.q] = value
+        for k in ORDER:
+            self.go(
+                lambda k=k: self.total.at[p.zs[k], p.q],
+                lambda k=k: self.arrived.at[3, k],
+                k - 1,
+                p.to_z[k],
+            )
+
+    def last(self):
+        p = self.p
+        self.got(self.arrived.at[3, pl.ds(1, 3)], 0, p.to_z[1])
+        value = self.total[p.z, p.q]
+        for k in ORDER:
+            value = value + self.arrived[3, k]
+        return value
+
+
 def scatter_buffers(tail, kind):
     return [
         pltpu.VMEM((2,) + tail, kind),
@@ -573,6 +619,7 @@
         held = []
         while end < len(order) and (order[end][0] not in loops or order[end][0] == kind):
             if order[end][0] == kind:
+                assert order[end][1] == first + len(slots)
                 slots[-1] += held
                 held = []
                 slots.append([])
@@ -668,10 +715,13 @@
     OWN_COLUMN,
     OWN_PART,
     PACK,
+    PREPARE,
     QKV_BACK,
     SECOND_BACK,
     SECOND_NORM,
     SETTLE,
+    SMALL_PLANE,
+    SMALL_SPREAD,
     SPREAD,
     START_XY,
     START_Z,
@@ -680,55 +730,56 @@
     XY_COLUMNS,
     XY_GOT,
     Z_GOT,
-) = range(37)
+) = range(40)
 SEQUENCE = (
     (START_Z, 8),
     (START_XY, 8),
     (FORM, 0),
     (FORM, 1),
-    (FORM, 2),
-    (FORM, 3),
+    (Z_GOT, 8, 1),
     (START_Z, 0),
     (START_Z, 1),
     (START_Z, 2),
     (START_Z, 3),
+    (Z_GOT, 8, 3),
+    (FORM, 2),
     (START_Z, 4),
+    (FORM, 3),
     (START_Z, 5),
     (START_Z, 6),
     (START_Z, 7),
-    (XY_GOT, 8, 0),
-    (Z_GOT, 8, 1),
-    (Z_GOT, 8, 3),
     (Z_GOT, 8, 2),
     (OWN_COLUMN, 8),
-    (START_XY, 0),
+    (XY_GOT, 8, 1),
     (START_XY, 1),
     (START_XY, 2),
-    (MASK_GRAD, 0),
-    (MASK_GRAD, 1),
-    (START_XY, 3),
-    (MASK_GRAD, 2),
-    (XY_GOT, 8, 1),
+    (START_XY, 0),
+    (XY_GOT, 8, 0),
     (XY_GOT, 8, 3),
+    (PREPARE,),
     (XY_GOT, 8, 2),
     (XY_COLUMNS, 8),
-    (MASK_GRAD, 3),
-    (XY_GOT, 0, 0),
     (Z_GOT, 0, 3),
+    (START_XY, 3),
+    (MASK_GRAD, 0),
     (XY_GOT, 1, 0),
+    (MASK_GRAD, 1),
+    (MASK_GRAD, 2),
     (Z_GOT, 0, 2),
     (XY_GOT, 2, 0),
     (Z_GOT, 0, 1),
     (OWN_COLUMN, 0),
-    (XY_GOT, 3, 0),
+    (MASK_GRAD, 3),
+    (XY_GOT, 0, 0),
     (D_GOT, 8),
+    (XY_GOT, 0, 3),
     (C_GOT, 8),
     (UNPACK,),
+    (XY_GOT, 3, 0),
     (XY_GOT, 0, 2),
-    (XY_GOT, 0, 3),
     (Z_GOT, 1, 3),
+    (Z_GOT, 1, 1),
     (Z_GOT, 1, 2),
-    (Z_GOT, 1, 1),
     (OWN_COLUMN, 1),
     (FIRST_NORM, 0),
     (FIRST_NORM, 1),
@@ -737,249 +788,227 @@
     (FIRST_NORM, 2),
     (FIRST_NORM, 3),
     (Z_GOT, 2, 3),
+    (Z_GOT, 2, 2),
+    (Z_GOT, 2, 1),
     (XY_GOT, 1, 3),
-    (Z_GOT, 2, 2),
+    (D_GOT, 0),
+    (OWN_COLUMN, 2),
+    (START_XY, 4),
+    (XY_GOT, 1, 1),
     (XY_GOT, 1, 2),
-    (Z_GOT, 2, 1),
-    (OWN_COLUMN, 2),
-    (XY_GOT, 1, 1),
-    (D_GOT, 0),
+    (C_GOT, 0),
     (XY_COLUMNS, 1),
-    (START_XY, 4),
-    (XY_GOT, 2, 3),
-    (C_GOT, 0),
     (HEADS, 0),
-    (D_GOT, 1),
+    (Z_GOT, 3, 1),
+    (Z_GOT, 3, 3),
     (XY_GOT, 2, 1),
     (XY_GOT, 2, 2),
-    (XY_COLUMNS, 2),
-    (Z_GOT, 3, 1),
-    (Z_GOT, 3, 3),
     (Z_GOT, 3, 2),
     (OWN_COLUMN, 3),
+    (XY_GOT, 2, 3),
+    (XY_COLUMNS, 2),
+    (XY_GOT, 4, 0),
     (HEADS, 1),
+    (D_GOT, 1),
+    (START_XY, 5),
+    (XY_GOT, 3, 1),
+    (XY_GOT, 3, 3),
     (C_GOT, 1),
-    (XY_GOT, 4, 0),
-    (START_XY, 5),
+    (HEADS, 2),
+    (Z_GOT, 4, 3),
     (D_GOT, 2),
-    (HEADS, 2),
+    (Z_GOT, 4, 2),
+    (XY_GOT, 3, 2),
+    (XY_COLUMNS, 3),
+    (HEADS, 3),
     (C_GOT, 2),
-    (XY_GOT, 3, 1),
-    (XY_GOT, 3, 2),
-    (XY_GOT, 3, 3),
-    (XY_COLUMNS, 3),
-    (Z_GOT, 4, 3),
-    (HEADS, 3),
     (Z_GOT, 4, 1),
-    (Z_GOT, 4, 2),
+    (XY_GOT, 5, 0),
     (OWN_COLUMN, 4),
-    (XY_GOT, 5, 0),
     (HEADS, 4),
+    (XY_GOT, 4, 2),
+    (XY_GOT, 4, 3),
+    (START_XY, 6),
     (D_GOT, 3),
-    (XY_GOT, 4, 3),
     (HEADS, 5),
+    (XY_GOT, 4, 1),
+    (XY_COLUMNS, 4),
+    (Z_GOT, 5, 3),
     (C_GOT, 3),
-    (XY_GOT, 4, 1),
-    (Z_GOT, 5, 3),
     (ATTENTION,),
-    (XY_GOT, 4, 2),
-    (XY_COLUMNS, 4),
+    (Z_GOT, 5, 2),
     (SECOND_NORM, 0),
-    (Z_GOT, 5, 2),
     (SECOND_NORM, 1),
+    (Z_GOT, 5, 1),
+    (OWN_COLUMN, 5),
     (SECOND_NORM, 2),
     (SECOND_NORM, 3),
-    (Z_GOT, 5, 1),
-    (OWN_COLUMN, 5),
+    (D_GOT, 4),
+    (XY_GOT, 6, 0),
     (XY_GOT, 5, 3),
-    (D_GOT, 4),
-    (START_XY, 6),
-    (XY_GOT, 5, 2),
     (C_GOT, 4),
     (EXPAND_LOW, 0),
+    (Z_GOT, 6, 3),
+    (XY_GOT, 5, 2),
     (EXPAND_LOW, 1),
     (XY_GOT, 5, 1),
     (XY_COLUMNS, 5),
-    (Z_GOT, 6, 3),
-    (EXPAND_LOW, 2),
     (Z_GOT, 6, 2),
-    (EXPAND_LOW, 3),
-    (XY_GOT, 6, 0),
+    (DOWN_LOW, 0),
+    (DOWN_LOW, 1),
     (Z_GOT, 6, 1),
     (OWN_COLUMN, 6),
-    (DOWN_LOW, 0),
-    (DOWN_LOW, 1),
+    (XY_GOT, 6, 3),
     (D_GOT, 5),
-    (DOWN_LOW, 2),
-    (DOWN_LOW, 3),
-    (XY_GOT, 6, 3),
     (START_XY, 7),
+    (XY_GOT, 6, 2),
     (C_GOT, 5),
     (EXPAND_HIGH, 0),
-    (XY_GOT, 6, 2),
-    (EXPAND_HIGH, 1),
-    (Z_GOT, 7, 3),
-    (EXPAND_HIGH, 2),
     (XY_GOT, 6, 1),
     (XY_COLUMNS, 6),
-    (EXPAND_HIGH, 3),
+    (Z_GOT, 7, 3),
+    (EXPAND_HIGH, 1),
     (Z_GOT, 7, 2),
     (DRAIN,),
+    (Z_GOT, 7, 1),
+    (OWN_COLUMN, 7),
+    (XY_GOT, 7, 0),
     (DOWN_HIGH, 0),
-    (Z_GOT, 7, 1),
-    (XY_GOT, 7, 0),
-    (OWN_COLUMN, 7),
     (DOWN_HIGH, 1),
-    (DOWN_HIGH, 2),
-    (XY_GOT, 7, 3),
-    (DOWN_HIGH, 3),
+    (D_GOT, 6),
     (GIVE, 0),
     (GIVE, 1),
-    (D_GOT, 6),
+    (XY_GOT, 7, 3),
+    (C_GOT, 6),
     (XY_GOT, 7, 2),
     (XY_GOT, 7, 1),
     (XY_COLUMNS, 7),
     (OWN_PART, 0),
     (DIAGONAL, 0),
+    (D_GOT, 7),
     (OWN_PART, 1),
-    (D_GOT, 7),
     (DIAGONAL, 1),
-    (C_GOT, 6),
     (CROSS, 0, 1),
     (CROSS, 0, 0),
+    (C_GOT, 7),
     (CROSS, 0, 3),
-    (C_GOT, 7),
     (NARROW, 0),
     (CROSS, 0, 2),
+    (CROSS, 1, 0),
     (CROSS, 1, 1),
     (NARROW, 1),
-    (CROSS, 1, 0),
     (CROSS, 1, 3),
+    (CROSS, 1, 2),
     (NARROW, 2),
-    (CROSS, 1, 2),
+    (SPREAD, 0, 1),
     (NARROW, 3),
-    (SPREAD, 0, 1),
-    (NARROW, 4),
-    (NARROW, 5),
-    (NARROW, 6),
+    (GIVE, 2),
     (SPREAD, 0, 3),
-    (NARROW, 7),
+    (PACK, 2),
     (SPREAD, 0, 2),
-    (GIVE, 2),
+    (GIVE, 3),
+    (OWN_PART, 2),
+    (DIAGONAL, 2),
     (SPREAD, 1, 1),
-    (GIVE, 3),
-    (SPREAD, 1, 3),
-    (OWN_PART, 2),
-    (SPREAD, 1, 2),
-    (DIAGONAL, 2),
     (FINISH, 0),
     (FINISH, 1),
+    (SPREAD, 1, 3),
     (FINISH, 2),
     (FINISH, 3),
     (UP_BACK,),
+    (SPREAD, 1, 2),
+    (LAST, 0),
     (CROSS, 2, 0),
     (CROSS, 2, 1),
-    (LAST, 0),
     (OWN_PART, 3),
+    (CROSS, 2, 3),
     (CROSS, 2, 2),
-    (CROSS, 2, 3),
     (DIAGONAL, 3),
     (SECOND_BACK, 0),
     (SECOND_BACK, 1),
     (SECOND_BACK, 2),
     (SECOND_BACK, 3),
     (GIVE, 4),
+    (SPREAD, 2, 1),
     (OUT_BACK,),
-    (SPREAD, 2, 1),
+    (SPREAD, 2, 3),
     (HEADS_BACK, 0),
-    (SPREAD, 2, 3),
-    (SPREAD, 2, 2),
+    (CROSS, 3, 0),
     (LAST, 1),
     (CLOSE, 3),
+    (CROSS, 3, 2),
+    (CROSS, 3, 1),
+    (SPREAD, 2, 2),
+    (CROSS, 3, 3),
     (OWN_PART, 4),
-    (CROSS, 3, 0),
-    (CROSS, 3, 1),
     (DIAGONAL, 4),
-    (HEADS_BACK, 1),
-    (CROSS, 3, 2),
-    (CROSS, 3, 3),
     (SETTLE, 3),
     (GIVE, 5),
-    (HEADS_BACK, 2),
+    (HEADS_BACK, 1),
+    (SPREAD, 3, 2),
+    (LAST, 2),
     (SPREAD, 3, 1),
+    (GIVE, 6),
+    (SPREAD, 3, 3),
+    (OWN_PART, 5),
+    (CROSS, 4, 1),
     (CROSS, 4, 0),
-    (CROSS, 4, 1),
     (CROSS, 4, 2),
     (CROSS, 4, 3),
-    (OWN_PART, 5),
     (DIAGONAL, 5),
-    (SPREAD, 3, 2),
-    (LAST, 2),
-    (HEADS_BACK, 3),
-    (SPREAD, 3, 3),
-    (GIVE, 6),
+    (HEADS_BACK, 2),
     (SPREAD, 4, 1),
-    (HEADS_BACK, 4),
     (SPREAD, 4, 3),
     (SPREAD, 4, 2),
     (CROSS, 5, 0),
     (CROSS, 5, 1),
+    (GIVE, 7),
     (CROSS, 5, 2),
     (CROSS, 5, 3),
     (OWN_PART, 6),
     (DIAGONAL, 6),
-    (HEADS_BACK, 5),
+    (PACK, 1),
+    (LAST, 3),
+    (CLOSE, 2),
     (SPREAD, 5, 1),
-    (LAST, 3),
-    (SPREAD, 5, 2),
-    (CLOSE, 2),
-    (GIVE, 7),
-    (SPREAD, 5, 3),
-    (CROSS, 6, 0),
-    (CROSS, 6, 1),
-    (SETTLE, 2),
-    (LAST, 4),
-    (CROSS, 6, 2),
-    (CROSS, 6, 3),
-    (CLOSE, 1),
     (OWN_PART, 7),
     (DIAGONAL, 7),
+    (SPREAD, 5, 2),
+    (QKV_BACK,),
+    (CROSS, 6, 2),
+    (CROSS, 6, 0),
+    (LAST, 4),
+    (CROSS, 7, 0),
+    (SPREAD, 5, 3),
+    (CROSS, 7, 2),
+    (CROSS, 7, 3),
+    (CROSS, 6, 1),
+    (CROSS, 6, 3),
+    (CROSS, 7, 1),
+    (CLOSE, 1),
+    (SETTLE, 2),
+    (FIRST_BACK, 0),
+    (SPREAD, 6, 2),
+    (FIRST_BACK, 1),
     (SETTLE, 1),
-    (QKV_BACK,),
+    (FIRST_BACK, 2),
+    (FIRST_BACK, 3),
+    (LAST, 5),
+    (SPREAD, 7, 2),
+    (PACK, 0),
+    (GIVE, 8),
+    (SPREAD, 7, 3),
     (SPREAD, 6, 1),
     (SPREAD, 6, 3),
-    (SPREAD, 6, 2),
-    (CROSS, 7, 0),
-    (CROSS, 7, 1),
-    (LAST, 5),
-    (CROSS, 7, 2),
-    (CROSS, 7, 3),
-    (FIRST_BACK, 0),
-    (FIRST_BACK, 1),
-    (FIRST_BACK, 2),
-    (FIRST_BACK, 3),
-    (PACK, 0),
+    (OWN_PART, 8),
+    (SMALL_PLANE,),
     (SPREAD, 7, 1),
-    (PACK, 1),
-    (PACK, 2),
-    (SPREAD, 7, 2),
-    (PACK, 3),
-    (GIVE, 8),
-    (SPREAD, 7, 3),
+    (SMALL_SPREAD,),
     (LAST, 6),
-    (OWN_PART, 8),
-    (DIAGONAL, 8),
-    (CROSS, 8, 0),
-    (CROSS, 8, 1),
-    (CROSS, 8, 2),
-    (CROSS, 8, 3),
     (LAST, 7),
-    (SPREAD, 8, 1),
-    (SPREAD, 8, 2),
-    (SPREAD, 8, 3),
     (CLOSE, 0),
+    (LAST, 8),
     (SETTLE, 0),
-    (LAST, 8),
 )
 
 
@@ -1071,10 +1100,12 @@
                     [jnp.where(c == 0, mine, theirs), jnp.where(c == 0, theirs, mine)], axis=0
                 ).astype(jnp.bfloat16)
 
-    fill_present(r.present, r.mask)
-    r.sums[...] = jnp.zeros_like(r.sums)
-    r.owner[...] = owners(width)
-    r.vec[...] = jnp.zeros_like(r.vec)
+    def prepare():
+        fill_present(r.present, r.mask)
+        r.sums[...] = jnp.zeros_like(r.sums)
+        r.owner[...] = owners(width)
+        r.vec[...] = jnp.zeros_like(r.vec)
+        r.small_part[...] = jnp.zeros_like(r.small_part)
 
     def unpack():
         for zz in range(4):
@@ -1188,10 +1219,10 @@
     def down_grad(t):
         cols = span(t * TILE, TILE, 128)
         grad = dot_tn(r.act[:, cols], r.grad_low[...]).astype(jnp.bfloat16)
-        r.down_part[t // 2, pl.ds((t % 2) * 2, 2)] = grad.reshape(2, TILE // 2, width)
-
-    low_tile = lambda u: u + 2 * (u // 2)
-    high_tile = lambda u: u + 2 * (u // 2) + 2
+        r.down_part[t] = grad.reshape(4, TILE // 4, width)
+
+    low_tile = lambda u: 2 * u
+    high_tile = lambda u: 2 * u + 1
 
     def scatter(j, block, column, whole):
         bufs = [getattr(r, "piece%d_%d" % (j, b)) for b in range(5)]
@@ -1237,14 +1268,7 @@
                 lambda s=s: r.qkv_total.at[s],
             )
         )
-    sums.append(
-        scatter(
-            8,
-            lambda zz, q: r.small_total.at[zz, q],
-            lambda q: r.small_total.at[:, q],
-            lambda: r.small_total,
-        )
-    )
+    sums.append(SmallScatter(place, r.small_total, r.small_got, r.send.at[4], r.scatter_recv.at[8]))
 
     def up_part(side, s):
         cols = span(side * (hidden // 2) + 768 * s, 768, 128)
@@ -1283,7 +1307,7 @@
             return lambda q: r.down_wide.at[:, q, pl.ds(96, 48), pl.ds(0, 384)]
         if p < 8:
             return lambda q: r.down_part.at[:, q, pl.ds(0, 144), pl.ds(128 * (p - 5), 128)]
-        return lambda q: r.small_part.at[:, q, 1 - c]
+        return lambda: r.small_part.at[:, :, 1 - c]
 
     def wide_sum(total, value):
         total[...] = (total[...].astype(jnp.float32) + value).astype(total.dtype)
@@ -1306,7 +1330,7 @@
                     value[:, 128 * g : 128 * g + 128].reshape(4, 4, 48, 128),
                 )
         else:
-            wide_sum(r.small_total, r.small_part[:, :, c])
+            r.small_total[...] += r.small_part[:, :, c]
 
     def narrow(t):
         slot = t % 2
@@ -1323,7 +1347,7 @@
             slope_in(t + 1, 1 - slot).start()
 
         cols = span(t * TILE, TILE, 128)
-        weights = r.down_wide[t // 2, pl.ds((t % 2) * 2, 2)].reshape(TILE, width)
+        weights = r.down_wide[t].reshape(TILE, width)
         r.acc[...] += dot(r.act[:, cols], weights)
         grad = (dot_nt(r.grad_low[...], weights) * r.slope[slot]).astype(jnp.bfloat16)
         r.act[:, cols] = grad
@@ -1371,8 +1395,11 @@
             jnp.bfloat16
         )
 
-    def heads_back(i):
-        hp = i // 2 + 3 * (i % 2)
+    def heads_back(s):
+        pair_back(s)
+        pair_back(s + 3)
+
+    def pair_back(hp):
         cols = span(hp * 128, 128, 128)
         query, key, value = r.joined[hp, 0], r.joined[hp, 1], r.joined[hp, 2]
         grad = r.mixed[:, cols]
@@ -1417,26 +1444,26 @@
         part = norm_back(r.acc[rows, :], normed, factor, 0)
         r.input_grad[rows, :] = (r.middle[rows, :] + part).astype(jnp.bfloat16)
 
-    def pack(zz):
-        first = (zz * 8).astype(jnp.float32)
-        for index, (start, size, m) in zip((None, 2, 6), segments(width)):
-            lanes = slice(start, start + size)
-            left = r.sums[:, lanes] if index is None else r.sums[index : index + 1, lanes]
-            owner = r.owner[:, lanes] - first
-            chosen = selection(size, m)
+    def pack(index):
+        start, size, m = segments(width)[index]
+        row = (None, 2, 6)[index]
+        lanes = slice(start, start + size)
+        chosen = selection(size, m)
+        for zz in range(4):
+            left = r.sums[:, lanes] if row is None else r.sums[row : row + 1, lanes]
             tile = 0.0
             for _ in range(2):
                 part = left.astype(jnp.bfloat16).astype(jnp.float32)
                 left = left - part
                 rows = jnp.concatenate(
-                    [jnp.where(owner == d, part, 0.0) for d in range(8)], axis=0
+                    [jnp.where(r.owner[:, lanes] == zz * 8 + d, part, 0.0) for d in range(8)], axis=0
                 ).astype(jnp.bfloat16)
                 tile = tile + dot_nt(rows, chosen)
-            if index is None:
-                r.small_part[zz] = tile.reshape(4, 2, 8, 128)
+            if row is None:
+                r.small_part[zz] += tile.reshape(4, 2, 8, 128)
             else:
                 for d in range(8):
-                    r.small_part[zz, d // 2, d % 2, index : index + 1, :] = tile[d : d + 1, :]
+                    r.small_part[zz, d // 2, d % 2, row : row + 1, :] += tile[d : d + 1, :]
 
     results = (r.qkv_result, r.out_result, r.up_result, r.down_result)
     finals = (r.qkv_final, r.out_final, r.up_final, r.down_final)
@@ -1494,6 +1521,9 @@
 
     steps = {(UNPACK,): unpack, (ATTENTION,): attention, (DRAIN,): drain_slope}
     steps.update({(UP_BACK,): up_back, (OUT_BACK,): out_back, (QKV_BACK,): qkv_back})
+    steps[PREPARE,] = prepare
+    for i in range(3):
+        steps[PACK, i] = functools.partial(pack, i)
     for i in range(4):
         steps[FORM, i] = functools.partial(form, i)
         steps[CLOSE, i] = functools.partial(close, i)
@@ -1508,20 +1538,24 @@
         steps[C_GOT, j] = piece.c
         steps[GIVE, j] = functools.partial(give, j)
         steps[OWN_PART, j] = functools.partial(own_part, j)
-        steps[DIAGONAL, j] = total.diagonal
         steps[LAST, j] = functools.partial(last, j)
         for k in range(4):
             steps[Z_GOT, j, k] = functools.partial(piece.z, k)
             steps[XY_GOT, j, k] = functools.partial(piece.xy, k)
+    for j, total in enumerate(sums[:8]):
+        steps[DIAGONAL, j] = total.diagonal
+        for k in range(4):
             steps[CROSS, j, k] = functools.partial(total.cross, k)
             steps[SPREAD, j, k] = functools.partial(total.spread, k)
+    steps[SMALL_PLANE,] = sums[8].plane
+    steps[SMALL_SPREAD,] = sums[8].spread
     loops = {
         FIRST_NORM: first_norm,
         MASK_GRAD: mask_grad,
         HEADS: heads,
         SECOND_NORM: second_norm,
         EXPAND_LOW: lambda u: expand(low_tile(u), u),
-        EXPAND_HIGH: lambda u: expand(high_tile(u), u + 4),
+        EXPAND_HIGH: lambda u: expand(high_tile(u), u + 2),
         DOWN_LOW: lambda u: down_grad(low_tile(u)),
         DOWN_HIGH: lambda u: down_grad(high_tile(u)),
         NARROW: narrow,
@@ -1529,7 +1563,6 @@
         SECOND_BACK: second_back,
         HEADS_BACK: heads_back,
         FIRST_BACK: first_back,
-        PACK: pack,
     }
     follow(SEQUENCE, steps, loops)
     for m in range(6):
@@ -1571,7 +1604,6 @@
         + [((48, 768), bf16)] * 2
         + [((48, 384), bf16)]
         + [((144, 128), bf16)] * 3
-        + [((8, 128), f32)]
     )
     scratch = []
     for j, (tail, kind) in enumerate(tails):
@@ -1593,6 +1625,7 @@
         small_wide=pltpu.VMEM((4, 4, 2, 8, 128), f32),
         small_part=pltpu.VMEM((4, 4, 2, 8, 128), f32),
         small_total=pltpu.VMEM((4, 4, 8, 128), f32),
+        small_got=pltpu.VMEM((4, 4, 8, 128), f32),
         down_part=pltpu.VMEM((4, 4, 192, width), bf16),
         down_total=pltpu.VMEM((4, 4, 192, 384), bf16),
         up_total=pltpu.VMEM((2, 4, 4, 48, 768), bf16),

time: 158 us -> 153 us (0.968)
  Pallas kernels: 156 us -> 152 us
    pallas_call x1, Pallas kernels: 153 us -> 148 us  [layer_call(): pl.pallas_call(functools.partial(layer_kernel, names), out_shape=tuple((j...]
where the time goes in v5:
time: 153 us
  Pallas kernels  152 us (99%)
    pallas_call x1, Pallas kernels, layer_call(): pl.pallas_call(functools.partial(layer_kernel, names), out_shape=tuple((j...  148 us
    pallas_call x1, Pallas kernels, deliver(): pl.pallas_call(functools.partial(deliver_kernel, count), out_shape=[jax.S...  3.9 us

profile of v5, /device:TPU:0, one launch (start us, length us, event | category | flops | bytes accessed | tf_op | source)
XLA Modules:
  0.0 152.9 jit_solution(10222454923398715279)
XLA Ops:
  0.7 148.2 %layer.1 = (f32[4,512,768]{2,1,0:T(8,128)}, bf16[512,768]{1,0:T(8,128)(2,1)}, bf16[512,768]{1,0:T(8,128)(2,1)}, f32[24,2304]{1,0:T(8,128)}, f32[24,768]{1,0:T(8,...) custom-call(bf16[512,768]{1,0:T(8,128)(2,1)} %refs_0_.1, s32[1,8]{1,0:T(1,128)} %refs_1_.1, ...), custom_call_target="tpu_custom_call" | custom-call | tf_op jit(solution)/shard_map/layer/pallas_call | solution.py:1665
  148.8 3.9 %deliver.1 = (bf16[512,768]{1,0:T(8,128)(2,1)}, bf16[512,768]{1,0:T(8,128)(2,1)}, f32[24,2304]{1,0:T(8,128)}, f32[24,768]{1,0:T(8,128)}, f32[24,3072]{1,0:T(8,12...) custom-call(bf16[512,768]{1,0:T(8,128)(2,1)} %get-tuple-element.35.r, ...), custom_call_target="tpu_custom_call" | custom-call | tf_op jit(solution)/shard_map/deliver/pallas_call | solution.py:1704

commit v6 on v5

--- a/solution.py
+++ b/solution.py
@@ -715,6 +715,8 @@
     OWN_COLUMN,
     OWN_PART,
     PACK,
+    PLANE_GOT,
+    PLANE_START,
     PREPARE,
     QKV_BACK,
     SECOND_BACK,
@@ -730,285 +732,291 @@
     XY_COLUMNS,
     XY_GOT,
     Z_GOT,
-) = range(40)
+) = range(42)
 SEQUENCE = (
     (START_Z, 8),
     (START_XY, 8),
     (FORM, 0),
+    (START_Z, 0),
     (FORM, 1),
-    (Z_GOT, 8, 1),
-    (START_Z, 0),
+    (FORM, 2),
+    (FORM, 3),
     (START_Z, 1),
     (START_Z, 2),
     (START_Z, 3),
-    (Z_GOT, 8, 3),
-    (FORM, 2),
     (START_Z, 4),
-    (FORM, 3),
     (START_Z, 5),
     (START_Z, 6),
+    (Z_GOT, 8, 3),
     (START_Z, 7),
     (Z_GOT, 8, 2),
+    (START_XY, 1),
+    (XY_GOT, 8, 0),
+    (Z_GOT, 8, 1),
     (OWN_COLUMN, 8),
-    (XY_GOT, 8, 1),
-    (START_XY, 1),
     (START_XY, 2),
     (START_XY, 0),
-    (XY_GOT, 8, 0),
+    (PREPARE,),
+    (START_XY, 3),
+    (MASK_GRAD, 0),
+    (MASK_GRAD, 1),
+    (Z_GOT, 0, 1),
     (XY_GOT, 8, 3),
-    (PREPARE,),
+    (MASK_GRAD, 2),
     (XY_GOT, 8, 2),
+    (MASK_GRAD, 3),
+    (XY_GOT, 1, 0),
+    (XY_GOT, 8, 1),
     (XY_COLUMNS, 8),
     (Z_GOT, 0, 3),
-    (START_XY, 3),
-    (MASK_GRAD, 0),
-    (XY_GOT, 1, 0),
-    (MASK_GRAD, 1),
-    (MASK_GRAD, 2),
     (Z_GOT, 0, 2),
+    (OWN_COLUMN, 0),
     (XY_GOT, 2, 0),
-    (Z_GOT, 0, 1),
-    (OWN_COLUMN, 0),
-    (MASK_GRAD, 3),
     (XY_GOT, 0, 0),
+    (XY_GOT, 3, 0),
+    (Z_GOT, 1, 1),
+    (XY_GOT, 0, 1),
     (D_GOT, 8),
-    (XY_GOT, 0, 3),
+    (Z_GOT, 1, 3),
     (C_GOT, 8),
     (UNPACK,),
-    (XY_GOT, 3, 0),
     (XY_GOT, 0, 2),
-    (Z_GOT, 1, 3),
-    (Z_GOT, 1, 1),
     (Z_GOT, 1, 2),
     (OWN_COLUMN, 1),
+    (XY_GOT, 0, 3),
+    (XY_COLUMNS, 0),
     (FIRST_NORM, 0),
     (FIRST_NORM, 1),
-    (XY_GOT, 0, 1),
-    (XY_COLUMNS, 0),
     (FIRST_NORM, 2),
+    (Z_GOT, 2, 1),
     (FIRST_NORM, 3),
+    (XY_GOT, 1, 1),
     (Z_GOT, 2, 3),
     (Z_GOT, 2, 2),
-    (Z_GOT, 2, 1),
+    (OWN_COLUMN, 2),
     (XY_GOT, 1, 3),
     (D_GOT, 0),
-    (OWN_COLUMN, 2),
+    (XY_GOT, 1, 2),
     (START_XY, 4),
-    (XY_GOT, 1, 1),
-    (XY_GOT, 1, 2),
+    (XY_COLUMNS, 1),
+    (Z_GOT, 3, 1),
+    (XY_GOT, 2, 1),
     (C_GOT, 0),
-    (XY_COLUMNS, 1),
     (HEADS, 0),
-    (Z_GOT, 3, 1),
     (Z_GOT, 3, 3),
-    (XY_GOT, 2, 1),
-    (XY_GOT, 2, 2),
+    (XY_GOT, 2, 3),
     (Z_GOT, 3, 2),
     (OWN_COLUMN, 3),
-    (XY_GOT, 2, 3),
+    (D_GOT, 1),
+    (XY_GOT, 2, 2),
     (XY_COLUMNS, 2),
+    (HEADS, 1),
     (XY_GOT, 4, 0),
-    (HEADS, 1),
-    (D_GOT, 1),
     (START_XY, 5),
     (XY_GOT, 3, 1),
-    (XY_GOT, 3, 3),
     (C_GOT, 1),
     (HEADS, 2),
-    (Z_GOT, 4, 3),
+    (Z_GOT, 4, 1),
+    (XY_GOT, 3, 3),
     (D_GOT, 2),
-    (Z_GOT, 4, 2),
+    (HEADS, 3),
     (XY_GOT, 3, 2),
     (XY_COLUMNS, 3),
-    (HEADS, 3),
+    (Z_GOT, 4, 3),
     (C_GOT, 2),
-    (Z_GOT, 4, 1),
+    (HEADS, 4),
+    (Z_GOT, 4, 2),
+    (XY_GOT, 4, 1),
+    (OWN_COLUMN, 4),
     (XY_GOT, 5, 0),
-    (OWN_COLUMN, 4),
-    (HEADS, 4),
-    (XY_GOT, 4, 2),
+    (HEADS, 5),
+    (D_GOT, 3),
     (XY_GOT, 4, 3),
-    (START_XY, 6),
-    (D_GOT, 3),
-    (HEADS, 5),
-    (XY_GOT, 4, 1),
-    (XY_COLUMNS, 4),
-    (Z_GOT, 5, 3),
+    (Z_GOT, 5, 1),
     (C_GOT, 3),
     (ATTENTION,),
+    (XY_GOT, 4, 2),
+    (XY_COLUMNS, 4),
+    (SECOND_NORM, 0),
+    (START_XY, 7),
+    (SECOND_NORM, 1),
+    (SECOND_NORM, 2),
+    (Z_GOT, 5, 3),
+    (SECOND_NORM, 3),
     (Z_GOT, 5, 2),
-    (SECOND_NORM, 0),
-    (SECOND_NORM, 1),
-    (Z_GOT, 5, 1),
     (OWN_COLUMN, 5),
-    (SECOND_NORM, 2),
-    (SECOND_NORM, 3),
+    (XY_GOT, 5, 1),
     (D_GOT, 4),
-    (XY_GOT, 6, 0),
-    (XY_GOT, 5, 3),
+    (XY_GOT, 7, 0),
     (C_GOT, 4),
     (EXPAND_LOW, 0),
+    (START_XY, 6),
+    (EXPAND_LOW, 1),
+    (Z_GOT, 6, 1),
+    (XY_GOT, 5, 3),
+    (DOWN_LOW, 0),
+    (XY_GOT, 5, 2),
+    (XY_COLUMNS, 5),
+    (DOWN_LOW, 1),
     (Z_GOT, 6, 3),
-    (XY_GOT, 5, 2),
-    (EXPAND_LOW, 1),
-    (XY_GOT, 5, 1),
-    (XY_COLUMNS, 5),
     (Z_GOT, 6, 2),
-    (DOWN_LOW, 0),
-    (DOWN_LOW, 1),
-    (Z_GOT, 6, 1),
     (OWN_COLUMN, 6),
+    (XY_GOT, 6, 0),
+    (XY_GOT, 6, 1),
+    (D_GOT, 5),
+    (Z_GOT, 7, 1),
     (XY_GOT, 6, 3),
-    (D_GOT, 5),
-    (START_XY, 7),
-    (XY_GOT, 6, 2),
     (C_GOT, 5),
     (EXPAND_HIGH, 0),
-    (XY_GOT, 6, 1),
+    (EXPAND_HIGH, 1),
+    (Z_GOT, 7, 3),
+    (XY_GOT, 6, 2),
     (XY_COLUMNS, 6),
-    (Z_GOT, 7, 3),
-    (EXPAND_HIGH, 1),
+    (DRAIN,),
+    (DOWN_HIGH, 0),
     (Z_GOT, 7, 2),
-    (DRAIN,),
-    (Z_GOT, 7, 1),
     (OWN_COLUMN, 7),
-    (XY_GOT, 7, 0),
-    (DOWN_HIGH, 0),
     (DOWN_HIGH, 1),
-    (D_GOT, 6),
+    (XY_GOT, 7, 1),
     (GIVE, 0),
     (GIVE, 1),
     (XY_GOT, 7, 3),
-    (C_GOT, 6),
+    (D_GOT, 6),
+    (OWN_PART, 0),
     (XY_GOT, 7, 2),
-    (XY_GOT, 7, 1),
     (XY_COLUMNS, 7),
-    (OWN_PART, 0),
     (DIAGONAL, 0),
-    (D_GOT, 7),
     (OWN_PART, 1),
     (DIAGONAL, 1),
+    (C_GOT, 6),
+    (D_GOT, 7),
+    (CROSS, 0, 0),
     (CROSS, 0, 1),
-    (CROSS, 0, 0),
+    (CROSS, 0, 2),
     (C_GOT, 7),
+    (NARROW, 0),
+    (NARROW, 1),
     (CROSS, 0, 3),
-    (NARROW, 0),
-    (CROSS, 0, 2),
     (CROSS, 1, 0),
     (CROSS, 1, 1),
-    (NARROW, 1),
-    (CROSS, 1, 3),
     (CROSS, 1, 2),
     (NARROW, 2),
-    (SPREAD, 0, 1),
+    (CROSS, 1, 3),
     (NARROW, 3),
     (GIVE, 2),
-    (SPREAD, 0, 3),
+    (SPREAD, 0, 1),
+    (GIVE, 3),
     (PACK, 2),
     (SPREAD, 0, 2),
-    (GIVE, 3),
+    (SPREAD, 0, 3),
     (OWN_PART, 2),
     (DIAGONAL, 2),
-    (SPREAD, 1, 1),
     (FINISH, 0),
     (FINISH, 1),
-    (SPREAD, 1, 3),
     (FINISH, 2),
     (FINISH, 3),
     (UP_BACK,),
     (SPREAD, 1, 2),
-    (LAST, 0),
+    (SPREAD, 1, 1),
+    (OWN_PART, 3),
+    (SPREAD, 1, 3),
+    (DIAGONAL, 3),
     (CROSS, 2, 0),
-    (CROSS, 2, 1),
-    (OWN_PART, 3),
-    (CROSS, 2, 3),
-    (CROSS, 2, 2),
-    (DIAGONAL, 3),
     (SECOND_BACK, 0),
     (SECOND_BACK, 1),
     (SECOND_BACK, 2),
+    (CROSS, 2, 2),
+    (CROSS, 2, 1),
     (SECOND_BACK, 3),
     (GIVE, 4),
-    (SPREAD, 2, 1),
+    (CROSS, 2, 3),
     (OUT_BACK,),
+    (LAST, 0),
+    (CROSS, 3, 0),
+    (CROSS, 3, 1),
+    (HEADS_BACK, 0),
+    (CROSS, 3, 2),
+    (CROSS, 3, 3),
+    (GIVE, 5),
+    (SPREAD, 2, 2),
+    (OWN_PART, 4),
+    (DIAGONAL, 4),
+    (HEADS_BACK, 1),
     (SPREAD, 2, 3),
-    (HEADS_BACK, 0),
-    (CROSS, 3, 0),
     (LAST, 1),
     (CLOSE, 3),
-    (CROSS, 3, 2),
-    (CROSS, 3, 1),
-    (SPREAD, 2, 2),
-    (CROSS, 3, 3),
-    (OWN_PART, 4),
-    (DIAGONAL, 4),
-    (SETTLE, 3),
-    (GIVE, 5),
-    (HEADS_BACK, 1),
-    (SPREAD, 3, 2),
-    (LAST, 2),
+    (SPREAD, 2, 1),
+    (OWN_PART, 5),
+    (DIAGONAL, 5),
     (SPREAD, 3, 1),
     (GIVE, 6),
+    (HEADS_BACK, 2),
     (SPREAD, 3, 3),
-    (OWN_PART, 5),
     (CROSS, 4, 1),
+    (CROSS, 4, 3),
+    (CROSS, 4, 2),
+    (CROSS, 5, 0),
     (CROSS, 4, 0),
-    (CROSS, 4, 2),
-    (CROSS, 4, 3),
-    (DIAGONAL, 5),
-    (HEADS_BACK, 2),
+    (CROSS, 5, 1),
+    (SPREAD, 3, 2),
+    (SETTLE, 3),
+    (OWN_PART, 6),
+    (CROSS, 5, 3),
+    (DIAGONAL, 6),
+    (LAST, 2),
+    (CROSS, 5, 2),
+    (GIVE, 7),
+    (PACK, 1),
     (SPREAD, 4, 1),
     (SPREAD, 4, 3),
     (SPREAD, 4, 2),
-    (CROSS, 5, 0),
-    (CROSS, 5, 1),
-    (GIVE, 7),
-    (CROSS, 5, 2),
-    (CROSS, 5, 3),
-    (OWN_PART, 6),
-    (DIAGONAL, 6),
-    (PACK, 1),
+    (OWN_PART, 7),
+    (DIAGONAL, 7),
+    (QKV_BACK,),
+    (SPREAD, 5, 1),
+    (SPREAD, 5, 3),
+    (FIRST_BACK, 0),
+    (CROSS, 6, 0),
+    (CROSS, 6, 1),
+    (FIRST_BACK, 1),
+    (CROSS, 6, 3),
+    (CROSS, 6, 2),
     (LAST, 3),
     (CLOSE, 2),
-    (SPREAD, 5, 1),
-    (OWN_PART, 7),
-    (DIAGONAL, 7),
+    (FIRST_BACK, 2),
     (SPREAD, 5, 2),
-    (QKV_BACK,),
-    (CROSS, 6, 2),
-    (CROSS, 6, 0),
+    (FIRST_BACK, 3),
+    (CROSS, 7, 0),
+    (CROSS, 7, 1),
+    (PACK, 0),
+    (CROSS, 7, 3),
+    (GIVE, 8),
+    (CROSS, 7, 2),
+    (SETTLE, 2),
     (LAST, 4),
-    (CROSS, 7, 0),
-    (SPREAD, 5, 3),
-    (CROSS, 7, 2),
-    (CROSS, 7, 3),
-    (CROSS, 6, 1),
-    (CROSS, 6, 3),
-    (CROSS, 7, 1),
     (CLOSE, 1),
-    (SETTLE, 2),
-    (FIRST_BACK, 0),
-    (SPREAD, 6, 2),
-    (FIRST_BACK, 1),
-    (SETTLE, 1),
-    (FIRST_BACK, 2),
-    (FIRST_BACK, 3),
-    (LAST, 5),
-    (SPREAD, 7, 2),
-    (PACK, 0),
-    (GIVE, 8),
-    (SPREAD, 7, 3),
     (SPREAD, 6, 1),
     (SPREAD, 6, 3),
     (OWN_PART, 8),
     (SMALL_PLANE,),
+    (SETTLE, 1),
+    (SPREAD, 6, 2),
+    (LAST, 5),
     (SPREAD, 7, 1),
+    (SPREAD, 7, 3),
+    (SPREAD, 7, 2),
     (SMALL_SPREAD,),
     (LAST, 6),
     (LAST, 7),
     (CLOSE, 0),
     (LAST, 8),
     (SETTLE, 0),
+)
+
+
+FETCHED = ("qkv_shard", "out_shard", "up_shard", "down_shard", "tokens", "out_grad")
+STORED = ("qkv_result", "out_result", "up_result", "down_result") + (
+    ("output", "input_grad", "small_result")
 )
 
 
@@ -1021,7 +1029,20 @@
     third = width // 2
     tiles = hidden // TILE
     shards = (r.qkv_shard, r.out_shard, r.up_shard, r.down_shard)
+
+    def fetch(i):
+        name = FETCHED[i]
+        return pltpu.make_async_copy(getattr(r, name + "_in"), getattr(r, name), r.load.at[i])
+
+    def store(i):
+        name = STORED[i]
+        return pltpu.make_async_copy(getattr(r, name), getattr(r, name + "_out"), r.save.at[i])
+
+    for i in range(len(FETCHED)):
+        fetch(i).start()
     meet(place)
+    for i in range(4):
+        fetch(i).wait()
 
     moves = [(0, g * width, third, (g,)) for g in range(3)] + [
         (i, 0, shards[i].shape[1] // 2, ()) for i in (1, 2, 3)
@@ -1101,6 +1122,8 @@
                 ).astype(jnp.bfloat16)
 
     def prepare():
+        for i in range(4, len(FETCHED)):
+            fetch(i).wait()
         fill_present(r.present, r.mask)
         r.sums[...] = jnp.zeros_like(r.sums)
         r.owner[...] = owners(width)
@@ -1365,6 +1388,10 @@
             r.middle[rows, :]
             + r.present[rows, 0:1] * (r.acc[rows, :] + r.vec[7:8, 0:width])
         ).astype(jnp.bfloat16)
+
+        @pl.when(t == tokens // 128 - 1)
+        def _():
+            store(4).start()
 
     def up_back():
         r.acc[...] = dot_nt(r.act[...], r.up_wide[...].reshape(width, hidden))
@@ -1444,6 +1471,10 @@
         part = norm_back(r.acc[rows, :], normed, factor, 0)
         r.input_grad[rows, :] = (r.middle[rows, :] + part).astype(jnp.bfloat16)
 
+        @pl.when(t == tokens // 128 - 1)
+        def _():
+            store(5).start()
+
     def pack(index):
         start, size, m = segments(width)[index]
         row = (None, 2, 6)[index]
@@ -1492,6 +1523,7 @@
         for m, move in enumerate(moves):
             if move[0] == i:
                 swap(m, 1 - c).wait_recv()
+        store(i).start()
 
     def last(p):
         value = sums[p].last()
@@ -1506,6 +1538,7 @@
                 r.qkv_final[g, :, 128 * (p - 5) : 128 * (p - 4)] = value[48 * g : 48 * g + 48]
         else:
             r.small_result[...] = value
+            store(6).start()
 
     def start_xy(j):
         if 4 <= j < 8:
@@ -1570,6 +1603,8 @@
         swap(m, c).wait_send()
     for piece in pieces + sums:
         piece.finish()
+    for i in range(len(STORED)):
+        store(i).wait()
 
 
 def layer_call(tokens, band_mask, out_grad, shards, smalls):
@@ -1580,32 +1615,23 @@
     tiles = hidden // TILE
     vmem = pl.BlockSpec(memory_space=pltpu.VMEM)
     anywhere = pl.BlockSpec(memory_space=pl.ANY)
-    inputs = triples(
-        tokens=(tokens, vmem),
-        mask=(band_mask, pl.BlockSpec(memory_space=pltpu.SMEM)),
-        out_grad=(out_grad, vmem),
-        qkv_shard=(shards[0], vmem),
-        out_shard=(shards[1], vmem),
-        up_shard=(shards[2], vmem),
-        down_shard=(shards[3], vmem),
-    ) + [("vector%d" % i, v, vmem) for i, v in enumerate(smalls)]
-    outs = triples(
-        slope_far=((tiles, count, TILE), f32),
-        output=((count, width), bf16),
-        input_grad=((count, width), bf16),
-        qkv_result=(shapes[0], f32),
-        out_result=(shapes[1], f32),
-        up_result=(shapes[2], f32),
-        down_result=(shapes[3], f32),
-        small_result=((8, 128), f32),
-    )
+    fetched = dict(zip(FETCHED, (*shards, tokens, out_grad)))
+    inputs = [(name + "_in", array, anywhere) for name, array in fetched.items()]
+    inputs += triples(mask=(band_mask, pl.BlockSpec(memory_space=pltpu.SMEM)))
+    inputs += [("vector%d" % i, v, vmem) for i, v in enumerate(smalls)]
+    stored = list(zip(STORED, shapes + [(count, width)] * 2 + [(8, 128)]))
+    kinds = [f32] * 4 + [bf16] * 2 + [f32]
+    outs = triples(slope_far=((tiles, count, TILE), f32)) + [
+        (name + "_out", shape, kind) for (name, shape), kind in zip(stored, kinds)
+    ]
     tails = (
         [((96, 384), bf16)] * 2
         + [((48, 768), bf16)] * 2
         + [((48, 384), bf16)]
         + [((144, 128), bf16)] * 3
     )
-    scratch = []
+    scratch = [(name, pltpu.VMEM(a.shape, a.dtype)) for name, a in fetched.items()]
+    scratch += [(name, pltpu.VMEM(shape, kind)) for (name, shape), kind in zip(stored, kinds)]
     for j, (tail, kind) in enumerate(tails):
         for b, one in enumerate(scatter_buffers(tail, kind)):
             scratch.append(("piece%d_%d" % (j, b), one))
@@ -1656,6 +1682,8 @@
         pre_recv=pltpu.SemaphoreType.DMA((6,)),
         end_send=pltpu.SemaphoreType.DMA((6,)),
         end_recv=pltpu.SemaphoreType.DMA((6,)),
+        load=pltpu.SemaphoreType.DMA((len(FETCHED),)),
+        save=pltpu.SemaphoreType.DMA((len(STORED),)),
         slope_send=pltpu.SemaphoreType.DMA((2,)),
         slope_recv=pltpu.SemaphoreType.DMA((2,)),
     )
@@ -1666,49 +1694,35 @@
         functools.partial(layer_kernel, names),
         out_shape=tuple(jax.ShapeDtypeStruct(shape, kind) for _, shape, kind in outs),
         in_specs=[spec for _, _, spec in inputs],
-        out_specs=(anywhere,) + (vmem,) * (len(outs) - 1),
+        out_specs=(anywhere,) * len(outs),
         scratch_shapes=[kind for _, kind in scratch],
         compiler_params=pltpu.CompilerParams(
             collective_id=0, has_side_effects=True, vmem_limit_bytes=VMEM_BYTES
         ),
         name="layer",
     )(*[array for _, array, _ in inputs])
-    return results[1:]
+    qkv, out, up, down, output, input_grad, small = results[1:]
+    return output, input_grad, qkv, out, up, down, small
 
 
 def deliver_kernel(count, *refs):
     sources, tile = refs[:count], refs[count]
     targets = refs[count + 1 : 2 * count + 1]
-    vectors = refs[2 * count + 1 : -count - 2]
-    stages = refs[-count - 2 : -2]
-    get, put = refs[-2:]
-    arriving = [
-        pltpu.make_async_copy(sources[i], stages[i], get.at[i]) for i in range(count)
-    ]
-    leaving = [pltpu.make_async_copy(stages[i], targets[i], put.at[i]) for i in range(count)]
-    for copy in arriving:
-        copy.start()
-    for i, vector in enumerate(vectors):
+    for source, target in zip(sources, targets):
+        target[...] = source[...]
+    for i, vector in enumerate(refs[2 * count + 1 :]):
         vector[...] = tile[i, 0 : vector.shape[0]]
-    for first, second in zip(arriving, leaving):
-        first.wait()
-        second.start()
-    for copy in leaving:
-        copy.wait()
 
 
 def deliver(whole, tile, sizes):
     count = len(whole)
-    anywhere = pl.BlockSpec(memory_space=pl.ANY)
     vmem = pl.BlockSpec(memory_space=pltpu.VMEM)
     return pl.pallas_call(
         functools.partial(deliver_kernel, count),
         out_shape=[jax.ShapeDtypeStruct(a.shape, a.dtype) for a in whole]
         + [jax.ShapeDtypeStruct((m,), jnp.float32) for m in sizes],
-        in_specs=[anywhere] * count + [vmem],
-        out_specs=[anywhere] * count + [vmem] * len(sizes),
-        scratch_shapes=[pltpu.VMEM(a.shape, a.dtype) for a in whole]
-        + [pltpu.SemaphoreType.DMA((count,))] * 2,
+        in_specs=[vmem] * (count + 1),
+        out_specs=[vmem] * (count + len(sizes)),
         compiler_params=pltpu.CompilerParams(vmem_limit_bytes=VMEM_BYTES),
         name="deliver",
     )(*whole, tile)

time: 153 us -> 146 us (0.954)
  Pallas kernels: 152 us -> 145 us
    pallas_call x1, Pallas kernels: 148 us -> 142 us  [layer_call(): pl.pallas_call(functools.partial(layer_kernel, names), out_shape=tuple((j...]
where the time goes in v6:
time: 146 us
  Pallas kernels  145 us (99%)
    pallas_call x1, Pallas kernels, layer_call(): pl.pallas_call(functools.partial(layer_kernel, names), out_shape=tuple((j...  142 us
    pallas_call x1, Pallas kernels, deliver(): pl.pallas_call(functools.partial(deliver_kernel, count), out_shape=[jax.S...  3.13 us

profile of v6, /device:TPU:0, one launch (start us, length us, event | category | flops | bytes accessed | tf_op | source)
XLA Modules:
  0.0 145.5 jit_solution(9891429046755991499)
XLA Ops:
  0.7 141.6 %layer.1 = (f32[4,512,768]{2,1,0:T(8,128)}, f32[24,2304]{1,0:T(8,128)}, f32[24,768]{1,0:T(8,128)}, f32[24,3072]{1,0:T(8,128)}, f32[96,768]{1,0:T(8,128)}, /*inde...) custom-call(f32[24,2304]{1,0:T(8,128)} %refs_0_.1, f32[24,768]{1,0:T(8,128)} %refs_1_.1, ...), custom_call_target="tpu_custom_call" | custom-call | tf_op jit(solution)/shard_map/layer/pallas_call | solution.py:1693
  142.2 3.1 %deliver.1 = (bf16[512,768]{1,0:T(8,128)(2,1)}, bf16[512,768]{1,0:T(8,128)(2,1)}, f32[24,2304]{1,0:T(8,128)}, f32[24,768]{1,0:T(8,128)}, f32[24,3072]{1,0:T(8,12...) custom-call(bf16[512,768]{1,0:T(8,128)(2,1)} %get-tuple-element.35.r, ...), custom_call_target="tpu_custom_call" | custom-call | tf_op jit(solution)/shard_map/deliver/pallas_call | solution.py:1720

commit v7 on v6

--- a/solution.py
+++ b/solution.py
@@ -737,272 +737,272 @@
     (START_Z, 8),
     (START_XY, 8),
     (FORM, 0),
-    (START_Z, 0),
     (FORM, 1),
     (FORM, 2),
     (FORM, 3),
+    (START_Z, 0),
     (START_Z, 1),
     (START_Z, 2),
+    (START_XY, 0),
+    (Z_GOT, 8, 1),
+    (Z_GOT, 8, 3),
+    (Z_GOT, 8, 2),
     (START_Z, 3),
     (START_Z, 4),
     (START_Z, 5),
     (START_Z, 6),
-    (Z_GOT, 8, 3),
     (START_Z, 7),
-    (Z_GOT, 8, 2),
+    (START_XY, 3),
+    (XY_GOT, 8, 0),
+    (OWN_COLUMN, 8),
     (START_XY, 1),
-    (XY_GOT, 8, 0),
-    (Z_GOT, 8, 1),
-    (OWN_COLUMN, 8),
     (START_XY, 2),
-    (START_XY, 0),
     (PREPARE,),
-    (START_XY, 3),
     (MASK_GRAD, 0),
     (MASK_GRAD, 1),
+    (MASK_GRAD, 2),
+    (XY_GOT, 8, 1),
+    (XY_GOT, 0, 0),
+    (XY_GOT, 8, 2),
+    (XY_GOT, 8, 3),
+    (XY_COLUMNS, 8),
+    (MASK_GRAD, 3),
     (Z_GOT, 0, 1),
-    (XY_GOT, 8, 3),
-    (MASK_GRAD, 2),
-    (XY_GOT, 8, 2),
-    (MASK_GRAD, 3),
+    (XY_GOT, 3, 0),
+    (Z_GOT, 0, 2),
     (XY_GOT, 1, 0),
-    (XY_GOT, 8, 1),
-    (XY_COLUMNS, 8),
     (Z_GOT, 0, 3),
-    (Z_GOT, 0, 2),
     (OWN_COLUMN, 0),
     (XY_GOT, 2, 0),
-    (XY_GOT, 0, 0),
-    (XY_GOT, 3, 0),
+    (D_GOT, 8),
     (Z_GOT, 1, 1),
     (XY_GOT, 0, 1),
-    (D_GOT, 8),
-    (Z_GOT, 1, 3),
     (C_GOT, 8),
     (UNPACK,),
+    (Z_GOT, 1, 3),
     (XY_GOT, 0, 2),
     (Z_GOT, 1, 2),
     (OWN_COLUMN, 1),
-    (XY_GOT, 0, 3),
-    (XY_COLUMNS, 0),
     (FIRST_NORM, 0),
     (FIRST_NORM, 1),
     (FIRST_NORM, 2),
     (Z_GOT, 2, 1),
+    (XY_GOT, 0, 3),
+    (XY_COLUMNS, 0),
     (FIRST_NORM, 3),
+    (Z_GOT, 2, 2),
+    (Z_GOT, 2, 3),
+    (OWN_COLUMN, 2),
     (XY_GOT, 1, 1),
-    (Z_GOT, 2, 3),
-    (Z_GOT, 2, 2),
-    (OWN_COLUMN, 2),
     (XY_GOT, 1, 3),
+    (Z_GOT, 3, 1),
+    (XY_GOT, 1, 2),
+    (XY_COLUMNS, 1),
     (D_GOT, 0),
-    (XY_GOT, 1, 2),
     (START_XY, 4),
-    (XY_COLUMNS, 1),
-    (Z_GOT, 3, 1),
+    (Z_GOT, 3, 2),
+    (Z_GOT, 3, 3),
+    (OWN_COLUMN, 3),
     (XY_GOT, 2, 1),
+    (XY_GOT, 2, 2),
+    (XY_GOT, 2, 3),
+    (XY_COLUMNS, 2),
     (C_GOT, 0),
     (HEADS, 0),
-    (Z_GOT, 3, 3),
-    (XY_GOT, 2, 3),
-    (Z_GOT, 3, 2),
-    (OWN_COLUMN, 3),
     (D_GOT, 1),
-    (XY_GOT, 2, 2),
-    (XY_COLUMNS, 2),
+    (XY_GOT, 3, 1),
+    (START_XY, 5),
     (HEADS, 1),
     (XY_GOT, 4, 0),
-    (START_XY, 5),
-    (XY_GOT, 3, 1),
+    (Z_GOT, 4, 1),
+    (XY_GOT, 3, 2),
     (C_GOT, 1),
     (HEADS, 2),
-    (Z_GOT, 4, 1),
+    (Z_GOT, 4, 2),
+    (D_GOT, 2),
+    (Z_GOT, 4, 3),
+    (OWN_COLUMN, 4),
     (XY_GOT, 3, 3),
-    (D_GOT, 2),
+    (XY_COLUMNS, 3),
     (HEADS, 3),
-    (XY_GOT, 3, 2),
-    (XY_COLUMNS, 3),
-    (Z_GOT, 4, 3),
+    (XY_GOT, 5, 0),
     (C_GOT, 2),
     (HEADS, 4),
-    (Z_GOT, 4, 2),
+    (Z_GOT, 5, 1),
     (XY_GOT, 4, 1),
-    (OWN_COLUMN, 4),
-    (XY_GOT, 5, 0),
+    (Z_GOT, 5, 2),
     (HEADS, 5),
+    (Z_GOT, 5, 3),
+    (XY_GOT, 4, 2),
+    (OWN_COLUMN, 5),
+    (XY_GOT, 4, 3),
+    (XY_COLUMNS, 4),
     (D_GOT, 3),
-    (XY_GOT, 4, 3),
-    (Z_GOT, 5, 1),
+    (XY_GOT, 5, 1),
     (C_GOT, 3),
     (ATTENTION,),
-    (XY_GOT, 4, 2),
-    (XY_COLUMNS, 4),
+    (START_XY, 7),
     (SECOND_NORM, 0),
-    (START_XY, 7),
     (SECOND_NORM, 1),
+    (XY_GOT, 5, 2),
     (SECOND_NORM, 2),
-    (Z_GOT, 5, 3),
     (SECOND_NORM, 3),
-    (Z_GOT, 5, 2),
-    (OWN_COLUMN, 5),
-    (XY_GOT, 5, 1),
+    (XY_GOT, 5, 3),
+    (XY_COLUMNS, 5),
     (D_GOT, 4),
-    (XY_GOT, 7, 0),
+    (START_XY, 6),
+    (Z_GOT, 6, 3),
+    (Z_GOT, 6, 2),
+    (Z_GOT, 6, 1),
+    (OWN_COLUMN, 6),
+    (Z_GOT, 7, 1),
     (C_GOT, 4),
     (EXPAND_LOW, 0),
-    (START_XY, 6),
+    (Z_GOT, 7, 2),
+    (Z_GOT, 7, 3),
+    (XY_GOT, 7, 0),
+    (OWN_COLUMN, 7),
     (EXPAND_LOW, 1),
-    (Z_GOT, 6, 1),
-    (XY_GOT, 5, 3),
+    (D_GOT, 5),
     (DOWN_LOW, 0),
-    (XY_GOT, 5, 2),
-    (XY_COLUMNS, 5),
     (DOWN_LOW, 1),
-    (Z_GOT, 6, 3),
-    (Z_GOT, 6, 2),
-    (OWN_COLUMN, 6),
     (XY_GOT, 6, 0),
-    (XY_GOT, 6, 1),
-    (D_GOT, 5),
-    (Z_GOT, 7, 1),
-    (XY_GOT, 6, 3),
     (C_GOT, 5),
     (EXPAND_HIGH, 0),
+    (XY_GOT, 6, 3),
     (EXPAND_HIGH, 1),
-    (Z_GOT, 7, 3),
     (XY_GOT, 6, 2),
-    (XY_COLUMNS, 6),
     (DRAIN,),
     (DOWN_HIGH, 0),
-    (Z_GOT, 7, 2),
-    (OWN_COLUMN, 7),
+    (XY_GOT, 6, 1),
+    (XY_COLUMNS, 6),
     (DOWN_HIGH, 1),
-    (XY_GOT, 7, 1),
     (GIVE, 0),
     (GIVE, 1),
+    (XY_GOT, 7, 1),
+    (XY_GOT, 7, 2),
     (XY_GOT, 7, 3),
+    (XY_COLUMNS, 7),
+    (OWN_PART, 0),
+    (DIAGONAL, 0),
     (D_GOT, 6),
-    (OWN_PART, 0),
-    (XY_GOT, 7, 2),
-    (XY_COLUMNS, 7),
-    (DIAGONAL, 0),
     (OWN_PART, 1),
     (DIAGONAL, 1),
+    (CROSS, 0, 1),
+    (D_GOT, 7),
     (C_GOT, 6),
-    (D_GOT, 7),
+    (CROSS, 0, 3),
     (CROSS, 0, 0),
-    (CROSS, 0, 1),
-    (CROSS, 0, 2),
     (C_GOT, 7),
     (NARROW, 0),
+    (CROSS, 1, 1),
     (NARROW, 1),
-    (CROSS, 0, 3),
+    (CROSS, 0, 2),
     (CROSS, 1, 0),
-    (CROSS, 1, 1),
+    (CROSS, 1, 3),
+    (NARROW, 2),
     (CROSS, 1, 2),
-    (NARROW, 2),
-    (CROSS, 1, 3),
     (NARROW, 3),
+    (SPREAD, 0, 1),
     (GIVE, 2),
-    (SPREAD, 0, 1),
+    (SPREAD, 0, 3),
     (GIVE, 3),
     (PACK, 2),
-    (SPREAD, 0, 2),
-    (SPREAD, 0, 3),
+    (SPREAD, 1, 1),
     (OWN_PART, 2),
     (DIAGONAL, 2),
+    (SPREAD, 0, 2),
     (FINISH, 0),
     (FINISH, 1),
     (FINISH, 2),
     (FINISH, 3),
     (UP_BACK,),
-    (SPREAD, 1, 2),
-    (SPREAD, 1, 1),
-    (OWN_PART, 3),
     (SPREAD, 1, 3),
-    (DIAGONAL, 3),
-    (CROSS, 2, 0),
     (SECOND_BACK, 0),
     (SECOND_BACK, 1),
+    (SPREAD, 1, 2),
+    (CROSS, 2, 1),
     (SECOND_BACK, 2),
-    (CROSS, 2, 2),
-    (CROSS, 2, 1),
+    (OWN_PART, 3),
+    (CROSS, 2, 0),
+    (CROSS, 2, 3),
+    (DIAGONAL, 3),
+    (LAST, 0),
     (SECOND_BACK, 3),
     (GIVE, 4),
-    (CROSS, 2, 3),
+    (CROSS, 2, 2),
     (OUT_BACK,),
-    (LAST, 0),
+    (SPREAD, 2, 1),
+    (HEADS_BACK, 0),
+    (SPREAD, 2, 3),
+    (GIVE, 5),
+    (LAST, 1),
     (CROSS, 3, 0),
     (CROSS, 3, 1),
-    (HEADS_BACK, 0),
-    (CROSS, 3, 2),
-    (CROSS, 3, 3),
-    (GIVE, 5),
-    (SPREAD, 2, 2),
+    (CLOSE, 3),
     (OWN_PART, 4),
     (DIAGONAL, 4),
     (HEADS_BACK, 1),
-    (SPREAD, 2, 3),
-    (LAST, 1),
-    (CLOSE, 3),
-    (SPREAD, 2, 1),
+    (CROSS, 3, 3),
+    (CROSS, 3, 2),
+    (SETTLE, 3),
+    (SPREAD, 2, 2),
     (OWN_PART, 5),
     (DIAGONAL, 5),
     (SPREAD, 3, 1),
     (GIVE, 6),
+    (CROSS, 4, 0),
+    (CROSS, 4, 1),
     (HEADS_BACK, 2),
+    (SPREAD, 3, 2),
+    (CROSS, 4, 2),
     (SPREAD, 3, 3),
-    (CROSS, 4, 1),
     (CROSS, 4, 3),
-    (CROSS, 4, 2),
     (CROSS, 5, 0),
-    (CROSS, 4, 0),
+    (LAST, 2),
     (CROSS, 5, 1),
-    (SPREAD, 3, 2),
-    (SETTLE, 3),
+    (GIVE, 7),
+    (CROSS, 5, 3),
+    (CROSS, 5, 2),
     (OWN_PART, 6),
-    (CROSS, 5, 3),
     (DIAGONAL, 6),
-    (LAST, 2),
-    (CROSS, 5, 2),
-    (GIVE, 7),
     (PACK, 1),
     (SPREAD, 4, 1),
-    (SPREAD, 4, 3),
     (SPREAD, 4, 2),
     (OWN_PART, 7),
+    (SPREAD, 4, 3),
     (DIAGONAL, 7),
     (QKV_BACK,),
     (SPREAD, 5, 1),
     (SPREAD, 5, 3),
     (FIRST_BACK, 0),
+    (SPREAD, 5, 2),
+    (FIRST_BACK, 1),
     (CROSS, 6, 0),
     (CROSS, 6, 1),
-    (FIRST_BACK, 1),
+    (FIRST_BACK, 2),
+    (FIRST_BACK, 3),
     (CROSS, 6, 3),
     (CROSS, 6, 2),
-    (LAST, 3),
-    (CLOSE, 2),
-    (FIRST_BACK, 2),
-    (SPREAD, 5, 2),
-    (FIRST_BACK, 3),
+    (PACK, 0),
+    (GIVE, 8),
     (CROSS, 7, 0),
     (CROSS, 7, 1),
-    (PACK, 0),
+    (LAST, 3),
     (CROSS, 7, 3),
-    (GIVE, 8),
+    (CLOSE, 2),
     (CROSS, 7, 2),
-    (SETTLE, 2),
+    (OWN_PART, 8),
+    (SMALL_PLANE,),
+    (SPREAD, 6, 1),
     (LAST, 4),
     (CLOSE, 1),
-    (SPREAD, 6, 1),
     (SPREAD, 6, 3),
-    (OWN_PART, 8),
-    (SMALL_PLANE,),
+    (SETTLE, 2),
+    (SPREAD, 6, 2),
     (SETTLE, 1),
-    (SPREAD, 6, 2),
+    (SPREAD, 7, 1),
     (LAST, 5),
-    (SPREAD, 7, 1),
     (SPREAD, 7, 3),
     (SPREAD, 7, 2),
     (SMALL_SPREAD,),

time: 146 us -> 144 us (0.986)
  Pallas kernels: 145 us -> 143 us
    pallas_call x1, Pallas kernels: 142 us -> 140 us  [layer_call(): pl.pallas_call(functools.partial(layer_kernel, names), out_shape=tuple((j...]
where the time goes in v7:
time: 144 us
  Pallas kernels  143 us (99%)
    pallas_call x1, Pallas kernels, layer_call(): pl.pallas_call(functools.partial(layer_kernel, names), out_shape=tuple((j...  140 us
    pallas_call x1, Pallas kernels, deliver(): pl.pallas_call(functools.partial(deliver_kernel, count), out_shape=[jax.S...  3.13 us

profile of v7, /device:TPU:0, one launch (start us, length us, event | category | flops | bytes accessed | tf_op | source)
XLA Modules:
  0.0 143.9 jit_solution(12500575415205712325)
XLA Ops:
  0.7 140.0 %layer.1 = (f32[4,512,768]{2,1,0:T(8,128)}, f32[24,2304]{1,0:T(8,128)}, f32[24,768]{1,0:T(8,128)}, f32[24,3072]{1,0:T(8,128)}, f32[96,768]{1,0:T(8,128)}, /*inde...) custom-call(f32[24,2304]{1,0:T(8,128)} %refs_0_.1, f32[24,768]{1,0:T(8,128)} %refs_1_.1, ...), custom_call_target="tpu_custom_call" | custom-call | tf_op jit(solution)/shard_map/layer/pallas_call | solution.py:1693
  140.6 3.1 %deliver.1 = (bf16[512,768]{1,0:T(8,128)(2,1)}, bf16[512,768]{1,0:T(8,128)(2,1)}, f32[24,2304]{1,0:T(8,128)}, f32[24,768]{1,0:T(8,128)}, f32[24,3072]{1,0:T(8,12...) custom-call(bf16[512,768]{1,0:T(8,128)(2,1)} %get-tuple-element.35.r, ...), custom_call_target="tpu_custom_call" | custom-call | tf_op jit(solution)/shard_map/deliver/pallas_call | solution.py:1720

commit v8 on v7

--- a/solution.py
+++ b/solution.py
@@ -737,269 +737,269 @@
     (START_Z, 8),
     (START_XY, 8),
     (FORM, 0),
+    (START_Z, 0),
     (FORM, 1),
     (FORM, 2),
     (FORM, 3),
-    (START_Z, 0),
     (START_Z, 1),
     (START_Z, 2),
-    (START_XY, 0),
-    (Z_GOT, 8, 1),
-    (Z_GOT, 8, 3),
-    (Z_GOT, 8, 2),
     (START_Z, 3),
     (START_Z, 4),
+    (START_XY, 2),
+    (START_XY, 1),
+    (Z_GOT, 8, 3),
+    (XY_GOT, 8, 0),
+    (Z_GOT, 8, 1),
+    (Z_GOT, 8, 2),
+    (OWN_COLUMN, 8),
     (START_Z, 5),
     (START_Z, 6),
     (START_Z, 7),
+    (START_XY, 0),
     (START_XY, 3),
-    (XY_GOT, 8, 0),
-    (OWN_COLUMN, 8),
-    (START_XY, 1),
-    (START_XY, 2),
     (PREPARE,),
     (MASK_GRAD, 0),
     (MASK_GRAD, 1),
     (MASK_GRAD, 2),
-    (XY_GOT, 8, 1),
-    (XY_GOT, 0, 0),
-    (XY_GOT, 8, 2),
-    (XY_GOT, 8, 3),
-    (XY_COLUMNS, 8),
     (MASK_GRAD, 3),
     (Z_GOT, 0, 1),
-    (XY_GOT, 3, 0),
+    (XY_GOT, 2, 0),
     (Z_GOT, 0, 2),
     (XY_GOT, 1, 0),
+    (XY_GOT, 8, 3),
     (Z_GOT, 0, 3),
     (OWN_COLUMN, 0),
-    (XY_GOT, 2, 0),
-    (D_GOT, 8),
+    (XY_GOT, 8, 1),
+    (XY_GOT, 8, 2),
+    (XY_COLUMNS, 8),
+    (XY_GOT, 0, 0),
+    (XY_GOT, 3, 0),
     (Z_GOT, 1, 1),
     (XY_GOT, 0, 1),
-    (C_GOT, 8),
-    (UNPACK,),
+    (Z_GOT, 1, 2),
     (Z_GOT, 1, 3),
+    (OWN_COLUMN, 1),
     (XY_GOT, 0, 2),
-    (Z_GOT, 1, 2),
-    (OWN_COLUMN, 1),
-    (FIRST_NORM, 0),
-    (FIRST_NORM, 1),
-    (FIRST_NORM, 2),
     (Z_GOT, 2, 1),
     (XY_GOT, 0, 3),
     (XY_COLUMNS, 0),
-    (FIRST_NORM, 3),
+    (D_GOT, 8),
     (Z_GOT, 2, 2),
     (Z_GOT, 2, 3),
     (OWN_COLUMN, 2),
+    (C_GOT, 8),
+    (UNPACK,),
     (XY_GOT, 1, 1),
+    (Z_GOT, 3, 1),
+    (FIRST_NORM, 0),
+    (XY_GOT, 1, 2),
+    (FIRST_NORM, 1),
+    (FIRST_NORM, 2),
+    (Z_GOT, 3, 2),
     (XY_GOT, 1, 3),
-    (Z_GOT, 3, 1),
-    (XY_GOT, 1, 2),
     (XY_COLUMNS, 1),
+    (Z_GOT, 3, 3),
     (D_GOT, 0),
+    (OWN_COLUMN, 3),
+    (FIRST_NORM, 3),
     (START_XY, 4),
-    (Z_GOT, 3, 2),
-    (Z_GOT, 3, 3),
-    (OWN_COLUMN, 3),
     (XY_GOT, 2, 1),
     (XY_GOT, 2, 2),
     (XY_GOT, 2, 3),
     (XY_COLUMNS, 2),
+    (XY_GOT, 3, 1),
     (C_GOT, 0),
     (HEADS, 0),
+    (Z_GOT, 4, 1),
     (D_GOT, 1),
-    (XY_GOT, 3, 1),
     (START_XY, 5),
+    (XY_GOT, 3, 2),
     (HEADS, 1),
+    (XY_GOT, 3, 3),
+    (Z_GOT, 4, 3),
+    (Z_GOT, 4, 2),
+    (XY_COLUMNS, 3),
+    (OWN_COLUMN, 4),
     (XY_GOT, 4, 0),
-    (Z_GOT, 4, 1),
-    (XY_GOT, 3, 2),
     (C_GOT, 1),
     (HEADS, 2),
-    (Z_GOT, 4, 2),
     (D_GOT, 2),
-    (Z_GOT, 4, 3),
-    (OWN_COLUMN, 4),
-    (XY_GOT, 3, 3),
-    (XY_COLUMNS, 3),
     (HEADS, 3),
+    (XY_GOT, 4, 1),
+    (Z_GOT, 5, 1),
     (XY_GOT, 5, 0),
     (C_GOT, 2),
     (HEADS, 4),
-    (Z_GOT, 5, 1),
-    (XY_GOT, 4, 1),
     (Z_GOT, 5, 2),
+    (Z_GOT, 5, 3),
+    (OWN_COLUMN, 5),
+    (D_GOT, 3),
+    (XY_GOT, 4, 3),
     (HEADS, 5),
-    (Z_GOT, 5, 3),
     (XY_GOT, 4, 2),
-    (OWN_COLUMN, 5),
-    (XY_GOT, 4, 3),
     (XY_COLUMNS, 4),
-    (D_GOT, 3),
-    (XY_GOT, 5, 1),
     (C_GOT, 3),
     (ATTENTION,),
-    (START_XY, 7),
     (SECOND_NORM, 0),
     (SECOND_NORM, 1),
+    (SECOND_NORM, 2),
+    (START_XY, 7),
+    (XY_GOT, 5, 1),
+    (SECOND_NORM, 3),
     (XY_GOT, 5, 2),
-    (SECOND_NORM, 2),
-    (SECOND_NORM, 3),
     (XY_GOT, 5, 3),
     (XY_COLUMNS, 5),
+    (Z_GOT, 7, 1),
     (D_GOT, 4),
+    (XY_GOT, 7, 0),
+    (Z_GOT, 7, 2),
+    (C_GOT, 4),
+    (EXPAND_LOW, 0),
+    (Z_GOT, 7, 3),
+    (OWN_COLUMN, 7),
+    (EXPAND_LOW, 1),
+    (DOWN_LOW, 0),
+    (D_GOT, 5),
     (START_XY, 6),
+    (Z_GOT, 6, 2),
     (Z_GOT, 6, 3),
-    (Z_GOT, 6, 2),
     (Z_GOT, 6, 1),
     (OWN_COLUMN, 6),
-    (Z_GOT, 7, 1),
-    (C_GOT, 4),
-    (EXPAND_LOW, 0),
-    (Z_GOT, 7, 2),
-    (Z_GOT, 7, 3),
-    (XY_GOT, 7, 0),
-    (OWN_COLUMN, 7),
-    (EXPAND_LOW, 1),
-    (D_GOT, 5),
-    (DOWN_LOW, 0),
+    (XY_GOT, 7, 1),
     (DOWN_LOW, 1),
-    (XY_GOT, 6, 0),
+    (XY_GOT, 7, 2),
     (C_GOT, 5),
     (EXPAND_HIGH, 0),
-    (XY_GOT, 6, 3),
     (EXPAND_HIGH, 1),
-    (XY_GOT, 6, 2),
+    (XY_GOT, 7, 3),
+    (XY_COLUMNS, 7),
     (DRAIN,),
     (DOWN_HIGH, 0),
+    (XY_GOT, 6, 0),
+    (DOWN_HIGH, 1),
+    (GIVE, 0),
+    (XY_GOT, 6, 2),
+    (GIVE, 1),
+    (XY_GOT, 6, 3),
     (XY_GOT, 6, 1),
     (XY_COLUMNS, 6),
-    (DOWN_HIGH, 1),
-    (GIVE, 0),
-    (GIVE, 1),
-    (XY_GOT, 7, 1),
-    (XY_GOT, 7, 2),
-    (XY_GOT, 7, 3),
-    (XY_COLUMNS, 7),
     (OWN_PART, 0),
     (DIAGONAL, 0),
-    (D_GOT, 6),
+    (D_GOT, 7),
     (OWN_PART, 1),
     (DIAGONAL, 1),
+    (D_GOT, 6),
     (CROSS, 0, 1),
-    (D_GOT, 7),
+    (C_GOT, 7),
+    (CROSS, 0, 0),
+    (CROSS, 0, 3),
     (C_GOT, 6),
-    (CROSS, 0, 3),
-    (CROSS, 0, 0),
-    (C_GOT, 7),
     (NARROW, 0),
-    (CROSS, 1, 1),
     (NARROW, 1),
     (CROSS, 0, 2),
+    (CROSS, 1, 1),
+    (NARROW, 2),
+    (CROSS, 1, 3),
+    (CROSS, 1, 2),
     (CROSS, 1, 0),
-    (CROSS, 1, 3),
-    (NARROW, 2),
-    (CROSS, 1, 2),
     (NARROW, 3),
     (SPREAD, 0, 1),
     (GIVE, 2),
-    (SPREAD, 0, 3),
     (GIVE, 3),
     (PACK, 2),
-    (SPREAD, 1, 1),
+    (SPREAD, 0, 3),
+    (SPREAD, 0, 2),
     (OWN_PART, 2),
     (DIAGONAL, 2),
-    (SPREAD, 0, 2),
+    (SPREAD, 1, 1),
     (FINISH, 0),
     (FINISH, 1),
     (FINISH, 2),
     (FINISH, 3),
     (UP_BACK,),
     (SPREAD, 1, 3),
+    (SPREAD, 1, 2),
+    (OWN_PART, 3),
+    (DIAGONAL, 3),
+    (CROSS, 2, 1),
     (SECOND_BACK, 0),
     (SECOND_BACK, 1),
-    (SPREAD, 1, 2),
-    (CROSS, 2, 1),
     (SECOND_BACK, 2),
-    (OWN_PART, 3),
     (CROSS, 2, 0),
     (CROSS, 2, 3),
-    (DIAGONAL, 3),
-    (LAST, 0),
     (SECOND_BACK, 3),
     (GIVE, 4),
     (CROSS, 2, 2),
     (OUT_BACK,),
+    (LAST, 0),
+    (HEADS_BACK, 0),
+    (CROSS, 3, 1),
+    (CROSS, 3, 2),
+    (CROSS, 3, 0),
     (SPREAD, 2, 1),
-    (HEADS_BACK, 0),
-    (SPREAD, 2, 3),
+    (CROSS, 3, 3),
+    (OWN_PART, 4),
+    (DIAGONAL, 4),
     (GIVE, 5),
     (LAST, 1),
-    (CROSS, 3, 0),
-    (CROSS, 3, 1),
     (CLOSE, 3),
-    (OWN_PART, 4),
-    (DIAGONAL, 4),
     (HEADS_BACK, 1),
-    (CROSS, 3, 3),
-    (CROSS, 3, 2),
+    (SPREAD, 2, 3),
+    (SPREAD, 3, 1),
     (SETTLE, 3),
     (SPREAD, 2, 2),
     (OWN_PART, 5),
     (DIAGONAL, 5),
-    (SPREAD, 3, 1),
+    (SPREAD, 3, 2),
     (GIVE, 6),
+    (HEADS_BACK, 2),
+    (CROSS, 4, 3),
     (CROSS, 4, 0),
-    (CROSS, 4, 1),
-    (HEADS_BACK, 2),
-    (SPREAD, 3, 2),
     (CROSS, 4, 2),
     (SPREAD, 3, 3),
-    (CROSS, 4, 3),
     (CROSS, 5, 0),
+    (CROSS, 4, 1),
+    (CROSS, 5, 1),
+    (OWN_PART, 6),
+    (CROSS, 5, 2),
+    (DIAGONAL, 6),
+    (CROSS, 5, 3),
+    (GIVE, 7),
+    (PACK, 1),
+    (SPREAD, 4, 3),
     (LAST, 2),
-    (CROSS, 5, 1),
-    (GIVE, 7),
-    (CROSS, 5, 3),
-    (CROSS, 5, 2),
-    (OWN_PART, 6),
-    (DIAGONAL, 6),
-    (PACK, 1),
-    (SPREAD, 4, 1),
+    (OWN_PART, 7),
     (SPREAD, 4, 2),
-    (OWN_PART, 7),
-    (SPREAD, 4, 3),
     (DIAGONAL, 7),
     (QKV_BACK,),
+    (SPREAD, 4, 1),
     (SPREAD, 5, 1),
-    (SPREAD, 5, 3),
+    (SPREAD, 5, 2),
     (FIRST_BACK, 0),
-    (SPREAD, 5, 2),
     (FIRST_BACK, 1),
     (CROSS, 6, 0),
     (CROSS, 6, 1),
     (FIRST_BACK, 2),
+    (CROSS, 6, 2),
+    (CROSS, 6, 3),
     (FIRST_BACK, 3),
-    (CROSS, 6, 3),
-    (CROSS, 6, 2),
+    (SPREAD, 5, 3),
     (PACK, 0),
     (GIVE, 8),
+    (CROSS, 7, 1),
     (CROSS, 7, 0),
-    (CROSS, 7, 1),
     (LAST, 3),
     (CROSS, 7, 3),
+    (CROSS, 7, 2),
     (CLOSE, 2),
-    (CROSS, 7, 2),
+    (SPREAD, 6, 1),
     (OWN_PART, 8),
     (SMALL_PLANE,),
-    (SPREAD, 6, 1),
     (LAST, 4),
     (CLOSE, 1),
+    (SPREAD, 6, 2),
+    (SETTLE, 2),
     (SPREAD, 6, 3),
-    (SETTLE, 2),
-    (SPREAD, 6, 2),
     (SETTLE, 1),
     (SPREAD, 7, 1),
     (LAST, 5),

time: 144 us -> 143 us (level)
  no operation moved by 1% of the time
where the time goes in v8:
time: 143 us
  Pallas kernels  142 us (99%)
    pallas_call x1, Pallas kernels, layer_call(): pl.pallas_call(functools.partial(layer_kernel, names), out_shape=tuple((j...  139 us
    pallas_call x1, Pallas kernels, deliver(): pl.pallas_call(functools.partial(deliver_kernel, count), out_shape=[jax.S...  3.13 us

profile of v8, /device:TPU:0, one launch (start us, length us, event | category | flops | bytes accessed | tf_op | source)
XLA Modules:
  0.0 143.3 jit_solution(17668331584735680631)
XLA Ops:
  0.7 139.3 %layer.1 = (f32[4,512,768]{2,1,0:T(8,128)}, f32[24,2304]{1,0:T(8,128)}, f32[24,768]{1,0:T(8,128)}, f32[24,3072]{1,0:T(8,128)}, f32[96,768]{1,0:T(8,128)}, /*inde...) custom-call(f32[24,2304]{1,0:T(8,128)} %refs_0_.1, f32[24,768]{1,0:T(8,128)} %refs_1_.1, ...), custom_call_target="tpu_custom_call" | custom-call | tf_op jit(solution)/shard_map/layer/pallas_call | solution.py:1693
  139.9 3.1 %deliver.1 = (bf16[512,768]{1,0:T(8,128)(2,1)}, bf16[512,768]{1,0:T(8,128)(2,1)}, f32[24,2304]{1,0:T(8,128)}, f32[24,768]{1,0:T(8,128)}, f32[24,3072]{1,0:T(8,12...) custom-call(bf16[512,768]{1,0:T(8,128)(2,1)} %get-tuple-element.35.r, ...), custom_call_target="tpu_custom_call" | custom-call | tf_op jit(solution)/shard_map/deliver/pallas_call | solution.py:1720
